TPU v7x, 32 devices: a whole 2x2x4 slice. The times are simulated.
32 devices in a mesh: row: 4 (over z), col: 8 (over y, x, core).
Axes of the slice: x: 2, y: 2, z: 4, core: 2. Of those that a mesh axis runs over, the one named last changes fastest.
Arguments:
- features: bfloat16 [8192, 512], P(('row', 'col')), may hold values from -6 to 6
- tile_values: bfloat16 [32, 16, 128, 128], P(('row', 'col')), may hold values from -0.21875 to 0.21875
- tile_blocks: int32 [32, 16, 2], P(('row', 'col')), may hold values from 0 to 63, as said below
- tile_count: int32 [32], P(('row', 'col')), may hold values from 1 to 16, as said below
- needed: int32 [32, 4], P(('row', 'col')), may hold values from 0 to 1
- weight_one: bfloat16 [512, 512], replicated, may hold values from -0.25 to 0.25
- weight_two: bfloat16 [512, 512], replicated, may hold values from -0.25 to 0.25
Outputs:
- nodes_out: bfloat16 [8192, 512], P(('row', 'col'))
Inputs may be any that keep to these rules, and one draw needn't show every extreme that they name: `tile_blocks`: every row block of device d lies among the row blocks owned by the devices that share its index along row; for each device e along col in device d's row, all live or dead tiles of device d whose row block is owned by e name the same one of e's 2 blocks; the last device's first slot names the last block. `tile_count`: some device in every draw has all 16 slots live.
All inputs are finite; a program needn't handle non-finite values.
Results may differ from a plain program's by a relative error of at most 0.017.
Values may be sent and summed in bfloat16 or wider, within the bound.
No kernel may reach another device: no remote copies, remote signals or barrier semaphores. Data moves between devices by JAX's collectives and lax.ppermute only.
A program may use at most 64 MiB of HBM per device.

v0:
```python
import jax
import jax.numpy as jnp
from jax import lax
from jax.sharding import PartitionSpec as P


def body(features, tile_values, tile_blocks, tile_count, needed, weight_one, weight_two):
    col_count = lax.axis_size("col")
    adjacency = tile_values[0]
    blocks_here = tile_blocks[0]
    tile_slots = adjacency.shape[0]
    tile_size = adjacency.shape[1]
    feat_width = features.shape[1]
    per_device = features.shape[0] // tile_size
    alive_mask = jnp.arange(tile_slots) < tile_count[0]
    source_owner = blocks_here[:, 1]
    wanted = needed[0]
    target = blocks_here[:, 0] // per_device % col_count
    local_block = blocks_here[:, 0] % per_device
    dest_hit = (target[:, None] == jnp.arange(col_count)[None, :]) & alive_mask[:, None]
    dest_weights = dest_hit.astype(jnp.bfloat16)
    both_weights = jnp.concatenate([dest_weights, dest_weights], axis=0)
    send_block = jnp.max(jnp.where(dest_hit, local_block[:, None], 0), axis=0)
    hidden = features
    for layer_index, weight in enumerate((weight_one, weight_two)):
        owned = hidden.reshape(per_device, tile_size, feat_width)
        panel_rows = lax.all_gather(owned, "row", axis=0, tiled=True)
        operands = panel_rows[source_owner * per_device + wanted[source_owner]]
        products = jnp.einsum(
            "tmk,tkf->tmf", adjacency, operands, preferred_element_type=jnp.float32
        )
        upper_part = products.astype(jnp.bfloat16)
        lower_part = (products - upper_part.astype(jnp.float32)).astype(jnp.bfloat16)
        stacked = jnp.concatenate([upper_part, lower_part], axis=0)
        partial_value = jnp.einsum(
            "tc,tmf->cmf", both_weights, stacked, preferred_element_type=jnp.float32
        )
        partial_value = partial_value.astype(jnp.bfloat16)
        arrived_parts = lax.all_to_all(
            partial_value, "col", split_axis=0, concat_axis=0, tiled=True
        )
        picked = lax.all_to_all(send_block, "col", split_axis=0, concat_axis=0, tiled=True)
        chooser = (picked[:, None] == jnp.arange(per_device)[None, :]).astype(jnp.bfloat16)
        summed = jnp.einsum(
            "sb,smf->bmf", chooser, arrived_parts, preferred_element_type=jnp.float32
        )
        mixed = summed.astype(jnp.bfloat16).reshape(per_device * tile_size, feat_width)
        result = jnp.dot(mixed, weight, preferred_element_type=jnp.float32)
        if layer_index == 0:
            hidden = jnp.maximum(result, 0.0).astype(jnp.bfloat16)
        else:
            hidden = result.astype(jnp.bfloat16)
    return hidden


def solution(mesh):
    placed = (
        P(("row", "col"), None),
        P(("row", "col"), None, None, None),
        P(("row", "col"), None, None),
        P(("row", "col")),
        P(("row", "col"), None),
        P(),
        P(),
    )
    return jax.shard_map(
        body, mesh=mesh, in_specs=placed, out_specs=P(("row", "col"), None), check_vma=False
    )
```

profile of v0, /device:TPU:0, one launch (start us, length us, event | category | flops | bytes accessed | tf_op | source)
XLA Modules:
  0.0 147.8 jit_solution(7393868171918821235)
XLA Ops:
  6.5 0.0 copy-start
  6.5 0.0 all-gather.3.cloned.1.call-start
  6.5 0.7 all-gather.3.cloned.1.call-update
  7.9 0.7 fusion.13
  8.6 0.8 fusion.12
  9.4 0.1 select_reduce_fusion
  9.5 0.7 copy.23
  10.2 5.2 %all-to-all-start = ((s32[8,1,1]{2,1,0:T(1,128)}), s32[8,1,1]{2,1,0:T(1,128)S(1)}, u32[]{:S(2)}, u32[]{:S(2)}) async-start(s32[8,1,1]{2,1,0:T(1,128)} %copy.23), calls=%async_computation | async-start | bytes 8192 | tf_op jit(solution)/shard_map/all_to_all | solution.py:42
  15.4 1.3 gather_fusion
  16.7 0.7 fusion.16
  17.4 22.2 %all-gather.3.cloned.1.call-done = bf16[8,128,512]{2,1,0:T(8,128)(2,1)} async-done(((bf16[2,128,512]{2,1,0:T(8,128)(2,1)}), bf16[8,128,512]{2,1,0:T(8,128)(2,1)}) %all-gather.3.cloned.1.call-update) | async-done | bytes 1048592 | tf_op jit(solution)/shard_map/all_gather | solution.py:27
  39.6 1.9 %gather_fusion.1 = bf16[16,128,512]{2,1,0:T(8,128)(2,1)S(1)} fusion(bf16[8,128,512]{2,1,0:T(8,128)(2,1)} %all-gather.3.cloned.1.call-done, s32[1024]{0:T(1024)S(1)} %pad_clamp_fusion), kind=kCustom, calls=%fused_computation.1 | custom fusion | bytes 4194368 | tf_op jit(solution)/shard_map/gather | solution.py:28
  41.5 0.0 copy-done
  41.5 1.0 fusion.1
  42.5 2.3 %pad_maximum_fusion = bf16[32,128,512]{1,2,0:T(8,128)(2,1)} fusion(bf16[16,128,512]{1,2,0:T(8,128)(2,1)S(1)} %get-tuple-element.9, bf16[16,128,512]{1,2,0:T(8,128)(2,1)S(1)} %get-tuple-element.10), kind=kLoop, calls=%fused_computation.3 | loop fusion | flops 2097152 | bytes 8388608 | tf_op jit(solution)/shard_map/concatenate | solution.py:34
  44.8 8.0 %copy.25 = bf16[32,128,512]{2,0,1:T(8,128)(2,1)} copy(bf16[32,128,512]{1,2,0:T(8,128)(2,1)} %pad_maximum_fusion) | data formatting | bytes 8388608 | tf_op jit(solution)/shard_map/concatenate | solution.py:34
  52.8 2.9 %convolution_convert_fusion.1 = bf16[8,128,512]{2,0,1:T(8,128)(2,1)S(1)} fusion(bf16[32,128,512]{2,0,1:T(8,128)(2,1)} %copy.25, pred[16,8]{0,1:T(8,128)(4,1)S(1)} %fusion.9), kind=kOutput, calls=%fused_computation.12 | convolution fusion | flops 34078976 | bytes 5243008 | tf_op jit(solution)/shard_map/tc,tmf->cmf/dot_general | solution.py:35
  55.7 1.3 copy.26
  57.0 0.0 copy-start.1
  57.0 0.0 all-to-all-done
  57.0 3.8 %all-to-all-start.1 = ((bf16[8,128,512]{2,1,0:T(8,128)(2,1)}), bf16[8,128,512]{2,1,0:T(8,128)(2,1)S(1)}, u32[]{:S(2)}, u32[]{:S(2)}) async-start(bf16[8,128,512]{2,1,0:T(8,128)(2,1)} %copy.26), calls=%async_computation.1 | async-start | bytes 2097152 | tf_op jit(solution)/shard_map/all_to_all | solution.py:39
  60.8 0.0 all-gather.5.cloned.1.call-start
  60.8 0.2 reduce
  61.0 15.1 %all-to-all-done.1 = bf16[8,128,512]{2,1,0:T(8,128)(2,1)S(1)} async-done(((bf16[8,128,512]{2,1,0:T(8,128)(2,1)}), bf16[8,128,512]{2,1,0:T(8,128)(2,1)S(1)}, u32[]{:S(2)}, u32[]{:S(2)}) %all-to-all-start.1) | async-done | bytes 1048608 | tf_op jit(solution)/shard_map/all_to_all | solution.py:39
  76.2 0.7 convolution_convert_fusion.4
  77.0 0.0 copy-done.1
  77.0 1.0 fusion.2
  78.0 0.0 all-gather.5.cloned.1.call-update
  78.0 25.8 %all-gather.5.cloned.1.call-done = bf16[8,128,512]{2,1,0:T(8,128)(2,1)} async-done(((bf16[2,128,512]{2,1,0:T(8,128)(2,1)}), bf16[8,128,512]{2,1,0:T(8,128)(2,1)}) %all-gather.5.cloned.1.call-update) | async-done | bytes 1048592 | tf_op jit(solution)/shard_map/all_gather | solution.py:27
  103.8 1.9 %gather_fusion.2 = bf16[16,128,512]{2,1,0:T(8,128)(2,1)S(1)} fusion(bf16[8,128,512]{2,1,0:T(8,128)(2,1)} %all-gather.5.cloned.1.call-done, s32[1024]{0:T(1024)S(1)} %pad_clamp_fusion), kind=kCustom, calls=%fused_computation.2 | custom fusion | bytes 4194368 | tf_op jit(solution)/shard_map/gather | solution.py:28
  105.7 1.0 fusion
  106.7 2.3 %pad_maximum_fusion.1 = bf16[32,128,512]{1,2,0:T(8,128)(2,1)} fusion(bf16[16,128,512]{1,2,0:T(8,128)(2,1)S(1)} %get-tuple-element.5, bf16[16,128,512]{1,2,0:T(8,128)(2,1)S(1)} %get-tuple-element.6), kind=kLoop, calls=%fused_computation.4 | loop fusion | flops 2097152 | bytes 8388608 | tf_op jit(solution)/shard_map/concatenate | solution.py:34
  109.0 8.0 %copy.30 = bf16[32,128,512]{2,0,1:T(8,128)(2,1)} copy(bf16[32,128,512]{1,2,0:T(8,128)(2,1)} %pad_maximum_fusion.1) | data formatting | bytes 8388608 | tf_op jit(solution)/shard_map/concatenate | solution.py:34
  117.0 2.9 %convolution_convert_fusion = bf16[8,128,512]{2,0,1:T(8,128)(2,1)S(1)} fusion(bf16[32,128,512]{2,0,1:T(8,128)(2,1)} %copy.30, pred[16,8]{0,1:T(8,128)(4,1)S(1)} %fusion.9), kind=kOutput, calls=%fused_computation.11 | convolution fusion | flops 34078976 | bytes 5243008 | tf_op jit(solution)/shard_map/tc,tmf->cmf/dot_general | solution.py:35
  119.9 0.3 copy.31
  120.2 0.0 copy-start.2
  120.2 18.9 %all_to_all.20 = bf16[8,128,512]{2,1,0:T(8,128)(2,1)S(1)} all-to-all(bf16[8,128,512]{2,1,0:T(8,128)(2,1)S(1)} %copy.31), channel_id=1, replica_groups=mesh['row'=4,'col'=8] {'col'}, dimensions={0} | all-to-all | bytes 2097152 | tf_op jit(solution)/shard_map/all_to_all | solution.py:39
  139.2 0.7 convolution_convert_fusion.3
  139.9 0.0 copy-done.2
  140.0 1.0 convolution_convert_fusion.2
  (6 shorter events, 0.1 us)
Async XLA Ops:
  6.5 35.0 %copy-start = (bf16[1,16,128,128]{3,2,1,0:T(8,128)(2,1)S(1)}, bf16[1,16,128,128]{3,2,1,0:T(8,128)(2,1)}, u32[]{:S(2)}) copy-start(bf16[1,16,128,128]{3,2,1,0:T(8,128)(2,1)} %param.8) | copy-start | bytes 1572868
  6.5 33.1 %all-gather.3.cloned.1.call-start = ((), (), s32[]{:S(2)}) async-start(), calls=%async_computation.3 | async-start | bytes 1310720 | tf_op jit(solution)/shard_map/all_gather | solution.py:27
  10.2 46.8 %all-to-all-start = ((s32[8,1,1]{2,1,0:T(1,128)}), s32[8,1,1]{2,1,0:T(1,128)S(1)}, u32[]{:S(2)}, u32[]{:S(2)}) async-start(s32[8,1,1]{2,1,0:T(1,128)} %copy.23), calls=%async_computation | async-start | bytes 8192 | tf_op jit(solution)/shard_map/all_to_all | solution.py:42
  57.0 20.0 %copy-start.1 = (bf16[512,512]{1,0:T(8,128)(2,1)S(1)}, bf16[512,512]{1,0:T(8,128)(2,1)}, u32[]{:S(2)}) copy-start(bf16[512,512]{1,0:T(8,128)(2,1)} %param.12) | copy-start | bytes 1572868
  57.0 19.2 %all-to-all-start.1 = ((bf16[8,128,512]{2,1,0:T(8,128)(2,1)}), bf16[8,128,512]{2,1,0:T(8,128)(2,1)S(1)}, u32[]{:S(2)}, u32[]{:S(2)}) async-start(bf16[8,128,512]{2,1,0:T(8,128)(2,1)} %copy.26), calls=%async_computation.1 | async-start | bytes 2097152 | tf_op jit(solution)/shard_map/all_to_all | solution.py:39
  60.8 43.0 %all-gather.5.cloned.1.call-start = ((), (), s32[]{:S(2)}) async-start(), calls=%async_computation.4 | async-start | bytes 1310720 | tf_op jit(solution)/shard_map/all_gather | solution.py:27
  120.2 19.7 %copy-start.2 = (bf16[512,512]{1,0:T(8,128)(2,1)S(1)}, bf16[512,512]{1,0:T(8,128)(2,1)}, u32[]{:S(2)}) copy-start(bf16[512,512]{1,0:T(8,128)(2,1)} %param.13) | copy-start | bytes 1572868
Sparse Core Ops, SparseCore 0:
  8.9 30.6 all-gather.2
  78.1 25.6 all-gather.4
where the time goes:
time: 149 us; the launch traced here: 148 us
  waiting for transfers between devices  63.9 us (43%)
  local copies, waits for them, and re-layouts  23.4 us (16%)
  blocking collectives  18.9 us (13%)
  between operations  14.2 us (10%)
  matrix products  11.3 us (8%)
  starting transfers between devices  9 us (6%)
  other arithmetic  7.17 us (5%)
    all_gather x2, waiting for transfers between devices, body(): panel_rows = lax.all_gather(owned, 'row', axis=0, tiled=True)  48 us
    all_to_all x1, blocking collectives, body(): lax.all_to_all(partial_value, 'col', split_axis=0, concat_axis=0, tiled=T...  18.9 us
    concatenate x2, local copies, waits for them, and re-layouts, body(): stacked = jnp.concatenate([upper_part, lower_part], axis=0)  15.9 us
    all_to_all x1, waiting for transfers between devices, body(): lax.all_to_all(partial_value, 'col', split_axis=0, concat_axis=0, tiled=T...  15.1 us
    dot_general x2, matrix products, body(): jnp.einsum('tc,tmf->cmf', both_weights, stacked, preferred_element_type=j...  5.81 us
    all_to_all x1, starting transfers between devices, body(): lax.all_to_all(send_block, 'col', split_axis=0, concat_axis=0, tiled=True)  5.17 us
    gather x3, local copies, waits for them, and re-layouts, body(): operands = panel_rows[source_owner * per_device + wanted[source_owner]]  5.12 us
    concatenate x2, other arithmetic, body(): stacked = jnp.concatenate([upper_part, lower_part], axis=0)  4.64 us
  transfers between devices with their start and end apart: 4, of which 3 were waited for; matrix products, arithmetic and copies ran while one was open for 15% of the time, Pallas kernels for 0%

commit v1 on v0

v1 whole, which is shorter than its diff:
```python
import jax
import jax.numpy as jnp
from jax import lax
from jax.experimental import pallas as pl
from jax.experimental.pallas import tpu as pltpu
from jax.sharding import PartitionSpec as P


def build_kernel(dest_ref, source_ref, own_ref, peer_ref, out_ref, acc_ref):
    chip = pl.program_id(0)
    per_device, sources, tile, _ = acc_ref.shape
    slots = own_ref.shape[0]
    acc_ref[...] = jnp.zeros_like(acc_ref)
    for base, tiles in ((0, own_ref), (slots, peer_ref)):

        def add(t, carry, base=base, tiles=tiles):
            dest = dest_ref[base + t]

            @pl.when(dest // per_device == chip)
            def _():
                b = dest % per_device
                s = source_ref[base + t]
                acc_ref[b, s] = acc_ref[b, s] + tiles[t].astype(jnp.float32)

            return carry

        lax.fori_loop(0, slots, add, 0)
    for b in range(per_device):
        for s in range(sources):
            out_ref[0, b * tile : (b + 1) * tile, s * tile : (s + 1) * tile] = acc_ref[b, s].astype(out_ref.dtype)


def build_dense(dest, source, own_tiles, peer_tiles, chips, per_device, sources):
    slots, tile, _ = own_tiles.shape
    whole = pl.BlockSpec((slots, tile, tile), lambda i, *_: (0, 0, 0))
    return pl.pallas_call(
        build_kernel,
        grid_spec=pltpu.PrefetchScalarGridSpec(
            num_scalar_prefetch=2,
            grid=(chips,),
            in_specs=[whole, whole],
            out_specs=pl.BlockSpec((1, per_device * tile, sources * tile), lambda i, *_: (i, 0, 0)),
            scratch_shapes=[pltpu.VMEM((per_device, sources, tile, tile), jnp.float32)],
        ),
        out_shape=jax.ShapeDtypeStruct((chips, per_device * tile, sources * tile), own_tiles.dtype),
        name="build_dense",
    )(dest, source, own_tiles, peer_tiles)


def body(features, tile_values, tile_blocks, tile_count, needed, weight_one, weight_two):
    row_count = lax.axis_size("row")
    col_count = lax.axis_size("col")
    row_pos = lax.axis_index("row")
    col_pos = lax.axis_index("col")
    chips = col_count // 2
    core = col_pos % 2
    chip_pos = col_pos // 2
    tiles = tile_values[0]
    blocks_here = tile_blocks[0]
    slots, tile, _ = tiles.shape
    per_device = features.shape[0] // tile
    sources = 2 * row_count
    swap = [(i, i ^ 1) for i in range(col_count)]

    owner = blocks_here[:, 0] // per_device % col_count
    alive = jnp.arange(slots, dtype=jnp.int32) < tile_count[0]
    dest = ((owner // 2) ^ chip_pos) * per_device + blocks_here[:, 0] % per_device
    source = (row_pos - blocks_here[:, 1]) % row_count
    dest_own = jnp.where(alive & (owner % 2 == core), dest, -1)
    dest_peer = jnp.where(alive & (owner % 2 != core), dest, -1)
    info = lax.ppermute(jnp.stack([dest_peer, source]), "col", swap)
    peer_tiles = lax.ppermute(tiles, "col", swap)
    dense = build_dense(
        jnp.concatenate([dest_own, info[0]]),
        jnp.concatenate([source, info[1] + row_count]),
        tiles,
        peer_tiles,
        chips,
        per_device,
        sources,
    )

    wanted = [needed[0, row_pos]]
    for shift in range(1, row_count):
        peer = (row_pos - shift) % row_count
        wanted.append(
            lax.ppermute(
                needed[0, peer][None, None], "row", [(i, (i - shift) % row_count) for i in range(row_count)]
            )[0, 0]
        )

    def aggregate(values):
        width = values.shape[1]
        panel = []
        for shift in range(row_count):
            piece = lax.dynamic_slice(values, (wanted[shift] * tile, 0), (tile, width))
            if shift:
                piece = lax.ppermute(piece, "row", [(i, (i + shift) % row_count) for i in range(row_count)])
            panel.append(piece)
        panel = jnp.concatenate(panel, axis=0)
        other = lax.ppermute(panel, "col", swap)
        operand = jnp.concatenate([panel, other], axis=0)
        total = None
        for rel in range(chips):
            part = jnp.dot(dense[rel], operand, preferred_element_type=jnp.float32)
            if rel:
                part = lax.ppermute(
                    part.astype(jnp.bfloat16), "col", [(i, i ^ (2 * rel)) for i in range(col_count)]
                ).astype(jnp.float32)
            total = part if total is None else total + part
        return total

    mixed = jnp.dot(features, weight_one, preferred_element_type=jnp.float32).astype(jnp.bfloat16)
    hidden = jnp.maximum(aggregate(mixed), 0.0).astype(jnp.bfloat16)
    mixed = aggregate(hidden).astype(jnp.bfloat16)
    return jnp.dot(mixed, weight_two, preferred_element_type=jnp.float32).astype(jnp.bfloat16)


def solution(mesh):
    placed = (
        P(("row", "col"), None),
        P(("row", "col"), None, None, None),
        P(("row", "col"), None, None),
        P(("row", "col")),
        P(("row", "col"), None),
        P(),
        P(),
    )
    return jax.shard_map(
        body, mesh=mesh, in_specs=placed, out_specs=P(("row", "col"), None), check_vma=False
    )
```

time: 149 us -> 93.3 us (0.63)
  blocking collectives: 18.9 us -> 0 us
  local copies, waits for them, and re-layouts: 23.4 us -> 4.83 us
  waiting for transfers between devices: 63.9 us -> 46.1 us
  starting transfers between devices: 9 us -> 21.2 us
  between operations: 14.2 us -> 3.41 us
  Pallas kernels: 0 us -> 6.05 us
  other arithmetic: 7.17 us -> 1.55 us
  matrix products: 11.3 us -> 9.77 us
    all_gather x2 -> x0, waiting for transfers between devices: 48 us -> none  [body(): panel_rows = lax.all_gather(owned, 'row', axis=0, tiled=True)]
    ppermute x0 -> x19, waiting for transfers between devices: none -> 46.1 us  [the longest x6 23.6 us: aggregate(): lax.ppermute(part.astype(jnp.bfloat16), 'col', [(i, i ^ 2 * rel) for i in...]
    ppermute x0 -> x19, starting transfers between devices: none -> 21.2 us  [the longest x6 7.34 us: aggregate(): lax.ppermute(piece, 'row', [(i, (i + shift) % row_count) for i in range(r...]
    all_to_all x1 -> x0, blocking collectives: 18.9 us -> none  [body(): lax.all_to_all(partial_value, 'col', split_axis=0, concat_axis=0, tiled=T...]
    all_to_all x2 -> x0, waiting for transfers between devices: 15.1 us -> none  [the longest x1 15.1 us: body(): lax.all_to_all(partial_value, 'col', split_axis=0, concat_axis=0, tiled=T...]
    concatenate x2, local copies, waits for them, and re-layouts: 15.9 us -> 2.05 us  [aggregate(): operand = jnp.concatenate([panel, other], axis=0)]
    all_to_all x2 -> x0, starting transfers between devices: 8.96 us -> none  [the longest x1 5.17 us: body(): lax.all_to_all(send_block, 'col', split_axis=0, concat_axis=0, tiled=True)]
    pallas_call x0 -> x1, Pallas kernels: none -> 6.05 us  [build_dense(): pl.pallas_call(build_kernel, grid_spec=pltpu.PrefetchScalarGridSpec(num_s...]
  transfers between devices with their start and end apart: 4 -> 19, of which waited for: 3 -> 9; matrix products, arithmetic and copies ran while one was open for 15% -> 3% of each run, Pallas kernels for 0% -> 7%
where the time goes in v1:
time: 93.3 us; the launch traced here: 92.9 us
  waiting for transfers between devices  46.1 us (49%)
  starting transfers between devices  21.2 us (23%)
  matrix products  9.77 us (10%)
  Pallas kernels  6.05 us (6%)
  local copies, waits for them, and re-layouts  4.83 us (5%)
  between operations  3.41 us (4%)
  other arithmetic  1.55 us (2%)
    ppermute x6, waiting for transfers between devices, aggregate(): lax.ppermute(part.astype(jnp.bfloat16), 'col', [(i, i ^ 2 * rel) for i in...  23.6 us
    ppermute x6, waiting for transfers between devices, aggregate(): lax.ppermute(piece, 'row', [(i, (i + shift) % row_count) for i in range(r...  20.6 us
    ppermute x6, starting transfers between devices, aggregate(): lax.ppermute(piece, 'row', [(i, (i + shift) % row_count) for i in range(r...  7.34 us
    ppermute x6, starting transfers between devices, aggregate(): lax.ppermute(part.astype(jnp.bfloat16), 'col', [(i, i ^ 2 * rel) for i in...  7.11 us
    ppermute x3, starting transfers between devices, body(): lax.ppermute(needed[0, peer][None, None], 'row', [(i, (i - shift) % row_c...  6.06 us
    pallas_call x1, Pallas kernels, build_dense(): pl.pallas_call(build_kernel, grid_spec=pltpu.PrefetchScalarGridSpec(num_s...  6.05 us
    dot_general x7, matrix products, aggregate(): part = jnp.dot(dense[rel], operand, preferred_element_type=jnp.float32)  5.79 us
    dot_general x1, matrix products, body(): jnp.dot(mixed, weight_two, preferred_element_type=jnp.float32)  2.74 us
  transfers between devices with their start and end apart: 19, of which 9 were waited for; matrix products, arithmetic and copies ran while one was open for 3% of the time, Pallas kernels for 7%

profile of v1, /device:TPU:0, one launch (start us, length us, event | category | flops | bytes accessed | tf_op | source)
XLA Modules:
  0.0 92.9 jit_solution(4341291140900501232)
XLA Ops:
  0.0 1.4 %constant_dynamic-slice_fusion.5 = (s32[1,1]{1,0:T(1,128)}, s32[1,1]{1,0:T(1,128)}, s32[1,1]{1,0:T(1,128)}, s32[1,1]{1,0:T(1,128)}) fusion(s32[1,4]{1,0:T(1,128)} %param.11, s32[]{:T(128)S(6)} %select_n.172, s32[]{:T(128)S(6)} %select_n.166, s32[]{:T(128)S(6)} %select_n.163, s32[]{:T(128)S(6)} %select_n.169), kind=kLoop, calls=%fused_computation.41 | loop fusion | bytes 48 | tf_op jit(solution)/shard_map/dynamic_slice | solution.py:88
  1.5 3.0 %collective-permute-start.6 = (s32[1,1]{1,0:T(1,128)}, s32[1,1]{1,0:T(1,128)}, u32[]{:S(2)}, u32[]{:S(2)}) collective-permute-start(s32[1,1]{1,0:T(1,128)} %get-tuple-element.25), channel_id=1, source_target_pairs={{0,8},{8,16},{16,24},{24,0},{1,9},{9,17},{17,25},{25,1},{2,10},{10... | collective-permute-start | bytes 20 | tf_op jit(solution)/shard_map/ppermute | solution.py:87
  4.5 2.0 %collective-permute-start.2 = (s32[1,1]{1,0:T(1,128)}, s32[1,1]{1,0:T(1,128)}, u32[]{:S(2)}, u32[]{:S(2)}) collective-permute-start(s32[1,1]{1,0:T(1,128)} %get-tuple-element.26), channel_id=1, source_target_pairs={{0,24},{8,0},{16,8},{24,16},{1,25},{9,1},{17,9},{25,17},{2,26},{10... | collective-permute-start | bytes 20 | tf_op jit(solution)/shard_map/ppermute | solution.py:87
  6.5 1.0 %collective-permute-start.4 = (s32[1,1]{1,0:T(1,128)}, s32[1,1]{1,0:T(1,128)}, u32[]{:S(2)}, u32[]{:S(2)}) collective-permute-start(s32[1,1]{1,0:T(1,128)} %get-tuple-element.28), channel_id=1, source_target_pairs={{0,16},{8,24},{16,0},{24,8},{1,17},{9,25},{17,1},{25,9},{2,18},{10... | collective-permute-start | bytes 20 | tf_op jit(solution)/shard_map/ppermute | solution.py:87
  8.2 0.8 and_select_fusion.4
  9.0 0.1 collective-permute-start
  9.1 0.5 collective-permute-start.1
  10.1 1.2 %convolution_convert_fusion.7 = bf16[256,512]{1,0:T(8,128)(2,1)S(1)} fusion(bf16[256,512]{1,0:T(8,128)(2,1)} %param.7, bf16[512,512]{1,0:T(8,128)(2,1)S(1)} %copy-done), kind=kOutput, calls=%fused_computation.16 | convolution fusion | flops 134348800 | bytes 1048576 | tf_op jit(solution)/shard_map/dot_general | solution.py:113
  11.4 0.0 collective-permute-done.6
  13.3 0.1 constant_dynamic-slice_fusion.4
  13.4 1.4 %collective-permute-start.7 = (bf16[128,512]{1,0:T(8,128)(2,1)S(1)}, bf16[128,512]{1,0:T(8,128)(2,1)S(1)}, u32[]{:S(2)}, u32[]{:S(2)}) collective-permute-start(bf16[128,512]{1,0:T(8,128)(2,1)S(1)} %get-tuple-element.14), channel_id=1, source_target_pairs={{0,24},{8,0},{16,8},{24,16},{1,25},{9,1},{17,9},{25,17},{2,26},{10... | collective-permute-start | bytes 393224 | tf_op jit(solution)/shard_map/ppermute | solution.py:98
  14.8 1.7 %collective-permute-start.5 = (bf16[128,512]{1,0:T(8,128)(2,1)S(1)}, bf16[128,512]{1,0:T(8,128)(2,1)S(1)}, u32[]{:S(2)}, u32[]{:S(2)}) collective-permute-start(bf16[128,512]{1,0:T(8,128)(2,1)S(1)} %get-tuple-element.15), channel_id=1, source_target_pairs={{0,16},{8,24},{16,0},{24,8},{1,17},{9,25},{17,1},{25,9},{2,18},{10... | collective-permute-start | bytes 393224 | tf_op jit(solution)/shard_map/ppermute | solution.py:98
  16.5 0.9 collective-permute-start.3
  17.4 1.5 %collective-permute-done.7 = bf16[128,512]{1,0:T(8,128)(2,1)S(1)} collective-permute-done((bf16[128,512]{1,0:T(8,128)(2,1)S(1)}, bf16[128,512]{1,0:T(8,128)(2,1)S(1)}, u32[]{:S(2)}, u32[]{:S(2)}) %collective-permute-start.7) | collective-permute-done | bytes 131104 | tf_op jit(solution)/shard_map/ppermute | solution.py:98
  18.9 9.4 %collective-permute-done.5 = bf16[128,512]{1,0:T(8,128)(2,1)S(1)} collective-permute-done((bf16[128,512]{1,0:T(8,128)(2,1)S(1)}, bf16[128,512]{1,0:T(8,128)(2,1)S(1)}, u32[]{:S(2)}, u32[]{:S(2)}) %collective-permute-start.5) | collective-permute-done | bytes 131104 | tf_op jit(solution)/shard_map/ppermute | solution.py:98
  28.4 0.1 collective-permute-start.8
  28.5 0.7 pad_add_fusion.1
  29.2 1.0 %copy-done.3 = bf16[1024,512]{1,0:T(8,128)(2,1)} copy-done((bf16[1024,512]{1,0:T(8,128)(2,1)}, bf16[1024,512]{1,0:T(8,128)(2,1)S(1)}, u32[]{:S(2)}) %copy-start.3) | copy-done | bytes 1048600
  30.2 0.2 copy-done.2
  30.3 6.1 %build_dense.1 = bf16[4,256,1024]{2,1,0:T(8,128)(2,1)} custom-call(s32[32]{0:T(128)} %get-tuple-element.29.dest_ref, s32[32]{0:T(128)} %get-tuple-element.30.source_ref, bf16[16,128,128]{2,1,0:T(8,128)(2,1)} %bitcast.72, bf16[16,128,128]{2,1,0:T(8,128)(2,1)} %copy-done.2), custom_call_target="tpu_custom_call" | custom-call | tf_op jit(solution)/shard_map/build_dense/pallas_call | solution.py:36
  36.4 2.0 %constant_dynamic-update-slice_fusion = bf16[1024,512]{1,0:T(8,128)(2,1)} fusion(bf16[1024,512]{1,0:T(8,128)(2,1)} %copy-done.3, bf16[512,512]{1,0:T(8,128)(2,1)} %collective-permute-done.8), kind=kLoop, calls=%fused_computation.26 | loop fusion | bytes 1048576 | tf_op jit(solution)/shard_map/concatenate | solution.py:102
  38.4 1.9 %convolution_convert_fusion.4 = bf16[256,512]{1,0:T(8,128)(2,1)S(1)} fusion(bf16[1024,512]{1,0:T(8,128)(2,1)} %constant_dynamic-update-slice_fusion, bf16[4,256,1024]{2,1,0:T(8,128)(2,1)} %build_dense.1), kind=kOutput, calls=%fused_computation.13 | convolution fusion | flops 268566528 | bytes 1835008 | tf_op jit(solution)/shard_map/dot_general | solution.py:105
  40.3 1.7 %convolution_convert_fusion.5 = bf16[256,512]{1,0:T(8,128)(2,1)S(1)} fusion(bf16[1024,512]{1,0:T(8,128)(2,1)} %constant_dynamic-update-slice_fusion, bf16[4,256,1024]{2,1,0:T(8,128)(2,1)S(1)} %copy-done.1), kind=kOutput, calls=%fused_computation.14 | convolution fusion | flops 268566528 | bytes 1835008 | tf_op jit(solution)/shard_map/dot_general | solution.py:105
  42.0 0.4 convolution_convert_fusion.6
  42.4 1.5 %collective-permute-start.9 = (bf16[256,512]{1,0:T(8,128)(2,1)S(1)}, bf16[256,512]{1,0:T(8,128)(2,1)S(1)}, u32[]{:S(2)}, u32[]{:S(2)}) collective-permute-start(bf16[256,512]{1,0:T(8,128)(2,1)S(1)} %convolution_convert_fusion.6), channel_id=1, source_target_pairs={{0,2},{1,3},{2,0},{3,1},{4,6},{5,7},{6,4},{7,5},{8,10},{9,11},{10,... | collective-permute-start | bytes 786440 | tf_op jit(solution)/shard_map/ppermute | solution.py:107
  44.0 1.5 %collective-permute-start.10 = (bf16[256,512]{1,0:T(8,128)(2,1)S(1)}, bf16[256,512]{1,0:T(8,128)(2,1)S(1)}, u32[]{:S(2)}, u32[]{:S(2)}) collective-permute-start(bf16[256,512]{1,0:T(8,128)(2,1)S(1)} %convolution_convert_fusion.5), channel_id=1, source_target_pairs={{0,4},{1,5},{2,6},{3,7},{4,0},{5,1},{6,2},{7,3},{8,12},{9,13},{10,... | collective-permute-start | bytes 786440 | tf_op jit(solution)/shard_map/ppermute | solution.py:107
  45.5 0.5 collective-permute-start.11
  46.0 5.6 %collective-permute-done.9 = bf16[256,512]{1,0:T(8,128)(2,1)S(1)} collective-permute-done((bf16[256,512]{1,0:T(8,128)(2,1)S(1)}, bf16[256,512]{1,0:T(8,128)(2,1)S(1)}, u32[]{:S(2)}, u32[]{:S(2)}) %collective-permute-start.9) | collective-permute-done | bytes 262176 | tf_op jit(solution)/shard_map/ppermute | solution.py:107
  51.6 6.4 %collective-permute-done.10 = bf16[256,512]{1,0:T(8,128)(2,1)S(1)} collective-permute-done((bf16[256,512]{1,0:T(8,128)(2,1)S(1)}, bf16[256,512]{1,0:T(8,128)(2,1)S(1)}, u32[]{:S(2)}, u32[]{:S(2)}) %collective-permute-start.10) | collective-permute-done | bytes 262176 | tf_op jit(solution)/shard_map/ppermute | solution.py:107
  58.0 0.5 fusion.5
  58.5 0.1 constant_dynamic-slice_fusion
  58.6 0.1 collective-permute-start.14
  58.6 1.3 %collective-permute-start.13 = (bf16[128,512]{1,0:T(8,128)(2,1)S(1)}, bf16[128,512]{1,0:T(8,128)(2,1)S(1)}, u32[]{:S(2)}, u32[]{:S(2)}) collective-permute-start(bf16[128,512]{1,0:T(8,128)(2,1)S(1)} %get-tuple-element.10), channel_id=1, source_target_pairs={{0,16},{8,24},{16,0},{24,8},{1,17},{9,25},{17,1},{25,9},{2,18},{10... | collective-permute-start | bytes 393224 | tf_op jit(solution)/shard_map/ppermute | solution.py:98
  60.0 1.9 %collective-permute-start.12 = (bf16[128,512]{1,0:T(8,128)(2,1)S(1)}, bf16[128,512]{1,0:T(8,128)(2,1)S(1)}, u32[]{:S(2)}, u32[]{:S(2)}) collective-permute-start(bf16[128,512]{1,0:T(8,128)(2,1)S(1)} %get-tuple-element.11), channel_id=1, source_target_pairs={{0,8},{8,16},{16,24},{24,0},{1,9},{9,17},{17,25},{25,1},{2,10},{10... | collective-permute-start | bytes 393224 | tf_op jit(solution)/shard_map/ppermute | solution.py:98
  61.9 2.4 %collective-permute-done.14 = bf16[128,512]{1,0:T(8,128)(2,1)S(1)} collective-permute-done((bf16[128,512]{1,0:T(8,128)(2,1)S(1)}, bf16[128,512]{1,0:T(8,128)(2,1)S(1)}, u32[]{:S(2)}, u32[]{:S(2)}) %collective-permute-start.14) | collective-permute-done | bytes 131104 | tf_op jit(solution)/shard_map/ppermute | solution.py:98
  64.3 7.3 %collective-permute-done.13 = bf16[128,512]{1,0:T(8,128)(2,1)S(1)} collective-permute-done((bf16[128,512]{1,0:T(8,128)(2,1)S(1)}, bf16[128,512]{1,0:T(8,128)(2,1)S(1)}, u32[]{:S(2)}, u32[]{:S(2)}) %collective-permute-start.13) | collective-permute-done | bytes 131104 | tf_op jit(solution)/shard_map/ppermute | solution.py:98
  71.6 0.1 collective-permute-start.15
  71.8 1.8 %collective-permute-done.15 = bf16[512,512]{1,0:T(8,128)(2,1)S(1)} collective-permute-done((bf16[512,512]{1,0:T(8,128)(2,1)S(1)}, bf16[512,512]{1,0:T(8,128)(2,1)S(1)}, u32[]{:S(2)}, u32[]{:S(2)}) %collective-permute-start.15) | collective-permute-done | bytes 524320 | tf_op jit(solution)/shard_map/ppermute | solution.py:101
  73.7 0.4 convolution_convert_fusion.1
  74.1 0.0 copy-start.7
  74.1 0.4 convolution_convert_fusion.2
  74.6 0.4 convolution_convert_fusion.3
  75.0 1.4 %collective-permute-start.16 = (bf16[256,512]{1,0:T(8,128)(2,1)S(1)}, bf16[256,512]{1,0:T(8,128)(2,1)S(1)}, u32[]{:S(2)}, u32[]{:S(2)}) collective-permute-start(bf16[256,512]{1,0:T(8,128)(2,1)S(1)} %convolution_convert_fusion.3), channel_id=1, source_target_pairs={{0,2},{1,3},{2,0},{3,1},{4,6},{5,7},{6,4},{7,5},{8,10},{9,11},{10,... | collective-permute-start | bytes 786440 | tf_op jit(solution)/shard_map/ppermute | solution.py:107
  76.4 0.5 collective-permute-start.17
  76.9 1.6 %collective-permute-start.18 = (bf16[256,512]{1,0:T(8,128)(2,1)S(1)}, bf16[256,512]{1,0:T(8,128)(2,1)}, u32[]{:S(2)}, u32[]{:S(2)}) collective-permute-start(bf16[256,512]{1,0:T(8,128)(2,1)S(1)} %convolution_convert_fusion.1), channel_id=1, source_target_pairs={{0,6},{1,7},{2,4},{3,5},{4,2},{5,3},{6,0},{7,1},{8,14},{9,15},{10,... | collective-permute-start | bytes 786440 | tf_op jit(solution)/shard_map/ppermute | solution.py:107
  78.6 5.7 %collective-permute-done.16 = bf16[256,512]{1,0:T(8,128)(2,1)S(1)} collective-permute-done((bf16[256,512]{1,0:T(8,128)(2,1)S(1)}, bf16[256,512]{1,0:T(8,128)(2,1)S(1)}, u32[]{:S(2)}, u32[]{:S(2)}) %collective-permute-start.16) | collective-permute-done | bytes 262176 | tf_op jit(solution)/shard_map/ppermute | solution.py:107
  84.2 6.0 %collective-permute-done.17 = bf16[256,512]{1,0:T(8,128)(2,1)} collective-permute-done((bf16[256,512]{1,0:T(8,128)(2,1)S(1)}, bf16[256,512]{1,0:T(8,128)(2,1)}, u32[]{:S(2)}, u32[]{:S(2)}) %collective-permute-start.17) | collective-permute-done | bytes 262176 | tf_op jit(solution)/shard_map/ppermute | solution.py:107
  90.2 2.7 %convolution_convert_fusion = bf16[256,512]{1,0:T(8,128)(2,1)} fusion(bf16[512,512]{1,0:T(8,128)(2,1)S(1)} %copy-done.7, bf16[1024,512]{1,0:T(8,128)(2,1)} %copy-done.5, bf16[256,512]{1,0:T(8,128)(2,1)} %collective-permute-done.18, bf16[256,512]{1,0:T(8,128)(2,1)} %collective-permute-done.17, bf16[256,512]{1,0:T(8,128)(2,1)S(1)} %collective-permute-done.16, ...), kind=kOutput, calls=%fused_computation.9 | convolution fusion | flops 403701760 | bytes 3145728 | tf_op jit(solution)/shard_map/dot_general | solution.py:116
  (34 shorter events, 0.3 us)
Async XLA Ops:
  0.0 10.1 %copy-start = (bf16[512,512]{1,0:T(8,128)(2,1)S(1)}, bf16[512,512]{1,0:T(8,128)(2,1)}, u32[]{:S(2)}) copy-start(bf16[512,512]{1,0:T(8,128)(2,1)} %param.12) | copy-start | bytes 1572868
  0.0 17.4 %copy-start.6 = (s32[1,16,2]{1,2,0:T(2,128)S(1)}, s32[1,16,2]{1,2,0:T(2,128)}, u32[]{:S(2)}) copy-start(s32[1,16,2]{1,2,0:T(2,128)} %param.9) | copy-start | bytes 388
  1.5 9.9 %collective-permute-start.6 = (s32[1,1]{1,0:T(1,128)}, s32[1,1]{1,0:T(1,128)}, u32[]{:S(2)}, u32[]{:S(2)}) collective-permute-start(s32[1,1]{1,0:T(1,128)} %get-tuple-element.25), channel_id=1, source_target_pairs={{0,8},{8,16},{16,24},{24,0},{1,9},{9,17},{17,25},{25,1},{2,10},{10... | collective-permute-start | bytes 20 | tf_op jit(solution)/shard_map/ppermute | solution.py:87
  4.5 7.6 %collective-permute-start.2 = (s32[1,1]{1,0:T(1,128)}, s32[1,1]{1,0:T(1,128)}, u32[]{:S(2)}, u32[]{:S(2)}) collective-permute-start(s32[1,1]{1,0:T(1,128)} %get-tuple-element.26), channel_id=1, source_target_pairs={{0,24},{8,0},{16,8},{24,16},{1,25},{9,1},{17,9},{25,17},{2,26},{10... | collective-permute-start | bytes 20 | tf_op jit(solution)/shard_map/ppermute | solution.py:87
  6.5 6.2 %collective-permute-start.4 = (s32[1,1]{1,0:T(1,128)}, s32[1,1]{1,0:T(1,128)}, u32[]{:S(2)}, u32[]{:S(2)}) collective-permute-start(s32[1,1]{1,0:T(1,128)} %get-tuple-element.28), channel_id=1, source_target_pairs={{0,16},{8,24},{16,0},{24,8},{1,17},{9,25},{17,1},{25,9},{2,18},{10... | collective-permute-start | bytes 20 | tf_op jit(solution)/shard_map/ppermute | solution.py:87
  9.0 19.5 %collective-permute-start = (s32[2,16]{1,0:T(2,128)S(1)}, s32[2,16]{1,0:T(2,128)S(1)}, u32[]{:S(2)}, u32[]{:S(2)}) collective-permute-start(s32[2,16]{1,0:T(2,128)S(1)} %pad_add_fusion), channel_id=1, source_target_pairs={{0,1},{1,0},{2,3},{3,2},{4,5},{5,4},{6,7},{7,6},{8,9},{9,8},{10,11... | collective-permute-start | bytes 392 | tf_op jit(solution)/shard_map/ppermute | solution.py:71
  9.1 20.1 %collective-permute-start.1 = (bf16[16,128,128]{2,1,0:T(8,128)(2,1)}, bf16[16,128,128]{2,1,0:T(8,128)(2,1)S(1)}, u32[]{:S(2)}, u32[]{:S(2)}) collective-permute-start(bf16[16,128,128]{2,1,0:T(8,128)(2,1)} %bitcast.71), channel_id=1, source_target_pairs={{0,1},{1,0},{2,3},{3,2},{4,5},{5,4},{6,7},{7,6},{8,9},{9,8},{10,11... | collective-permute-start | bytes 1572872 | tf_op jit(solution)/shard_map/ppermute | solution.py:72
  13.4 5.5 %collective-permute-start.7 = (bf16[128,512]{1,0:T(8,128)(2,1)S(1)}, bf16[128,512]{1,0:T(8,128)(2,1)S(1)}, u32[]{:S(2)}, u32[]{:S(2)}) collective-permute-start(bf16[128,512]{1,0:T(8,128)(2,1)S(1)} %get-tuple-element.14), channel_id=1, source_target_pairs={{0,24},{8,0},{16,8},{24,16},{1,25},{9,1},{17,9},{25,17},{2,26},{10... | collective-permute-start | bytes 393224 | tf_op jit(solution)/shard_map/ppermute | solution.py:98
  14.8 13.6 %collective-permute-start.5 = (bf16[128,512]{1,0:T(8,128)(2,1)S(1)}, bf16[128,512]{1,0:T(8,128)(2,1)S(1)}, u32[]{:S(2)}, u32[]{:S(2)}) collective-permute-start(bf16[128,512]{1,0:T(8,128)(2,1)S(1)} %get-tuple-element.15), channel_id=1, source_target_pairs={{0,16},{8,24},{16,0},{24,8},{1,17},{9,25},{17,1},{25,9},{2,18},{10... | collective-permute-start | bytes 393224 | tf_op jit(solution)/shard_map/ppermute | solution.py:98
  16.5 11.9 %collective-permute-start.3 = (bf16[128,512]{1,0:T(8,128)(2,1)S(1)}, bf16[128,512]{1,0:T(8,128)(2,1)S(1)}, u32[]{:S(2)}, u32[]{:S(2)}) collective-permute-start(bf16[128,512]{1,0:T(8,128)(2,1)S(1)} %get-tuple-element.16), channel_id=1, source_target_pairs={{0,8},{8,16},{16,24},{24,0},{1,9},{9,17},{17,25},{25,1},{2,10},{10... | collective-permute-start | bytes 393224 | tf_op jit(solution)/shard_map/ppermute | solution.py:98
  28.4 8.0 %collective-permute-start.8 = (bf16[512,512]{1,0:T(8,128)(2,1)S(1)}, bf16[512,512]{1,0:T(8,128)(2,1)}, u32[]{:S(2)}, u32[]{:S(2)}) collective-permute-start(bf16[512,512]{1,0:T(8,128)(2,1)S(1)} %pad_maximum_fusion), channel_id=1, source_target_pairs={{0,1},{1,0},{2,3},{3,2},{4,5},{5,4},{6,7},{7,6},{8,9},{9,8},{10,11... | collective-permute-start | bytes 1572872 | tf_op jit(solution)/shard_map/ppermute | solution.py:101
  29.2 1.0 %copy-start.3 = (bf16[1024,512]{1,0:T(8,128)(2,1)}, bf16[1024,512]{1,0:T(8,128)(2,1)S(1)}, u32[]{:S(2)}) copy-start(bf16[1024,512]{1,0:T(8,128)(2,1)S(1)} %constant_dynamic-update-slice_fusion.1) | copy-start | bytes 3145732
  29.2 1.1 %copy-start.2 = (bf16[16,128,128]{2,1,0:T(8,128)(2,1)}, bf16[16,128,128]{2,1,0:T(8,128)(2,1)S(1)}, u32[]{:S(2)}) copy-start(bf16[16,128,128]{2,1,0:T(8,128)(2,1)S(1)} %collective-permute-done.1.peer_ref) | copy-start | bytes 1572868
  36.4 3.9 %copy-start.1 = (bf16[4,256,1024]{2,1,0:T(8,128)(2,1)S(1)}, bf16[4,256,1024]{2,1,0:T(8,128)(2,1)}, u32[]{:S(2)}) copy-start(bf16[4,256,1024]{2,1,0:T(8,128)(2,1)} %build_dense.1) | copy-start | bytes 6291460
  38.4 3.6 %copy-start.4 = (bf16[1024,512]{1,0:T(8,128)(2,1)S(1)}, bf16[1024,512]{1,0:T(8,128)(2,1)}, u32[]{:S(2)}) copy-start(bf16[1024,512]{1,0:T(8,128)(2,1)} %constant_dynamic-update-slice_fusion) | copy-start | bytes 3145732
  42.4 9.2 %collective-permute-start.9 = (bf16[256,512]{1,0:T(8,128)(2,1)S(1)}, bf16[256,512]{1,0:T(8,128)(2,1)S(1)}, u32[]{:S(2)}, u32[]{:S(2)}) collective-permute-start(bf16[256,512]{1,0:T(8,128)(2,1)S(1)} %convolution_convert_fusion.6), channel_id=1, source_target_pairs={{0,2},{1,3},{2,0},{3,1},{4,6},{5,7},{6,4},{7,5},{8,10},{9,11},{10,... | collective-permute-start | bytes 786440 | tf_op jit(solution)/shard_map/ppermute | solution.py:107
  44.0 14.0 %collective-permute-start.10 = (bf16[256,512]{1,0:T(8,128)(2,1)S(1)}, bf16[256,512]{1,0:T(8,128)(2,1)S(1)}, u32[]{:S(2)}, u32[]{:S(2)}) collective-permute-start(bf16[256,512]{1,0:T(8,128)(2,1)S(1)} %convolution_convert_fusion.5), channel_id=1, source_target_pairs={{0,4},{1,5},{2,6},{3,7},{4,0},{5,1},{6,2},{7,3},{8,12},{9,13},{10,... | collective-permute-start | bytes 786440 | tf_op jit(solution)/shard_map/ppermute | solution.py:107
  45.5 12.5 %collective-permute-start.11 = (bf16[256,512]{1,0:T(8,128)(2,1)S(1)}, bf16[256,512]{1,0:T(8,128)(2,1)S(1)}, u32[]{:S(2)}, u32[]{:S(2)}) collective-permute-start(bf16[256,512]{1,0:T(8,128)(2,1)S(1)} %convolution_convert_fusion.4), channel_id=1, source_target_pairs={{0,6},{1,7},{2,4},{3,5},{4,2},{5,3},{6,0},{7,1},{8,14},{9,15},{10,... | collective-permute-start | bytes 786440 | tf_op jit(solution)/shard_map/ppermute | solution.py:107
  58.6 5.7 %collective-permute-start.14 = (bf16[128,512]{1,0:T(8,128)(2,1)S(1)}, bf16[128,512]{1,0:T(8,128)(2,1)S(1)}, u32[]{:S(2)}, u32[]{:S(2)}) collective-permute-start(bf16[128,512]{1,0:T(8,128)(2,1)S(1)} %get-tuple-element.9), channel_id=1, source_target_pairs={{0,24},{8,0},{16,8},{24,16},{1,25},{9,1},{17,9},{25,17},{2,26},{10... | collective-permute-start | bytes 393224 | tf_op jit(solution)/shard_map/ppermute | solution.py:98
  58.6 12.9 %collective-permute-start.13 = (bf16[128,512]{1,0:T(8,128)(2,1)S(1)}, bf16[128,512]{1,0:T(8,128)(2,1)S(1)}, u32[]{:S(2)}, u32[]{:S(2)}) collective-permute-start(bf16[128,512]{1,0:T(8,128)(2,1)S(1)} %get-tuple-element.10), channel_id=1, source_target_pairs={{0,16},{8,24},{16,0},{24,8},{1,17},{9,25},{17,1},{25,9},{2,18},{10... | collective-permute-start | bytes 393224 | tf_op jit(solution)/shard_map/ppermute | solution.py:98
  60.0 11.6 %collective-permute-start.12 = (bf16[128,512]{1,0:T(8,128)(2,1)S(1)}, bf16[128,512]{1,0:T(8,128)(2,1)S(1)}, u32[]{:S(2)}, u32[]{:S(2)}) collective-permute-start(bf16[128,512]{1,0:T(8,128)(2,1)S(1)} %get-tuple-element.11), channel_id=1, source_target_pairs={{0,8},{8,16},{16,24},{24,0},{1,9},{9,17},{17,25},{25,1},{2,10},{10... | collective-permute-start | bytes 393224 | tf_op jit(solution)/shard_map/ppermute | solution.py:98
  71.6 2.0 %collective-permute-start.15 = (bf16[512,512]{1,0:T(8,128)(2,1)S(1)}, bf16[512,512]{1,0:T(8,128)(2,1)S(1)}, u32[]{:S(2)}, u32[]{:S(2)}) collective-permute-start(bf16[512,512]{1,0:T(8,128)(2,1)S(1)} %pad_maximum_fusion.1), channel_id=1, source_target_pairs={{0,1},{1,0},{2,3},{3,2},{4,5},{5,4},{6,7},{7,6},{8,9},{9,8},{10,11... | collective-permute-start | bytes 1572872 | tf_op jit(solution)/shard_map/ppermute | solution.py:101
  73.6 1.3 %copy-start.5 = (bf16[1024,512]{1,0:T(8,128)(2,1)}, bf16[1024,512]{1,0:T(8,128)(2,1)S(1)}, u32[]{:S(2)}) copy-start(bf16[1024,512]{1,0:T(8,128)(2,1)S(1)} %constant_dynamic-update-slice_fusion.5) | copy-start | bytes 3145732
  74.1 16.1 %copy-start.7 = (bf16[512,512]{1,0:T(8,128)(2,1)S(1)}, bf16[512,512]{1,0:T(8,128)(2,1)}, u32[]{:S(2)}) copy-start(bf16[512,512]{1,0:T(8,128)(2,1)} %param.13) | copy-start | bytes 1572868
  75.0 9.2 %collective-permute-start.16 = (bf16[256,512]{1,0:T(8,128)(2,1)S(1)}, bf16[256,512]{1,0:T(8,128)(2,1)S(1)}, u32[]{:S(2)}, u32[]{:S(2)}) collective-permute-start(bf16[256,512]{1,0:T(8,128)(2,1)S(1)} %convolution_convert_fusion.3), channel_id=1, source_target_pairs={{0,2},{1,3},{2,0},{3,1},{4,6},{5,7},{6,4},{7,5},{8,10},{9,11},{10,... | collective-permute-start | bytes 786440 | tf_op jit(solution)/shard_map/ppermute | solution.py:107
  76.4 13.8 %collective-permute-start.17 = (bf16[256,512]{1,0:T(8,128)(2,1)S(1)}, bf16[256,512]{1,0:T(8,128)(2,1)}, u32[]{:S(2)}, u32[]{:S(2)}) collective-permute-start(bf16[256,512]{1,0:T(8,128)(2,1)S(1)} %convolution_convert_fusion.2), channel_id=1, source_target_pairs={{0,4},{1,5},{2,6},{3,7},{4,0},{5,1},{6,2},{7,3},{8,12},{9,13},{10,... | collective-permute-start | bytes 786440 | tf_op jit(solution)/shard_map/ppermute | solution.py:107
  76.9 13.3 %collective-permute-start.18 = (bf16[256,512]{1,0:T(8,128)(2,1)S(1)}, bf16[256,512]{1,0:T(8,128)(2,1)}, u32[]{:S(2)}, u32[]{:S(2)}) collective-permute-start(bf16[256,512]{1,0:T(8,128)(2,1)S(1)} %convolution_convert_fusion.1), channel_id=1, source_target_pairs={{0,6},{1,7},{2,4},{3,5},{4,2},{5,3},{6,0},{7,1},{8,14},{9,15},{10,... | collective-permute-start | bytes 786440 | tf_op jit(solution)/shard_map/ppermute | solution.py:107

commit v2 on v0

v2 whole, which is shorter than its diff:
```python
import jax
import jax.numpy as jnp
from jax import lax
from jax.experimental import pallas as pl
from jax.experimental.pallas import tpu as pltpu
from jax.sharding import PartitionSpec as P

CHUNKS = 1
SMEM = pl.BlockSpec(memory_space=pltpu.SMEM)
VMEM = pl.BlockSpec(memory_space=pltpu.VMEM)
HALF = jnp.bfloat16
FULL = jnp.float32


def build_kernel(own_at, peer_at, own_count, peer_count, own_tiles, peer_tiles, dense, picks):
    _, owners, tile, _ = dense.shape
    per_device = 2
    rows = dense.shape[3] // tile
    row_pos = lax.axis_index("row")
    col_pos = lax.axis_index("col")
    dense[...] = jnp.zeros_like(dense)
    for r, at, count, tiles in ((0, own_at, own_count, own_tiles), (1, peer_at, peer_count, peer_tiles)):
        for e in range(owners):
            picks[r, e] = 0

        def add(t, carry, r=r, at=at, tiles=tiles):
            block = at[0, t, 0]
            e = ((block // per_device) % owners) ^ col_pos
            s = (at[0, t, 1] % rows) ^ row_pos
            picks[r, e] = block % per_device
            cols = pl.ds(pl.multiple_of(s * tile, tile), tile)
            dense[r, e, :, cols] = (dense[r, e, :, cols].astype(FULL) + tiles[0, t].astype(FULL)).astype(HALF)
            return carry

        lax.fori_loop(0, count[0], add, 0)


def project_kernel(own, peer, weight, *outs):
    half = weight.shape[1] // 2
    width = half // len(outs)
    core = lax.axis_index("col") % 2
    for j, out in enumerate(outs):
        columns = weight[:, pl.ds(pl.multiple_of(core * half + j * width, width), width)]
        for r, x in enumerate((own, peer)):
            product = jnp.dot(x[...], columns, preferred_element_type=FULL).astype(HALF)
            out[r] = product.reshape(out.shape[1:])


def select_kernel(*refs):
    rows = (len(refs) - 1) // 2
    wanted, values, outs = refs[:rows], refs[rows], refs[rows + 1 :]
    row_pos = lax.axis_index("row")
    for s, out in enumerate(outs):
        for r in range(2):
            out[r] = values[r, wanted[s][r, row_pos]]


def multiply_kernel(*refs):
    picks, dense = refs[:2]
    _, owners, tile, depth = dense.shape
    rows = depth // tile
    pieces, outs = refs[2 : 2 + rows], refs[2 + rows :]
    operands = [jnp.concatenate([piece[r] for piece in pieces], axis=0) for r in range(2)]
    for e in range(owners):
        own = jnp.dot(dense[0, e], operands[0], preferred_element_type=FULL)
        peer = jnp.dot(dense[1, e], operands[1], preferred_element_type=FULL)
        for b in range(2):
            total = jnp.where(picks[0, e] == b, own, 0.0) + jnp.where(picks[1, e] == b, peer, 0.0)
            outs[e // 2][e % 2, b] = total.astype(HALF)


def added(parts, r, b):
    total = parts[0][r, b].astype(FULL)
    for part in parts[1:]:
        total = total + part[r, b].astype(FULL)
    return total


def hidden_kernel(*refs):
    values = refs[-1]
    rows = CHIPS_ROWS[1]
    wanted, parts, outs = refs[:rows], refs[rows : rows + CHIPS_ROWS[0]], refs[rows + CHIPS_ROWS[0] : -1]
    for r in range(2):
        for b in range(2):
            values[r, b] = jnp.maximum(added(parts, r, b), 0.0).astype(HALF)
    select_kernel(*wanted, values, *outs)


def mixed_kernel(*refs):
    parts, own, peer = refs[:-2], refs[-2], refs[-1]
    for b in range(2):
        own[b] = added(parts, 0, b).astype(HALF)
        peer[b] = added(parts, 1, b).astype(HALF)


def final_kernel(*refs):
    weight, out = refs[-2:]
    chunks = (len(refs) - 2) // 2
    half = weight.shape[0] // 2
    width = half // chunks
    core = lax.axis_index("col") % 2
    total = None
    for side in range(2):
        for j in range(chunks):
            x = refs[side * chunks + j][...].reshape(out.shape[0], width)
            at = pl.multiple_of((core ^ side) * half + j * width, width)
            product = jnp.dot(x, weight[pl.ds(at, width), :], preferred_element_type=FULL)
            total = product if total is None else total + product
    out[...] = total.astype(HALF)


CHIPS_ROWS = [0, 0]


def body(features, tile_values, tile_blocks, tile_count, needed, weight_one, weight_two):
    row_count = lax.axis_size("row")
    col_count = lax.axis_size("col")
    chips = col_count // 2
    CHIPS_ROWS[:] = [chips, row_count]
    _, slots, tile, _ = tile_values.shape
    feat = features.shape[1]
    width = feat // 2 // CHUNKS
    limit = min(60, 12 + 3 * (col_count * row_count * tile * tile) // 2**19) * 2**20
    swap_pairs = [(i, i ^ 1) for i in range(col_count)]

    def swap(x):
        return lax.ppermute(x, "col", swap_pairs)

    def by_row(x, s):
        return lax.ppermute(x, "row", [(i, i ^ s) for i in range(row_count)])

    def by_chip(x, c):
        return lax.ppermute(x, "col", [(i, i ^ (2 * c)) for i in range(col_count)])

    def shape(*dims):
        return jax.ShapeDtypeStruct(dims, HALF)

    both_needed = jnp.concatenate([needed, swap(needed)], axis=0)
    wanted = [both_needed] + [by_row(both_needed, s) for s in range(1, row_count)]
    peer_features = swap(features)
    dense, picks = pl.pallas_call(
        build_kernel,
        in_specs=[SMEM] * 4 + [VMEM] * 2,
        out_specs=[VMEM, SMEM],
        out_shape=[shape(2, col_count, tile, row_count * tile), jax.ShapeDtypeStruct((2, col_count), jnp.int32)],
        cost_estimate=pl.CostEstimate(flops=1_000_000_000, bytes_accessed=4_000_000, transcendentals=0),
        compiler_params=pltpu.CompilerParams(vmem_limit_bytes=limit),
        name="build",
    )(tile_blocks, swap(tile_blocks), tile_count, swap(tile_count), tile_values, swap(tile_values))
    projected = pl.pallas_call(
        project_kernel,
        in_specs=[VMEM] * 3,
        out_specs=[VMEM] * CHUNKS,
        out_shape=[shape(2, 2, tile, width)] * CHUNKS,
        compiler_params=pltpu.CompilerParams(vmem_limit_bytes=limit),
        name="project",
    )(features, peer_features, weight_one)

    piece = shape(2, tile, width)
    part = shape(2, 2, tile, width)

    def to_readers(pieces):
        return [x if s == 0 else by_row(x, s) for s, x in enumerate(pieces)]

    def to_owners(pieces):
        parts = pl.pallas_call(
            multiply_kernel,
            in_specs=[SMEM] + [VMEM] * (1 + row_count),
            out_specs=[VMEM] * chips,
            out_shape=[part] * chips,
            compiler_params=pltpu.CompilerParams(vmem_limit_bytes=limit),
        name="multiply",
        )(picks, dense, *pieces)
        return [x if c == 0 else by_chip(x, c) for c, x in enumerate(parts)]

    pieces = []
    for values in projected:
        chosen = pl.pallas_call(
            select_kernel,
            in_specs=[SMEM] * row_count + [VMEM],
            out_specs=[VMEM] * row_count,
            out_shape=[piece] * row_count,
            compiler_params=pltpu.CompilerParams(vmem_limit_bytes=limit),
        name="select",
        )(*wanted, values)
        pieces.append(to_readers(chosen))
    arrived = [to_owners(x) for x in pieces]
    pieces = []
    for parts in arrived:
        chosen = pl.pallas_call(
            hidden_kernel,
            in_specs=[SMEM] * row_count + [VMEM] * chips,
            out_specs=[VMEM] * row_count,
            out_shape=[piece] * row_count,
            scratch_shapes=[pltpu.VMEM((2, 2, tile, width), HALF)],
            compiler_params=pltpu.CompilerParams(vmem_limit_bytes=limit),
        name="hidden",
        )(*wanted, *parts)
        pieces.append(to_readers(chosen))
    arrived = [to_owners(x) for x in pieces]
    own, other = [], []
    for parts in arrived:
        mine, theirs = pl.pallas_call(
            mixed_kernel,
            in_specs=[VMEM] * chips,
            out_specs=[VMEM] * 2,
            out_shape=[shape(2, tile, width)] * 2,
            compiler_params=pltpu.CompilerParams(vmem_limit_bytes=limit),
        name="mixed",
        )(*parts)
        own.append(mine)
        other.append(swap(theirs))
    return pl.pallas_call(
        final_kernel,
        in_specs=[VMEM] * (2 * CHUNKS + 1),
        out_specs=VMEM,
        out_shape=shape(*features.shape),
        compiler_params=pltpu.CompilerParams(vmem_limit_bytes=limit),
        name="final",
    )(*own, *other, weight_two)


def solution(mesh):
    placed = (
        P(("row", "col"), None),
        P(("row", "col"), None, None, None),
        P(("row", "col"), None, None),
        P(("row", "col")),
        P(("row", "col"), None),
        P(),
        P(),
    )
    return jax.shard_map(
        body, mesh=mesh, in_specs=placed, out_specs=P(("row", "col"), None), check_vma=False
    )
```

time: 149 us -> 72.1 us (0.48)
  waiting for transfers between devices: 63.9 us -> 34.8 us
  local copies, waits for them, and re-layouts: 23.4 us -> 3.8 us
  blocking collectives: 18.9 us -> 0 us
  starting transfers between devices: 9 us -> 23.3 us
  between operations: 14.2 us -> 0.76 us
  matrix products: 11.3 us -> 0 us
  Pallas kernels: 0 us -> 7.8 us
  other arithmetic: 7.17 us -> 0.66 us
    all_gather x2 -> x0, waiting for transfers between devices: 48 us -> none  [body(): panel_rows = lax.all_gather(owned, 'row', axis=0, tiled=True)]
    ppermute x0 -> x21, waiting for transfers between devices: none -> 34.8 us  [the longest x6 19.6 us: by_chip(): return lax.ppermute(x, 'col', [(i, i ^ 2 * c) for i in range(col_count)])]
    ppermute x0 -> x21, starting transfers between devices: none -> 23.3 us  [the longest x9 15 us: by_row(): return lax.ppermute(x, 'row', [(i, i ^ s) for i in range(row_count)])]
    all_to_all x1 -> x0, blocking collectives: 18.9 us -> none  [body(): lax.all_to_all(partial_value, 'col', split_axis=0, concat_axis=0, tiled=T...]
    concatenate x2 -> x0, local copies, waits for them, and re-layouts: 15.9 us -> none  [body(): stacked = jnp.concatenate([upper_part, lower_part], axis=0)]
    all_to_all x2 -> x0, waiting for transfers between devices: 15.1 us -> none  [the longest x1 15.1 us: body(): lax.all_to_all(partial_value, 'col', split_axis=0, concat_axis=0, tiled=T...]
    dot_general x8 -> x0, matrix products: 11.3 us -> none  [the longest x2 5.81 us: body(): jnp.einsum('tc,tmf->cmf', both_weights, stacked, preferred_element_type=j...]
    all_to_all x2 -> x0, starting transfers between devices: 8.96 us -> none  [the longest x1 5.17 us: body(): lax.all_to_all(send_block, 'col', split_axis=0, concat_axis=0, tiled=True)]
  transfers between devices with their start and end apart: 4 -> 21, of which waited for: 3 -> 12; matrix products, arithmetic and copies ran while one was open for 15% -> 2% of each run, Pallas kernels for 0% -> 5%
where the time goes in v2:
time: 72.1 us; the launch traced here: 71.2 us
  waiting for transfers between devices  34.8 us (48%)
  starting transfers between devices  23.3 us (32%)
  Pallas kernels  7.8 us (11%)
  local copies, waits for them, and re-layouts  3.8 us (5%)
  between operations  0.76 us (1%)
    ppermute x6, waiting for transfers between devices, by_chip(): return lax.ppermute(x, 'col', [(i, i ^ 2 * c) for i in range(col_count)])  19.6 us
    ppermute x9, starting transfers between devices, by_row(): return lax.ppermute(x, 'row', [(i, i ^ s) for i in range(row_count)])  15 us
    ppermute x9, waiting for transfers between devices, by_row(): return lax.ppermute(x, 'row', [(i, i ^ s) for i in range(row_count)])  11.5 us
    ppermute x6, starting transfers between devices, by_chip(): return lax.ppermute(x, 'col', [(i, i ^ 2 * c) for i in range(col_count)])  7.11 us
    unnamed x9, local copies, waits for them, and re-layouts  3.8 us
    ppermute x6, waiting for transfers between devices, swap(): return lax.ppermute(x, 'col', swap_pairs)  3.72 us
    pallas_call x2, Pallas kernels, to_owners(): pl.pallas_call(multiply_kernel, in_specs=[SMEM] + [VMEM] * (1 + row_count...  2.54 us
    pallas_call x1, Pallas kernels, body(): pl.pallas_call(build_kernel, in_specs=[SMEM] * 4 + [VMEM] * 2, out_specs=...  2.39 us
  transfers between devices with their start and end apart: 21, of which 12 were waited for; matrix products, arithmetic and copies ran while one was open for 2% of the time, Pallas kernels for 5%

profile of v2, /device:TPU:0, one launch (start us, length us, event | category | flops | bytes accessed | tf_op | source)
XLA Modules:
  0.0 71.2 jit_solution(15004424254107521969)
XLA Ops:
  0.0 0.5 collective-permute-start.2
  0.5 0.1 collective-permute-start.7
  0.5 0.5 collective-permute-start.3
  1.0 1.6 %collective-permute-done.3 = s32[1,4]{1,0:T(1,128)S(1)} collective-permute-done((s32[1,4]{1,0:T(1,128)}, s32[1,4]{1,0:T(1,128)S(1)}, u32[]{:S(2)}, u32[]{:S(2)}) %collective-permute-start.3) | collective-permute-done | bytes 48 | tf_op jit(solution)/shard_map/ppermute | solution.py:127
  2.6 0.7 pad_add_fusion.refs_0_
  3.2 5.0 %collective-permute-start.6 = (s32[2,4]{1,0:T(2,128)S(1)}, s32[2,4]{1,0:T(2,128)S(1)}, u32[]{:S(2)}, u32[]{:S(2)}) collective-permute-start(s32[2,4]{1,0:T(2,128)S(1)} %pad_add_fusion.refs_0_), channel_id=1, source_target_pairs={{0,24},{8,16},{16,8},{24,0},{1,25},{9,17},{17,9},{25,1},{2,26},{10... | collective-permute-start | bytes 104 | tf_op jit(solution)/shard_map/ppermute | solution.py:130
  8.2 0.6 collective-permute-start.4
  8.8 1.0 %copy-done = bf16[512,512]{1,0:T(8,128)(2,1)S(1)} copy-done((bf16[512,512]{1,0:T(8,128)(2,1)S(1)}, bf16[512,512]{1,0:T(8,128)(2,1)}, u32[]{:S(2)}) %copy-start) | copy-done | bytes 524312
  9.9 0.9 %copy-done.2 = bf16[256,512]{1,0:T(8,128)(2,1)S(1)} copy-done((bf16[256,512]{1,0:T(8,128)(2,1)S(1)}, bf16[256,512]{1,0:T(8,128)(2,1)}, u32[]{:S(2)}) %copy-start.2) | copy-done | bytes 262168
  10.8 0.3 project.1.refs_4_
  11.1 0.0 collective-permute-done.6.refs_3_
  11.2 1.5 %collective-permute-done.5.refs_2_ = s32[2,4]{1,0:T(2,128)S(1)} collective-permute-done((s32[2,4]{1,0:T(2,128)S(1)}, s32[2,4]{1,0:T(2,128)S(1)}, u32[]{:S(2)}, u32[]{:S(2)}) %collective-permute-start.5) | collective-permute-done | bytes 64 | tf_op jit(solution)/shard_map/ppermute | solution.py:130
  12.7 0.6 select.1
  13.3 0.1 collective-permute-start.8
  13.4 2.8 %collective-permute-start.9 = (bf16[2,128,256]{2,1,0:T(8,128)(2,1)S(1)}, bf16[2,128,256]{2,1,0:T(8,128)(2,1)S(1)}, u32[]{:S(2)}, u32[]{:S(2)}) collective-permute-start(bf16[2,128,256]{2,1,0:T(8,128)(2,1)S(1)} %get-tuple-element.29), channel_id=1, source_target_pairs={{0,16},{8,24},{16,0},{24,8},{1,17},{9,25},{17,1},{25,9},{2,18},{10... | collective-permute-start | bytes 393224 | tf_op jit(solution)/shard_map/ppermute | solution.py:130
  16.2 1.6 %collective-permute-start.10 = (bf16[2,128,256]{2,1,0:T(8,128)(2,1)S(1)}, bf16[2,128,256]{2,1,0:T(8,128)(2,1)S(1)}, u32[]{:S(2)}, u32[]{:S(2)}) collective-permute-start(bf16[2,128,256]{2,1,0:T(8,128)(2,1)S(1)} %get-tuple-element.30), channel_id=1, source_target_pairs={{0,24},{8,16},{16,8},{24,0},{1,25},{9,17},{17,9},{25,1},{2,26},{10... | collective-permute-start | bytes 393224 | tf_op jit(solution)/shard_map/ppermute | solution.py:130
  17.8 0.0 collective-permute-start.1
  17.8 0.8 %copy.9.own_at = s32[1,16,2]{2,1,0:T(8,128)S(1)} copy(s32[1,16,2]{1,2,0:T(2,128)} %param.9) | data formatting | bytes 256 | tf_op args[2]
  18.5 0.5 collective-permute-done.1.peer_count
  19.0 0.2 collective-permute-start
  19.9 0.3 collective-permute-done.peer_at
  20.2 0.0 collective-permute-done.2.peer_tiles
  20.2 1.0 %copy-done.3 = bf16[1,16,128,128]{3,2,1,0:T(8,128)(2,1)S(1)} copy-done((bf16[1,16,128,128]{3,2,1,0:T(8,128)(2,1)S(1)}, bf16[1,16,128,128]{3,2,1,0:T(8,128)(2,1)}, u32[]{:S(2)}) %copy-start.3) | copy-done | bytes 524312
  21.2 2.4 %build.1 = (bf16[2,8,128,512]{3,2,1,0:T(8,128)(2,1)S(1)}, s32[2,8]{1,0:T(2,128)S(1)}) custom-call(s32[1,16,2]{2,1,0:T(8,128)S(1)} %copy.9.own_at, s32[1,16,2]{2,1,0:T(8,128)S(1)} %collective-permute-done.peer_at, s32[1]{0:T(128)S(6)} %copy.10.own_count, s32[1]{0:T(128)} %collective-permute-done.1.peer_count, bf16[1,16,128,128]{3,2,1,0:T(8,128)(2,1)S(1)} %copy-done.3, ...), custom_call_target="tpu_custom_call" | custom-call | flops 1000000000 | bytes 4000000 | tf_op jit(solution)/shard_map/build/pallas_call | solution.py:141
  23.6 2.2 %collective-permute-done.9.refs_4_ = bf16[2,128,256]{2,1,0:T(8,128)(2,1)S(1)} collective-permute-done((bf16[2,128,256]{2,1,0:T(8,128)(2,1)S(1)}, bf16[2,128,256]{2,1,0:T(8,128)(2,1)S(1)}, u32[]{:S(2)}, u32[]{:S(2)}) %collective-permute-start.9) | collective-permute-done | bytes 131104 | tf_op jit(solution)/shard_map/ppermute | solution.py:130
  25.9 1.3 %multiply.2 = (bf16[2,2,128,256]{3,2,1,0:T(8,128)(2,1)S(1)}, bf16[2,2,128,256]{3,2,1,0:T(8,128)(2,1)S(1)}, bf16[2,2,128,256]{3,2,1,0:T(8,128)(2,1)S(1)}, bf16[2,2,128,256]{3,2,1,0:T(8,128)(2,1)S(1)}) custom-call(s32[2,8]{1,0:T(2,128)S(1)} %get-tuple-element.25.refs_0_, bf16[2,8,128,512]{3,2,1,0:T(8,128)(2,1)S(1)} %get-tuple-element.26.refs_1_, ...), custom_call_target="tpu_custom_call" | custom-call | tf_op jit(solution)/shard_map/multiply/pallas_call | solution.py:166
  27.2 1.6 %collective-permute-start.11 = (bf16[2,2,128,256]{3,2,1,0:T(8,128)(2,1)S(1)}, bf16[2,2,128,256]{3,2,1,0:T(8,128)(2,1)S(1)}, u32[]{:S(2)}, u32[]{:S(2)}) collective-permute-start(bf16[2,2,128,256]{3,2,1,0:T(8,128)(2,1)S(1)} %get-tuple-element.32), channel_id=1, source_target_pairs={{0,2},{1,3},{2,0},{3,1},{4,6},{5,7},{6,4},{7,5},{8,10},{9,11},{10,... | collective-permute-start | bytes 786440 | tf_op jit(solution)/shard_map/ppermute | solution.py:133
  28.7 1.5 %collective-permute-start.12 = (bf16[2,2,128,256]{3,2,1,0:T(8,128)(2,1)S(1)}, bf16[2,2,128,256]{3,2,1,0:T(8,128)(2,1)S(1)}, u32[]{:S(2)}, u32[]{:S(2)}) collective-permute-start(bf16[2,2,128,256]{3,2,1,0:T(8,128)(2,1)S(1)} %get-tuple-element.33), channel_id=1, source_target_pairs={{0,4},{1,5},{2,6},{3,7},{4,0},{5,1},{6,2},{7,3},{8,12},{9,13},{10,... | collective-permute-start | bytes 786440 | tf_op jit(solution)/shard_map/ppermute | solution.py:133
  30.2 0.5 collective-permute-start.13
  30.7 5.6 %collective-permute-done.11.refs_5_ = bf16[2,2,128,256]{3,2,1,0:T(8,128)(2,1)S(1)} collective-permute-done((bf16[2,2,128,256]{3,2,1,0:T(8,128)(2,1)S(1)}, bf16[2,2,128,256]{3,2,1,0:T(8,128)(2,1)S(1)}, u32[]{:S(2)}, u32[]{:S(2)}) %collective-permute-start.11) | collective-permute-done | bytes 262176 | tf_op jit(solution)/shard_map/ppermute | solution.py:133
  36.3 4.3 %collective-permute-done.12.refs_6_ = bf16[2,2,128,256]{3,2,1,0:T(8,128)(2,1)S(1)} collective-permute-done((bf16[2,2,128,256]{3,2,1,0:T(8,128)(2,1)S(1)}, bf16[2,2,128,256]{3,2,1,0:T(8,128)(2,1)S(1)}, u32[]{:S(2)}, u32[]{:S(2)}) %collective-permute-start.12) | collective-permute-done | bytes 262176 | tf_op jit(solution)/shard_map/ppermute | solution.py:133
  40.6 0.8 %hidden.1 = (bf16[2,128,256]{2,1,0:T(8,128)(2,1)S(1)}, bf16[2,128,256]{2,1,0:T(8,128)(2,1)S(1)}, bf16[2,128,256]{2,1,0:T(8,128)(2,1)S(1)}, bf16[2,128,256]{2,1,0:T(8,128)(2,1)S(1)}) custom-call(s32[2,4]{1,0:T(2,128)S(1)} %pad_add_fusion.refs_0_, s32[2,4]{1,0:T(2,128)S(1)} %collective-permute-done.4.refs_1_, s32[2,4]{1,0:T(2,128)S(1)} %collective-permute-done.5.refs_2_, ...), custom_call_target="tpu_custom_call" | custom-call | tf_op jit(solution)/shard_map/hidden/pallas_call | solution.py:190
  41.4 0.0 copy-start.1
  41.4 2.5 %collective-permute-start.14 = (bf16[2,128,256]{2,1,0:T(8,128)(2,1)S(1)}, bf16[2,128,256]{2,1,0:T(8,128)(2,1)S(1)}, u32[]{:S(2)}, u32[]{:S(2)}) collective-permute-start(bf16[2,128,256]{2,1,0:T(8,128)(2,1)S(1)} %get-tuple-element.36), channel_id=1, source_target_pairs={{0,8},{8,0},{16,24},{24,16},{1,9},{9,1},{17,25},{25,17},{2,10},{10... | collective-permute-start | bytes 393224 | tf_op jit(solution)/shard_map/ppermute | solution.py:130
  43.9 0.4 collective-permute-start.15
  44.3 2.0 %collective-permute-start.16 = (bf16[2,128,256]{2,1,0:T(8,128)(2,1)S(1)}, bf16[2,128,256]{2,1,0:T(8,128)(2,1)S(1)}, u32[]{:S(2)}, u32[]{:S(2)}) collective-permute-start(bf16[2,128,256]{2,1,0:T(8,128)(2,1)S(1)} %get-tuple-element.38), channel_id=1, source_target_pairs={{0,24},{8,16},{16,8},{24,0},{1,25},{9,17},{17,9},{25,1},{2,26},{10... | collective-permute-start | bytes 393224 | tf_op jit(solution)/shard_map/ppermute | solution.py:130
  46.3 3.3 %collective-permute-done.14.refs_3_ = bf16[2,128,256]{2,1,0:T(8,128)(2,1)S(1)} collective-permute-done((bf16[2,128,256]{2,1,0:T(8,128)(2,1)S(1)}, bf16[2,128,256]{2,1,0:T(8,128)(2,1)S(1)}, u32[]{:S(2)}, u32[]{:S(2)}) %collective-permute-start.14) | collective-permute-done | bytes 131104 | tf_op jit(solution)/shard_map/ppermute | solution.py:130
  49.7 4.4 %collective-permute-done.15.refs_4_ = bf16[2,128,256]{2,1,0:T(8,128)(2,1)S(1)} collective-permute-done((bf16[2,128,256]{2,1,0:T(8,128)(2,1)S(1)}, bf16[2,128,256]{2,1,0:T(8,128)(2,1)S(1)}, u32[]{:S(2)}, u32[]{:S(2)}) %collective-permute-start.15) | collective-permute-done | bytes 131104 | tf_op jit(solution)/shard_map/ppermute | solution.py:130
  54.0 1.3 %multiply.3 = (bf16[2,2,128,256]{3,2,1,0:T(8,128)(2,1)S(1)}, bf16[2,2,128,256]{3,2,1,0:T(8,128)(2,1)S(1)}, bf16[2,2,128,256]{3,2,1,0:T(8,128)(2,1)S(1)}, bf16[2,2,128,256]{3,2,1,0:T(8,128)(2,1)S(1)}) custom-call(s32[2,8]{1,0:T(2,128)S(1)} %get-tuple-element.25.refs_0_, bf16[2,8,128,512]{3,2,1,0:T(8,128)(2,1)S(1)} %get-tuple-element.26.refs_1_, ...), custom_call_target="tpu_custom_call" | custom-call | tf_op jit(solution)/shard_map/multiply/pallas_call | solution.py:166
  55.3 1.3 %collective-permute-start.17 = (bf16[2,2,128,256]{3,2,1,0:T(8,128)(2,1)S(1)}, bf16[2,2,128,256]{3,2,1,0:T(8,128)(2,1)S(1)}, u32[]{:S(2)}, u32[]{:S(2)}) collective-permute-start(bf16[2,2,128,256]{3,2,1,0:T(8,128)(2,1)S(1)} %get-tuple-element.40), channel_id=1, source_target_pairs={{0,2},{1,3},{2,0},{3,1},{4,6},{5,7},{6,4},{7,5},{8,10},{9,11},{10,... | collective-permute-start | bytes 786440 | tf_op jit(solution)/shard_map/ppermute | solution.py:133
  56.6 0.8 %collective-permute-start.18 = (bf16[2,2,128,256]{3,2,1,0:T(8,128)(2,1)S(1)}, bf16[2,2,128,256]{3,2,1,0:T(8,128)(2,1)S(1)}, u32[]{:S(2)}, u32[]{:S(2)}) collective-permute-start(bf16[2,2,128,256]{3,2,1,0:T(8,128)(2,1)S(1)} %get-tuple-element.41), channel_id=1, source_target_pairs={{0,4},{1,5},{2,6},{3,7},{4,0},{5,1},{6,2},{7,3},{8,12},{9,13},{10,... | collective-permute-start | bytes 786440 | tf_op jit(solution)/shard_map/ppermute | solution.py:133
  57.4 1.4 %collective-permute-start.19 = (bf16[2,2,128,256]{3,2,1,0:T(8,128)(2,1)S(1)}, bf16[2,2,128,256]{3,2,1,0:T(8,128)(2,1)S(1)}, u32[]{:S(2)}, u32[]{:S(2)}) collective-permute-start(bf16[2,2,128,256]{3,2,1,0:T(8,128)(2,1)S(1)} %get-tuple-element.42), channel_id=1, source_target_pairs={{0,6},{1,7},{2,4},{3,5},{4,2},{5,3},{6,0},{7,1},{8,14},{9,15},{10,... | collective-permute-start | bytes 786440 | tf_op jit(solution)/shard_map/ppermute | solution.py:133
  58.9 5.5 %collective-permute-done.17.refs_1_ = bf16[2,2,128,256]{3,2,1,0:T(8,128)(2,1)S(1)} collective-permute-done((bf16[2,2,128,256]{3,2,1,0:T(8,128)(2,1)S(1)}, bf16[2,2,128,256]{3,2,1,0:T(8,128)(2,1)S(1)}, u32[]{:S(2)}, u32[]{:S(2)}) %collective-permute-start.17) | collective-permute-done | bytes 262176 | tf_op jit(solution)/shard_map/ppermute | solution.py:133
  64.4 4.2 %collective-permute-done.18.refs_2_ = bf16[2,2,128,256]{3,2,1,0:T(8,128)(2,1)S(1)} collective-permute-done((bf16[2,2,128,256]{3,2,1,0:T(8,128)(2,1)S(1)}, bf16[2,2,128,256]{3,2,1,0:T(8,128)(2,1)S(1)}, u32[]{:S(2)}, u32[]{:S(2)}) %collective-permute-start.18) | collective-permute-done | bytes 262176 | tf_op jit(solution)/shard_map/ppermute | solution.py:133
  68.6 0.1 mixed.1
  68.7 0.1 collective-permute-start.20
  68.8 1.3 %collective-permute-done.20.refs_1_ = bf16[2,128,256]{2,1,0:T(8,128)(2,1)S(1)} collective-permute-done((bf16[2,128,256]{2,1,0:T(8,128)(2,1)S(1)}, bf16[2,128,256]{2,1,0:T(8,128)(2,1)S(1)}, u32[]{:S(2)}, u32[]{:S(2)}) %collective-permute-start.20) | collective-permute-done | bytes 131104 | tf_op jit(solution)/shard_map/ppermute | solution.py:127
  70.2 1.0 %final.1 = bf16[256,512]{1,0:T(8,128)(2,1)} custom-call(bf16[2,128,256]{2,1,0:T(8,128)(2,1)S(1)} %get-tuple-element.43.refs_0_, bf16[2,128,256]{2,1,0:T(8,128)(2,1)S(1)} %collective-permute-done.20.refs_1_, bf16[512,512]{1,0:T(8,128)(2,1)S(1)} %copy-done.1), custom_call_target="tpu_custom_call" | custom-call | tf_op jit(solution)/shard_map/final/pallas_call | solution.py:213
  (12 shorter events, 0.0 us)
Async XLA Ops:
  0.0 20.2 %collective-permute-start.2 = (bf16[1,16,128,128]{3,2,1,0:T(8,128)(2,1)}, bf16[1,16,128,128]{3,2,1,0:T(8,128)(2,1)S(1)}, u32[]{:S(2)}, u32[]{:S(2)}) collective-permute-start(bf16[1,16,128,128]{3,2,1,0:T(8,128)(2,1)} %own_tiles.1), channel_id=1, source_target_pairs={{0,1},{1,0},{2,3},{3,2},{4,5},{5,4},{6,7},{7,6},{8,9},{9,8},{10,11... | collective-permute-start | bytes 1572872 | tf_op jit(solution)/shard_map/ppermute | solution.py:127
  0.5 8.4 %collective-permute-start.7 = (bf16[256,512]{1,0:T(8,128)(2,1)}, bf16[256,512]{1,0:T(8,128)(2,1)S(1)}, u32[]{:S(2)}, u32[]{:S(2)}) collective-permute-start(bf16[256,512]{1,0:T(8,128)(2,1)} %own.1), channel_id=1, source_target_pairs={{0,1},{1,0},{2,3},{3,2},{4,5},{5,4},{6,7},{7,6},{8,9},{9,8},{10,11... | collective-permute-start | bytes 786440 | tf_op jit(solution)/shard_map/ppermute | solution.py:127
  0.5 2.1 %collective-permute-start.3 = (s32[1,4]{1,0:T(1,128)}, s32[1,4]{1,0:T(1,128)S(1)}, u32[]{:S(2)}, u32[]{:S(2)}) collective-permute-start(s32[1,4]{1,0:T(1,128)} %param.11), channel_id=1, source_target_pairs={{0,1},{1,0},{2,3},{3,2},{4,5},{5,4},{6,7},{7,6},{8,9},{9,8},{10,11... | collective-permute-start | bytes 56 | tf_op jit(solution)/shard_map/ppermute | solution.py:127
  3.2 7.9 %collective-permute-start.6 = (s32[2,4]{1,0:T(2,128)S(1)}, s32[2,4]{1,0:T(2,128)S(1)}, u32[]{:S(2)}, u32[]{:S(2)}) collective-permute-start(s32[2,4]{1,0:T(2,128)S(1)} %pad_add_fusion.refs_0_), channel_id=1, source_target_pairs={{0,24},{8,16},{16,8},{24,0},{1,25},{9,17},{17,9},{25,1},{2,26},{10... | collective-permute-start | bytes 104 | tf_op jit(solution)/shard_map/ppermute | solution.py:130
  8.2 4.5 %collective-permute-start.5 = (s32[2,4]{1,0:T(2,128)S(1)}, s32[2,4]{1,0:T(2,128)S(1)}, u32[]{:S(2)}, u32[]{:S(2)}) collective-permute-start(s32[2,4]{1,0:T(2,128)S(1)} %pad_add_fusion.refs_0_), channel_id=1, source_target_pairs={{0,16},{8,24},{16,0},{24,8},{1,17},{9,25},{17,1},{25,9},{2,18},{10... | collective-permute-start | bytes 104 | tf_op jit(solution)/shard_map/ppermute | solution.py:130
  8.2 4.5 %collective-permute-start.4 = (s32[2,4]{1,0:T(2,128)S(1)}, s32[2,4]{1,0:T(2,128)S(1)}, u32[]{:S(2)}, u32[]{:S(2)}) collective-permute-start(s32[2,4]{1,0:T(2,128)S(1)} %pad_add_fusion.refs_0_), channel_id=1, source_target_pairs={{0,8},{8,0},{16,24},{24,16},{1,9},{9,1},{17,25},{25,17},{2,10},{10... | collective-permute-start | bytes 104 | tf_op jit(solution)/shard_map/ppermute | solution.py:130
  8.8 1.0 %copy-start = (bf16[512,512]{1,0:T(8,128)(2,1)S(1)}, bf16[512,512]{1,0:T(8,128)(2,1)}, u32[]{:S(2)}) copy-start(bf16[512,512]{1,0:T(8,128)(2,1)} %weight.1) | copy-start | bytes 1572868
  9.9 0.9 %copy-start.2 = (bf16[256,512]{1,0:T(8,128)(2,1)S(1)}, bf16[256,512]{1,0:T(8,128)(2,1)}, u32[]{:S(2)}) copy-start(bf16[256,512]{1,0:T(8,128)(2,1)} %own.1) | copy-start | bytes 786436
  13.3 10.3 %collective-permute-start.8 = (bf16[2,128,256]{2,1,0:T(8,128)(2,1)S(1)}, bf16[2,128,256]{2,1,0:T(8,128)(2,1)S(1)}, u32[]{:S(2)}, u32[]{:S(2)}) collective-permute-start(bf16[2,128,256]{2,1,0:T(8,128)(2,1)S(1)} %get-tuple-element.28), channel_id=1, source_target_pairs={{0,8},{8,0},{16,24},{24,16},{1,9},{9,1},{17,25},{25,17},{2,10},{10... | collective-permute-start | bytes 393224 | tf_op jit(solution)/shard_map/ppermute | solution.py:130
  13.4 12.5 %collective-permute-start.9 = (bf16[2,128,256]{2,1,0:T(8,128)(2,1)S(1)}, bf16[2,128,256]{2,1,0:T(8,128)(2,1)S(1)}, u32[]{:S(2)}, u32[]{:S(2)}) collective-permute-start(bf16[2,128,256]{2,1,0:T(8,128)(2,1)S(1)} %get-tuple-element.29), channel_id=1, source_target_pairs={{0,16},{8,24},{16,0},{24,8},{1,17},{9,25},{17,1},{25,9},{2,18},{10... | collective-permute-start | bytes 393224 | tf_op jit(solution)/shard_map/ppermute | solution.py:130
  16.2 9.7 %collective-permute-start.10 = (bf16[2,128,256]{2,1,0:T(8,128)(2,1)S(1)}, bf16[2,128,256]{2,1,0:T(8,128)(2,1)S(1)}, u32[]{:S(2)}, u32[]{:S(2)}) collective-permute-start(bf16[2,128,256]{2,1,0:T(8,128)(2,1)S(1)} %get-tuple-element.30), channel_id=1, source_target_pairs={{0,24},{8,16},{16,8},{24,0},{1,25},{9,17},{17,9},{25,1},{2,26},{10... | collective-permute-start | bytes 393224 | tf_op jit(solution)/shard_map/ppermute | solution.py:130
  17.8 1.2 %collective-permute-start.1 = (s32[1]{0:T(128)}, s32[1]{0:T(128)}, u32[]{:S(2)}, u32[]{:S(2)}) collective-permute-start(s32[1]{0:T(128)} %param.10), channel_id=1, source_target_pairs={{0,1},{1,0},{2,3},{3,2},{4,5},{5,4},{6,7},{7,6},{8,9},{9,8},{10,11... | collective-permute-start | bytes 20 | tf_op jit(solution)/shard_map/ppermute | solution.py:127
  19.0 1.2 %collective-permute-start = (s32[1,16,2]{2,1,0:T(8,128)S(1)}, s32[1,16,2]{2,1,0:T(8,128)S(1)}, u32[]{:S(2)}, u32[]{:S(2)}) collective-permute-start(s32[1,16,2]{2,1,0:T(8,128)S(1)} %copy.9.own_at), channel_id=1, source_target_pairs={{0,1},{1,0},{2,3},{3,2},{4,5},{5,4},{6,7},{7,6},{8,9},{9,8},{10,11... | collective-permute-start | bytes 392 | tf_op jit(solution)/shard_map/ppermute | solution.py:127
  20.2 1.0 %copy-start.3 = (bf16[1,16,128,128]{3,2,1,0:T(8,128)(2,1)S(1)}, bf16[1,16,128,128]{3,2,1,0:T(8,128)(2,1)}, u32[]{:S(2)}) copy-start(bf16[1,16,128,128]{3,2,1,0:T(8,128)(2,1)} %own_tiles.1) | copy-start | bytes 1572868
  27.2 9.2 %collective-permute-start.11 = (bf16[2,2,128,256]{3,2,1,0:T(8,128)(2,1)S(1)}, bf16[2,2,128,256]{3,2,1,0:T(8,128)(2,1)S(1)}, u32[]{:S(2)}, u32[]{:S(2)}) collective-permute-start(bf16[2,2,128,256]{3,2,1,0:T(8,128)(2,1)S(1)} %get-tuple-element.32), channel_id=1, source_target_pairs={{0,2},{1,3},{2,0},{3,1},{4,6},{5,7},{6,4},{7,5},{8,10},{9,11},{10,... | collective-permute-start | bytes 786440 | tf_op jit(solution)/shard_map/ppermute | solution.py:133
  28.7 11.9 %collective-permute-start.12 = (bf16[2,2,128,256]{3,2,1,0:T(8,128)(2,1)S(1)}, bf16[2,2,128,256]{3,2,1,0:T(8,128)(2,1)S(1)}, u32[]{:S(2)}, u32[]{:S(2)}) collective-permute-start(bf16[2,2,128,256]{3,2,1,0:T(8,128)(2,1)S(1)} %get-tuple-element.33), channel_id=1, source_target_pairs={{0,4},{1,5},{2,6},{3,7},{4,0},{5,1},{6,2},{7,3},{8,12},{9,13},{10,... | collective-permute-start | bytes 786440 | tf_op jit(solution)/shard_map/ppermute | solution.py:133
  30.2 10.4 %collective-permute-start.13 = (bf16[2,2,128,256]{3,2,1,0:T(8,128)(2,1)S(1)}, bf16[2,2,128,256]{3,2,1,0:T(8,128)(2,1)S(1)}, u32[]{:S(2)}, u32[]{:S(2)}) collective-permute-start(bf16[2,2,128,256]{3,2,1,0:T(8,128)(2,1)S(1)} %get-tuple-element.34), channel_id=1, source_target_pairs={{0,6},{1,7},{2,4},{3,5},{4,2},{5,3},{6,0},{7,1},{8,14},{9,15},{10,... | collective-permute-start | bytes 786440 | tf_op jit(solution)/shard_map/ppermute | solution.py:133
  41.4 28.8 %copy-start.1 = (bf16[512,512]{1,0:T(8,128)(2,1)S(1)}, bf16[512,512]{1,0:T(8,128)(2,1)}, u32[]{:S(2)}) copy-start(bf16[512,512]{1,0:T(8,128)(2,1)} %refs_2_.1) | copy-start | bytes 1572868
  41.4 8.3 %collective-permute-start.14 = (bf16[2,128,256]{2,1,0:T(8,128)(2,1)S(1)}, bf16[2,128,256]{2,1,0:T(8,128)(2,1)S(1)}, u32[]{:S(2)}, u32[]{:S(2)}) collective-permute-start(bf16[2,128,256]{2,1,0:T(8,128)(2,1)S(1)} %get-tuple-element.36), channel_id=1, source_target_pairs={{0,8},{8,0},{16,24},{24,16},{1,9},{9,1},{17,25},{25,17},{2,10},{10... | collective-permute-start | bytes 393224 | tf_op jit(solution)/shard_map/ppermute | solution.py:130
  43.9 10.1 %collective-permute-start.15 = (bf16[2,128,256]{2,1,0:T(8,128)(2,1)S(1)}, bf16[2,128,256]{2,1,0:T(8,128)(2,1)S(1)}, u32[]{:S(2)}, u32[]{:S(2)}) collective-permute-start(bf16[2,128,256]{2,1,0:T(8,128)(2,1)S(1)} %get-tuple-element.37), channel_id=1, source_target_pairs={{0,16},{8,24},{16,0},{24,8},{1,17},{9,25},{17,1},{25,9},{2,18},{10... | collective-permute-start | bytes 393224 | tf_op jit(solution)/shard_map/ppermute | solution.py:130
  44.3 9.7 %collective-permute-start.16 = (bf16[2,128,256]{2,1,0:T(8,128)(2,1)S(1)}, bf16[2,128,256]{2,1,0:T(8,128)(2,1)S(1)}, u32[]{:S(2)}, u32[]{:S(2)}) collective-permute-start(bf16[2,128,256]{2,1,0:T(8,128)(2,1)S(1)} %get-tuple-element.38), channel_id=1, source_target_pairs={{0,24},{8,16},{16,8},{24,0},{1,25},{9,17},{17,9},{25,1},{2,26},{10... | collective-permute-start | bytes 393224 | tf_op jit(solution)/shard_map/ppermute | solution.py:130
  55.3 9.1 %collective-permute-start.17 = (bf16[2,2,128,256]{3,2,1,0:T(8,128)(2,1)S(1)}, bf16[2,2,128,256]{3,2,1,0:T(8,128)(2,1)S(1)}, u32[]{:S(2)}, u32[]{:S(2)}) collective-permute-start(bf16[2,2,128,256]{3,2,1,0:T(8,128)(2,1)S(1)} %get-tuple-element.40), channel_id=1, source_target_pairs={{0,2},{1,3},{2,0},{3,1},{4,6},{5,7},{6,4},{7,5},{8,10},{9,11},{10,... | collective-permute-start | bytes 786440 | tf_op jit(solution)/shard_map/ppermute | solution.py:133
  56.6 12.0 %collective-permute-start.18 = (bf16[2,2,128,256]{3,2,1,0:T(8,128)(2,1)S(1)}, bf16[2,2,128,256]{3,2,1,0:T(8,128)(2,1)S(1)}, u32[]{:S(2)}, u32[]{:S(2)}) collective-permute-start(bf16[2,2,128,256]{3,2,1,0:T(8,128)(2,1)S(1)} %get-tuple-element.41), channel_id=1, source_target_pairs={{0,4},{1,5},{2,6},{3,7},{4,0},{5,1},{6,2},{7,3},{8,12},{9,13},{10,... | collective-permute-start | bytes 786440 | tf_op jit(solution)/shard_map/ppermute | solution.py:133
  57.4 11.2 %collective-permute-start.19 = (bf16[2,2,128,256]{3,2,1,0:T(8,128)(2,1)S(1)}, bf16[2,2,128,256]{3,2,1,0:T(8,128)(2,1)S(1)}, u32[]{:S(2)}, u32[]{:S(2)}) collective-permute-start(bf16[2,2,128,256]{3,2,1,0:T(8,128)(2,1)S(1)} %get-tuple-element.42), channel_id=1, source_target_pairs={{0,6},{1,7},{2,4},{3,5},{4,2},{5,3},{6,0},{7,1},{8,14},{9,15},{10,... | collective-permute-start | bytes 786440 | tf_op jit(solution)/shard_map/ppermute | solution.py:133
  68.7 1.4 %collective-permute-start.20 = (bf16[2,128,256]{2,1,0:T(8,128)(2,1)S(1)}, bf16[2,128,256]{2,1,0:T(8,128)(2,1)S(1)}, u32[]{:S(2)}, u32[]{:S(2)}) collective-permute-start(bf16[2,128,256]{2,1,0:T(8,128)(2,1)S(1)} %get-tuple-element.44), channel_id=1, source_target_pairs={{0,1},{1,0},{2,3},{3,2},{4,5},{5,4},{6,7},{7,6},{8,9},{9,8},{10,11... | collective-permute-start | bytes 393224 | tf_op jit(solution)/shard_map/ppermute | solution.py:127

commit v3 on v2

v3 whole, which is shorter than its diff:
```python
import functools

import jax
import jax.numpy as jnp
from jax import lax
from jax.experimental import pallas as pl
from jax.experimental.pallas import tpu as pltpu
from jax.sharding import PartitionSpec as P

CHUNKS = 2
SMEM = pl.BlockSpec(memory_space=pltpu.SMEM)
VMEM = pl.BlockSpec(memory_space=pltpu.VMEM)
HALF = jnp.bfloat16
FULL = jnp.float32


def build_kernel(own_at, peer_at, own_count, peer_count, own_tiles, peer_tiles, dense, picks):
    _, owners, tile, _ = dense.shape
    per_device = 2
    rows = dense.shape[3] // tile
    row_pos = lax.axis_index("row")
    col_pos = lax.axis_index("col")
    dense[...] = jnp.zeros_like(dense)
    for r, at, count, tiles in ((0, own_at, own_count, own_tiles), (1, peer_at, peer_count, peer_tiles)):
        for e in range(owners):
            picks[r, e] = 0

        def add(t, carry, r=r, at=at, tiles=tiles):
            block = at[0, t, 0]
            e = ((block // per_device) % owners) ^ col_pos
            s = (at[0, t, 1] % rows) ^ row_pos
            picks[r, e] = block % per_device
            cols = pl.ds(pl.multiple_of(s * tile, tile), tile)
            dense[r, e, :, cols] = (dense[r, e, :, cols].astype(FULL) + tiles[0, t].astype(FULL)).astype(HALF)
            return carry

        lax.fori_loop(0, count[0], add, 0)


def project_kernel(own, peer, weight, out):
    width = weight.shape[1] // 2
    core = lax.axis_index("col") % 2
    columns = weight[:, pl.ds(pl.multiple_of(core * width, width), width)]
    for r, x in enumerate((own, peer)):
        product = jnp.dot(x[...], columns, preferred_element_type=FULL).astype(HALF)
        out[r] = product.reshape(out.shape[1:])


def select(wanted, values, outs):
    row_pos = lax.axis_index("row")
    for s, out in enumerate(outs):
        for r in range(2):
            out[r] = values[r, wanted[s][r, row_pos]]


def select_kernel(*refs):
    rows = (len(refs) - 1) // 2
    select(refs[:rows], refs[rows], refs[rows + 1 :])


def multiply_kernel(*refs):
    picks, dense = refs[:2]
    _, owners, tile, depth = dense.shape
    rows = depth // tile
    pieces, outs = refs[2 : 2 + rows], refs[2 + rows :]
    chips = owners // 2
    columns = outs[0].shape[-1]
    ordered = pieces[:1] + pieces[:0:-1]
    operands = [jnp.concatenate([piece[r] for piece in ordered], axis=0) for r in range(2)]
    for e in range(owners):
        own = jnp.dot(dense[0, e], operands[0], preferred_element_type=FULL)
        peer = jnp.dot(dense[1, e], operands[1], preferred_element_type=FULL)
        for b in range(2):
            total = jnp.where(picks[0, e] == b, own, 0.0) + jnp.where(picks[1, e] == b, peer, 0.0)
            for j in range(len(outs) // chips):
                outs[j * chips + e // 2][e % 2, b] = total[:, j * columns : (j + 1) * columns].astype(HALF)


def added(parts, r, b):
    total = parts[0][r, b].astype(FULL)
    for part in parts[1:]:
        total = total + part[r, b].astype(FULL)
    return total


def hidden_kernel(*refs, rows):
    values = refs[-1]
    wanted, parts, outs = refs[:rows], refs[rows : -1 - rows], refs[-1 - rows : -1]
    for r in range(2):
        for b in range(2):
            values[r, b] = jnp.maximum(added(parts, r, b), 0.0).astype(HALF)
    select(wanted, values, outs)


def mixed_kernel(*refs):
    parts, own, peer = refs[:-2], refs[-2], refs[-1]
    for b in range(2):
        own[b] = added(parts, 0, b).astype(HALF)
        peer[b] = added(parts, 1, b).astype(HALF)


def final_kernel(*refs):
    weight, out = refs[-2:]
    sides = refs[: len(refs) // 2 - 1], refs[len(refs) // 2 - 1 : -2]
    core = lax.axis_index("col") % 2
    total = None
    for side, chunks in enumerate(sides):
        at = (core ^ side) * (weight.shape[0] // 2)
        for x in chunks:
            width = x.shape[-1]
            rows = x[...].reshape(out.shape[0], width)
            columns = weight[pl.ds(pl.multiple_of(at, width), width), :]
            product = jnp.dot(rows, columns, preferred_element_type=FULL)
            total = product if total is None else total + product
            at = at + width
    out[...] = total.astype(HALF)


def body(features, tile_values, tile_blocks, tile_count, needed, weight_one, weight_two):
    row_count = lax.axis_size("row")
    col_count = lax.axis_size("col")
    chips = col_count // 2
    _, slots, tile, _ = tile_values.shape
    width = features.shape[1] // 2
    limit = min(60, 12 + 3 * (col_count * row_count * tile * tile) // 2**19) * 2**20

    def call(kernel, out_shape, args, in_specs=None, out_specs=None, **options):
        many = isinstance(out_shape, list)
        return pl.pallas_call(
            kernel,
            in_specs=in_specs or [VMEM] * len(args),
            out_specs=out_specs or ([VMEM] * len(out_shape) if many else VMEM),
            out_shape=out_shape,
            compiler_params=pltpu.CompilerParams(vmem_limit_bytes=limit),
            cost_estimate=pl.CostEstimate(flops=1_000_000_000, bytes_accessed=10_000_000, transcendentals=0),
            **options,
        )(*args)

    def by_col(x, masks):
        return lax.ppermute(x, "col", [(i, i ^ masks[i % 2]) for i in range(col_count)])

    def swap(x):
        return by_col(x, (1, 1))

    def by_row(x, s):
        return lax.ppermute(x, "row", [(i, i ^ s) for i in range(row_count)])

    def shape(*dims, dtype=HALF):
        return jax.ShapeDtypeStruct(dims, dtype)

    both_needed = jnp.concatenate([needed, swap(needed)], axis=0)
    wanted = [both_needed] + [by_row(both_needed, s) for s in range(1, row_count)]
    projected = call(project_kernel, shape(2, 2, tile, width), [features, swap(features), weight_one], name="project")
    dense, picks = call(
        build_kernel,
        [shape(2, col_count, tile, row_count * tile), shape(2, col_count, dtype=jnp.int32)],
        [tile_blocks, swap(tile_blocks), tile_count, swap(tile_count), tile_values, swap(tile_values)],
        in_specs=[SMEM] * 4 + [VMEM] * 2,
        out_specs=[VMEM, SMEM],
        name="build",
    )

    columns = width // CHUNKS

    def to_readers(pieces):
        return [pieces[0]] + [by_row(pieces[s], s) for s in range(row_count - 1, 0, -1)]

    def to_owners(pieces):
        chunks = pieces[0].shape[-1] // columns
        parts = call(
            multiply_kernel,
            [shape(2, 2, tile, columns)] * (chips * chunks),
            [picks, dense, *pieces],
            in_specs=[SMEM] + [VMEM] * (1 + row_count),
            name="multiply",
        )
        parts = [parts[j * chips : (j + 1) * chips] for j in range(chunks)]
        return [[x[0]] + [by_col(x[c], (2 * c, 2 * c)) for c in range(1, chips)] for x in parts]

    selected = call(
        select_kernel,
        [shape(2, tile, width)] * row_count,
        [*wanted, projected],
        in_specs=[SMEM] * row_count + [VMEM],
        name="select",
    )
    arrived = to_owners(to_readers(selected))
    panels = []
    for parts in arrived:
        selected = call(
            functools.partial(hidden_kernel, rows=row_count),
            [shape(2, tile, columns)] * row_count,
            [*wanted, *parts],
            in_specs=[SMEM] * row_count + [VMEM] * len(parts),
            scratch_shapes=[pltpu.VMEM((2, 2, tile, columns), HALF)],
            name="hidden",
        )
        panels.append(to_readers(selected))
    arrived = [to_owners(panel)[0] for panel in panels]
    mine, theirs = [], []
    for parts in arrived:
        own, other = call(mixed_kernel, [shape(2, tile, columns)] * 2, parts, name="mixed")
        mine.append(own)
        theirs.append(swap(other))
    return call(final_kernel, shape(*features.shape), [*mine, *theirs, weight_two], name="final")


def solution(mesh):
    placed = (
        P(("row", "col"), None),
        P(("row", "col"), None, None, None),
        P(("row", "col"), None, None),
        P(("row", "col")),
        P(("row", "col"), None),
        P(),
        P(),
    )
    return jax.shard_map(
        body, mesh=mesh, in_specs=placed, out_specs=P(("row", "col"), None), check_vma=False
    )
```

time: 72.1 us -> 65.2 us (0.904); the launches traced: 71.2 us -> 65 us
  waiting for transfers between devices: 34.8 us -> 15.6 us
  starting transfers between devices: 23.3 us -> 36.2 us
  Pallas kernels: 7.8 us -> 9.67 us
  local copies, waits for them, and re-layouts: 3.8 us -> 2.09 us
    ppermute x12 -> x19, waiting for transfers between devices: 23.3 us -> 10.4 us  [by_col(): lax.ppermute(x, 'col', [(i, i ^ masks[i % 2]) for i in range(col_count)])]
    ppermute x12 -> x19, starting transfers between devices: 8.37 us -> 17.3 us  [by_col(): lax.ppermute(x, 'col', [(i, i ^ masks[i % 2]) for i in range(col_count)])]
    ppermute x9 -> x12, waiting for transfers between devices: 11.5 us -> 5.18 us  [by_row(): return lax.ppermute(x, 'row', [(i, i ^ s) for i in range(row_count)])]
    ppermute x9 -> x12, starting transfers between devices: 15 us -> 19 us  [by_row(): return lax.ppermute(x, 'row', [(i, i ^ s) for i in range(row_count)])]
    pallas_call x8 -> x11, Pallas kernels: 7.8 us -> 9.67 us  [call(): pl.pallas_call(kernel, in_specs=in_specs or [VMEM] * len(args), out_specs...]
    unnamed x9 -> x11, local copies, waits for them, and re-layouts: 3.8 us -> 2.09 us
  transfers between devices with their start and end apart: 21 -> 31, of which waited for: 12 -> 11; matrix products, arithmetic and copies ran while one was open for 2% -> 1% of each run, Pallas kernels for 5% -> 11%
where the time goes in v3:
time: 65.2 us; the launch traced here: 65 us
  starting transfers between devices  36.2 us (56%)
  waiting for transfers between devices  15.6 us (24%)
  Pallas kernels  9.67 us (15%)
  local copies, waits for them, and re-layouts  2.09 us (3%)
  between operations  0.82 us (1%)
  other arithmetic  0.66 us (1%)
    ppermute x12, starting transfers between devices, by_row(): return lax.ppermute(x, 'row', [(i, i ^ s) for i in range(row_count)])  19 us
    ppermute x19, starting transfers between devices, by_col(): lax.ppermute(x, 'col', [(i, i ^ masks[i % 2]) for i in range(col_count)])  17.3 us
    ppermute x19, waiting for transfers between devices, by_col(): lax.ppermute(x, 'col', [(i, i ^ masks[i % 2]) for i in range(col_count)])  10.4 us
    pallas_call x11, Pallas kernels, call(): pl.pallas_call(kernel, in_specs=in_specs or [VMEM] * len(args), out_specs...  9.67 us
    ppermute x12, waiting for transfers between devices, by_row(): return lax.ppermute(x, 'row', [(i, i ^ s) for i in range(row_count)])  5.18 us
    unnamed x11, local copies, waits for them, and re-layouts  2.09 us
  transfers between devices with their start and end apart: 31, of which 11 were waited for; matrix products, arithmetic and copies ran while one was open for 1% of the time, Pallas kernels for 11%

profile of v3, /device:TPU:0, one launch (start us, length us, event | category | flops | bytes accessed | tf_op | source)
XLA Modules:
  0.0 65.0 jit_solution(17297771328622200854)
XLA Ops:
  0.0 0.5 collective-permute-start.2
  0.5 0.5 collective-permute-start.3
  1.0 1.6 %collective-permute-done.3 = s32[1,4]{1,0:T(1,128)S(1)} collective-permute-done((s32[1,4]{1,0:T(1,128)}, s32[1,4]{1,0:T(1,128)S(1)}, u32[]{:S(2)}, u32[]{:S(2)}) %collective-permute-start.3) | collective-permute-done | bytes 48 | tf_op jit(solution)/shard_map/ppermute | solution.py:140
  2.6 0.7 %pad_add_fusion.refs_0_ = s32[2,4]{1,0:T(2,128)S(1)} fusion(s32[1,4]{1,0:T(1,128)S(1)} %collective-permute-done.3, s32[1,4]{1,0:T(1,128)} %param.11), kind=kLoop, calls=%fused_computation | loop fusion | flops 8 | bytes 64 | tf_op jit(solution)/shard_map/concatenate | solution.py:151
  3.2 5.0 %collective-permute-start.6 = (s32[2,4]{1,0:T(2,128)S(1)}, s32[2,4]{1,0:T(2,128)S(1)}, u32[]{:S(2)}, u32[]{:S(2)}) collective-permute-start(s32[2,4]{1,0:T(2,128)S(1)} %pad_add_fusion.refs_0_), channel_id=1, source_target_pairs={{0,24},{8,16},{16,8},{24,0},{1,25},{9,17},{17,9},{25,1},{2,26},{10... | collective-permute-start | bytes 104 | tf_op jit(solution)/shard_map/ppermute | solution.py:146
  8.2 0.6 collective-permute-start.4
  8.8 1.0 %copy-done = bf16[512,512]{1,0:T(8,128)(2,1)S(1)} copy-done((bf16[512,512]{1,0:T(8,128)(2,1)S(1)}, bf16[512,512]{1,0:T(8,128)(2,1)}, u32[]{:S(2)}) %copy-start) | copy-done | bytes 524312
  9.9 0.9 %copy-done.3 = bf16[256,512]{1,0:T(8,128)(2,1)S(1)} copy-done((bf16[256,512]{1,0:T(8,128)(2,1)S(1)}, bf16[256,512]{1,0:T(8,128)(2,1)}, u32[]{:S(2)}) %copy-start.3) | copy-done | bytes 262168
  10.8 0.3 project.1.refs_4_
  11.2 1.5 %collective-permute-done.5.refs_2_ = s32[2,4]{1,0:T(2,128)S(1)} collective-permute-done((s32[2,4]{1,0:T(2,128)S(1)}, s32[2,4]{1,0:T(2,128)S(1)}, u32[]{:S(2)}, u32[]{:S(2)}) %collective-permute-start.5) | collective-permute-done | bytes 64 | tf_op jit(solution)/shard_map/ppermute | solution.py:146
  12.7 0.6 select.1
  13.3 2.3 %collective-permute-start.8 = (bf16[2,128,256]{2,1,0:T(8,128)(2,1)S(1)}, bf16[2,128,256]{2,1,0:T(8,128)(2,1)S(1)}, u32[]{:S(2)}, u32[]{:S(2)}) collective-permute-start(bf16[2,128,256]{2,1,0:T(8,128)(2,1)S(1)} %get-tuple-element.42), channel_id=1, source_target_pairs={{0,24},{8,16},{16,8},{24,0},{1,25},{9,17},{17,9},{25,1},{2,26},{10... | collective-permute-start | bytes 393224 | tf_op jit(solution)/shard_map/ppermute | solution.py:146
  15.7 2.1 %collective-permute-start.10 = (bf16[2,128,256]{2,1,0:T(8,128)(2,1)S(1)}, bf16[2,128,256]{2,1,0:T(8,128)(2,1)S(1)}, u32[]{:S(2)}, u32[]{:S(2)}) collective-permute-start(bf16[2,128,256]{2,1,0:T(8,128)(2,1)S(1)} %get-tuple-element.44), channel_id=1, source_target_pairs={{0,8},{8,0},{16,24},{24,16},{1,9},{9,1},{17,25},{25,17},{2,10},{10... | collective-permute-start | bytes 393224 | tf_op jit(solution)/shard_map/ppermute | solution.py:146
  17.8 0.1 copy.9.own_at
  17.9 1.3 %collective-permute-done.1.peer_count = s32[1]{0:T(128)} collective-permute-done((s32[1]{0:T(128)}, s32[1]{0:T(128)}, u32[]{:S(2)}, u32[]{:S(2)}) %collective-permute-start.1) | collective-permute-done | bytes 36 | tf_op jit(solution)/shard_map/ppermute | solution.py:140
  19.2 0.2 collective-permute-start
  20.0 0.3 collective-permute-done.peer_at
  20.4 2.3 %build.1 = (bf16[2,8,128,512]{3,2,1,0:T(8,128)(2,1)S(1)}, s32[2,8]{1,0:T(2,128)S(1)}) custom-call(s32[1,16,2]{2,1,0:T(8,128)S(1)} %copy.9.own_at, s32[1,16,2]{2,1,0:T(8,128)S(1)} %collective-permute-done.peer_at, s32[1]{0:T(128)S(6)} %copy.10.own_count, s32[1]{0:T(128)} %collective-permute-done.1.peer_count, bf16[1,16,128,128]{3,2,1,0:T(8,128)(2,1)S(1)} %copy-done.1, ...), custom_call_target="tpu_custom_call" | custom-call | flops 1000000000 | bytes 10000000 | tf_op jit(solution)/shard_map/build/pallas_call | solution.py:129
  22.7 3.6 %collective-permute-done.9.refs_4_ = bf16[2,128,256]{2,1,0:T(8,128)(2,1)S(1)} collective-permute-done((bf16[2,128,256]{2,1,0:T(8,128)(2,1)S(1)}, bf16[2,128,256]{2,1,0:T(8,128)(2,1)S(1)}, u32[]{:S(2)}, u32[]{:S(2)}) %collective-permute-start.9) | collective-permute-done | bytes 131104 | tf_op jit(solution)/shard_map/ppermute | solution.py:146
  26.3 1.3 %multiply.3 = (bf16[2,2,128,128]{3,2,1,0:T(8,128)(2,1)S(1)}, bf16[2,2,128,128]{3,2,1,0:T(8,128)(2,1)S(1)}, bf16[2,2,128,128]{3,2,1,0:T(8,128)(2,1)S(1)}, bf16[2,...) custom-call(s32[2,8]{1,0:T(2,128)S(1)} %get-tuple-element.39.refs_0_, ...), custom_call_target="tpu_custom_call" | custom-call | flops 1000000000 | bytes 10000000 | tf_op jit(solution)/shard_map/multiply/pallas_call | solution.py:129
  27.6 1.6 %collective-permute-start.20 = (bf16[2,2,128,128]{3,2,1,0:T(8,128)(2,1)S(1)}, bf16[2,2,128,128]{3,2,1,0:T(8,128)(2,1)S(1)}, u32[]{:S(2)}, u32[]{:S(2)}) collective-permute-start(bf16[2,2,128,128]{3,2,1,0:T(8,128)(2,1)S(1)} %get-tuple-element.59), channel_id=1, source_target_pairs={{0,2},{1,3},{2,0},{3,1},{4,6},{5,7},{6,4},{7,5},{8,10},{9,11},{10,... | collective-permute-start | bytes 393224 | tf_op jit(solution)/shard_map/ppermute | solution.py:140
  29.2 1.5 %collective-permute-start.21 = (bf16[2,2,128,128]{3,2,1,0:T(8,128)(2,1)S(1)}, bf16[2,2,128,128]{3,2,1,0:T(8,128)(2,1)S(1)}, u32[]{:S(2)}, u32[]{:S(2)}) collective-permute-start(bf16[2,2,128,128]{3,2,1,0:T(8,128)(2,1)S(1)} %get-tuple-element.60), channel_id=1, source_target_pairs={{0,4},{1,5},{2,6},{3,7},{4,0},{5,1},{6,2},{7,3},{8,12},{9,13},{10,... | collective-permute-start | bytes 393224 | tf_op jit(solution)/shard_map/ppermute | solution.py:140
  30.7 0.5 collective-permute-start.22
  31.2 1.5 %collective-permute-start.11 = (bf16[2,2,128,128]{3,2,1,0:T(8,128)(2,1)S(1)}, bf16[2,2,128,128]{3,2,1,0:T(8,128)(2,1)S(1)}, u32[]{:S(2)}, u32[]{:S(2)}) collective-permute-start(bf16[2,2,128,128]{3,2,1,0:T(8,128)(2,1)S(1)} %get-tuple-element.46), channel_id=1, source_target_pairs={{0,2},{1,3},{2,0},{3,1},{4,6},{5,7},{6,4},{7,5},{8,10},{9,11},{10,... | collective-permute-start | bytes 393224 | tf_op jit(solution)/shard_map/ppermute | solution.py:140
  32.7 1.5 %collective-permute-start.12 = (bf16[2,2,128,128]{3,2,1,0:T(8,128)(2,1)S(1)}, bf16[2,2,128,128]{3,2,1,0:T(8,128)(2,1)S(1)}, u32[]{:S(2)}, u32[]{:S(2)}) collective-permute-start(bf16[2,2,128,128]{3,2,1,0:T(8,128)(2,1)S(1)} %get-tuple-element.47), channel_id=1, source_target_pairs={{0,4},{1,5},{2,6},{3,7},{4,0},{5,1},{6,2},{7,3},{8,12},{9,13},{10,... | collective-permute-start | bytes 393224 | tf_op jit(solution)/shard_map/ppermute | solution.py:140
  34.2 2.3 %collective-permute-start.13 = (bf16[2,2,128,128]{3,2,1,0:T(8,128)(2,1)S(1)}, bf16[2,2,128,128]{3,2,1,0:T(8,128)(2,1)S(1)}, u32[]{:S(2)}, u32[]{:S(2)}) collective-permute-start(bf16[2,2,128,128]{3,2,1,0:T(8,128)(2,1)S(1)} %get-tuple-element.48), channel_id=1, source_target_pairs={{0,6},{1,7},{2,4},{3,5},{4,2},{5,3},{6,0},{7,1},{8,14},{9,15},{10,... | collective-permute-start | bytes 393224 | tf_op jit(solution)/shard_map/ppermute | solution.py:140
  36.5 2.1 %collective-permute-done.21.refs_6_ = bf16[2,2,128,128]{3,2,1,0:T(8,128)(2,1)S(1)} collective-permute-done((bf16[2,2,128,128]{3,2,1,0:T(8,128)(2,1)S(1)}, bf16[2,2,128,128]{3,2,1,0:T(8,128)(2,1)S(1)}, u32[]{:S(2)}, u32[]{:S(2)}) %collective-permute-start.21) | collective-permute-done | bytes 131104 | tf_op jit(solution)/shard_map/ppermute | solution.py:140
  38.6 0.7 %hidden.3 = (bf16[2,128,128]{2,1,0:T(8,128)(2,1)S(1)}, bf16[2,128,128]{2,1,0:T(8,128)(2,1)S(1)}, bf16[2,128,128]{2,1,0:T(8,128)(2,1)S(1)}, bf16[2,128,128]{2,1,0:T(8,128)(2,1)S(1)}) custom-call(s32[2,4]{1,0:T(2,128)S(1)} %pad_add_fusion.refs_0_, s32[2,4]{1,0:T(2,128)S(1)} %collective-permute-done.4.refs_1_, s32[2,4]{1,0:T(2,128)S(1)} %collective-permute-done.5.refs_2_, ...), custom_call_target="tpu_custom_call" | custom-call | flops 1000000000 | bytes 10000000 | tf_op jit(solution)/shard_map/hidden/pallas_call | solution.py:129
  39.3 2.3 %collective-permute-start.23 = (bf16[2,128,128]{2,1,0:T(8,128)(2,1)S(1)}, bf16[2,128,128]{2,1,0:T(8,128)(2,1)S(1)}, u32[]{:S(2)}, u32[]{:S(2)}) collective-permute-start(bf16[2,128,128]{2,1,0:T(8,128)(2,1)S(1)} %get-tuple-element.63), channel_id=1, source_target_pairs={{0,24},{8,16},{16,8},{24,0},{1,25},{9,17},{17,9},{25,1},{2,26},{10... | collective-permute-start | bytes 196616 | tf_op jit(solution)/shard_map/ppermute | solution.py:146
  41.5 2.2 %collective-permute-start.25 = (bf16[2,128,128]{2,1,0:T(8,128)(2,1)S(1)}, bf16[2,128,128]{2,1,0:T(8,128)(2,1)S(1)}, u32[]{:S(2)}, u32[]{:S(2)}) collective-permute-start(bf16[2,128,128]{2,1,0:T(8,128)(2,1)S(1)} %get-tuple-element.65), channel_id=1, source_target_pairs={{0,8},{8,0},{16,24},{24,16},{1,9},{9,1},{17,25},{25,17},{2,10},{10... | collective-permute-start | bytes 196616 | tf_op jit(solution)/shard_map/ppermute | solution.py:146
  43.7 0.7 %hidden.2 = (bf16[2,128,128]{2,1,0:T(8,128)(2,1)S(1)}, bf16[2,128,128]{2,1,0:T(8,128)(2,1)S(1)}, bf16[2,128,128]{2,1,0:T(8,128)(2,1)S(1)}, bf16[2,128,128]{2,1,0:T(8,128)(2,1)S(1)}) custom-call(s32[2,4]{1,0:T(2,128)S(1)} %pad_add_fusion.refs_0_, s32[2,4]{1,0:T(2,128)S(1)} %collective-permute-done.4.refs_1_, s32[2,4]{1,0:T(2,128)S(1)} %collective-permute-done.5.refs_2_, ...), custom_call_target="tpu_custom_call" | custom-call | flops 1000000000 | bytes 10000000 | tf_op jit(solution)/shard_map/hidden/pallas_call | solution.py:129
  44.4 2.3 %collective-permute-start.14 = (bf16[2,128,128]{2,1,0:T(8,128)(2,1)S(1)}, bf16[2,128,128]{2,1,0:T(8,128)(2,1)S(1)}, u32[]{:S(2)}, u32[]{:S(2)}) collective-permute-start(bf16[2,128,128]{2,1,0:T(8,128)(2,1)S(1)} %get-tuple-element.50), channel_id=1, source_target_pairs={{0,24},{8,16},{16,8},{24,0},{1,25},{9,17},{17,9},{25,1},{2,26},{10... | collective-permute-start | bytes 196616 | tf_op jit(solution)/shard_map/ppermute | solution.py:146
  46.7 2.2 %collective-permute-start.16 = (bf16[2,128,128]{2,1,0:T(8,128)(2,1)S(1)}, bf16[2,128,128]{2,1,0:T(8,128)(2,1)S(1)}, u32[]{:S(2)}, u32[]{:S(2)}) collective-permute-start(bf16[2,128,128]{2,1,0:T(8,128)(2,1)S(1)} %get-tuple-element.52), channel_id=1, source_target_pairs={{0,8},{8,0},{16,24},{24,16},{1,9},{9,1},{17,25},{25,17},{2,10},{10... | collective-permute-start | bytes 196616 | tf_op jit(solution)/shard_map/ppermute | solution.py:146
  48.9 1.2 %multiply.5 = (bf16[2,2,128,128]{3,2,1,0:T(8,128)(2,1)S(1)}, bf16[2,2,128,128]{3,2,1,0:T(8,128)(2,1)S(1)}, bf16[2,2,128,128]{3,2,1,0:T(8,128)(2,1)S(1)}, bf16[2,2,128,128]{3,2,1,0:T(8,128)(2,1)S(1)}) custom-call(s32[2,8]{1,0:T(2,128)S(1)} %get-tuple-element.39.refs_0_, bf16[2,8,128,512]{3,2,1,0:T(8,128)(2,1)S(1)} %get-tuple-element.40.refs_1_, ...), custom_call_target="tpu_custom_call" | custom-call | flops 1000000000 | bytes 10000000 | tf_op jit(solution)/shard_map/multiply/pallas_call | solution.py:129
  50.2 0.8 %collective-permute-start.26 = (bf16[2,2,128,128]{3,2,1,0:T(8,128)(2,1)S(1)}, bf16[2,2,128,128]{3,2,1,0:T(8,128)(2,1)S(1)}, u32[]{:S(2)}, u32[]{:S(2)}) collective-permute-start(bf16[2,2,128,128]{3,2,1,0:T(8,128)(2,1)S(1)} %get-tuple-element.67), channel_id=1, source_target_pairs={{0,2},{1,3},{2,0},{3,1},{4,6},{5,7},{6,4},{7,5},{8,10},{9,11},{10,... | collective-permute-start | bytes 393224 | tf_op jit(solution)/shard_map/ppermute | solution.py:140
  51.0 0.8 %collective-permute-start.27 = (bf16[2,2,128,128]{3,2,1,0:T(8,128)(2,1)S(1)}, bf16[2,2,128,128]{3,2,1,0:T(8,128)(2,1)S(1)}, u32[]{:S(2)}, u32[]{:S(2)}) collective-permute-start(bf16[2,2,128,128]{3,2,1,0:T(8,128)(2,1)S(1)} %get-tuple-element.68), channel_id=1, source_target_pairs={{0,4},{1,5},{2,6},{3,7},{4,0},{5,1},{6,2},{7,3},{8,12},{9,13},{10,... | collective-permute-start | bytes 393224 | tf_op jit(solution)/shard_map/ppermute | solution.py:140
  51.8 1.9 %collective-permute-start.28 = (bf16[2,2,128,128]{3,2,1,0:T(8,128)(2,1)S(1)}, bf16[2,2,128,128]{3,2,1,0:T(8,128)(2,1)S(1)}, u32[]{:S(2)}, u32[]{:S(2)}) collective-permute-start(bf16[2,2,128,128]{3,2,1,0:T(8,128)(2,1)S(1)} %get-tuple-element.69), channel_id=1, source_target_pairs={{0,6},{1,7},{2,4},{3,5},{4,2},{5,3},{6,0},{7,1},{8,14},{9,15},{10,... | collective-permute-start | bytes 393224 | tf_op jit(solution)/shard_map/ppermute | solution.py:140
  53.7 1.2 %multiply.4 = (bf16[2,2,128,128]{3,2,1,0:T(8,128)(2,1)S(1)}, bf16[2,2,128,128]{3,2,1,0:T(8,128)(2,1)S(1)}, bf16[2,2,128,128]{3,2,1,0:T(8,128)(2,1)S(1)}, bf16[2,2,128,128]{3,2,1,0:T(8,128)(2,1)S(1)}) custom-call(s32[2,8]{1,0:T(2,128)S(1)} %get-tuple-element.39.refs_0_, bf16[2,8,128,512]{3,2,1,0:T(8,128)(2,1)S(1)} %get-tuple-element.40.refs_1_, ...), custom_call_target="tpu_custom_call" | custom-call | flops 1000000000 | bytes 10000000 | tf_op jit(solution)/shard_map/multiply/pallas_call | solution.py:129
  55.0 0.8 %collective-permute-start.17 = (bf16[2,2,128,128]{3,2,1,0:T(8,128)(2,1)S(1)}, bf16[2,2,128,128]{3,2,1,0:T(8,128)(2,1)S(1)}, u32[]{:S(2)}, u32[]{:S(2)}) collective-permute-start(bf16[2,2,128,128]{3,2,1,0:T(8,128)(2,1)S(1)} %get-tuple-element.54), channel_id=1, source_target_pairs={{0,2},{1,3},{2,0},{3,1},{4,6},{5,7},{6,4},{7,5},{8,10},{9,11},{10,... | collective-permute-start | bytes 393224 | tf_op jit(solution)/shard_map/ppermute | solution.py:140
  55.8 0.8 %collective-permute-start.18 = (bf16[2,2,128,128]{3,2,1,0:T(8,128)(2,1)S(1)}, bf16[2,2,128,128]{3,2,1,0:T(8,128)(2,1)S(1)}, u32[]{:S(2)}, u32[]{:S(2)}) collective-permute-start(bf16[2,2,128,128]{3,2,1,0:T(8,128)(2,1)S(1)} %get-tuple-element.55), channel_id=1, source_target_pairs={{0,4},{1,5},{2,6},{3,7},{4,0},{5,1},{6,2},{7,3},{8,12},{9,13},{10,... | collective-permute-start | bytes 393224 | tf_op jit(solution)/shard_map/ppermute | solution.py:140
  56.6 1.9 %collective-permute-start.19 = (bf16[2,2,128,128]{3,2,1,0:T(8,128)(2,1)S(1)}, bf16[2,2,128,128]{3,2,1,0:T(8,128)(2,1)S(1)}, u32[]{:S(2)}, u32[]{:S(2)}) collective-permute-start(bf16[2,2,128,128]{3,2,1,0:T(8,128)(2,1)S(1)} %get-tuple-element.56), channel_id=1, source_target_pairs={{0,6},{1,7},{2,4},{3,5},{4,2},{5,3},{6,0},{7,1},{8,14},{9,15},{10,... | collective-permute-start | bytes 393224 | tf_op jit(solution)/shard_map/ppermute | solution.py:140
  58.6 0.5 collective-permute-done.28.refs_3_
  59.1 0.1 mixed.3
  59.3 0.8 %collective-permute-done.17.refs_1_ = bf16[2,2,128,128]{3,2,1,0:T(8,128)(2,1)S(1)} collective-permute-done((bf16[2,2,128,128]{3,2,1,0:T(8,128)(2,1)S(1)}, bf16[2,2,128,128]{3,2,1,0:T(8,128)(2,1)S(1)}, u32[]{:S(2)}, u32[]{:S(2)}) %collective-permute-start.17) | collective-permute-done | bytes 131104 | tf_op jit(solution)/shard_map/ppermute | solution.py:140
  60.0 0.8 %collective-permute-done.18.refs_2_ = bf16[2,2,128,128]{3,2,1,0:T(8,128)(2,1)S(1)} collective-permute-done((bf16[2,2,128,128]{3,2,1,0:T(8,128)(2,1)S(1)}, bf16[2,2,128,128]{3,2,1,0:T(8,128)(2,1)S(1)}, u32[]{:S(2)}, u32[]{:S(2)}) %collective-permute-start.18) | collective-permute-done | bytes 131104 | tf_op jit(solution)/shard_map/ppermute | solution.py:140
  60.8 1.7 %collective-permute-done.19.refs_3_ = bf16[2,2,128,128]{3,2,1,0:T(8,128)(2,1)S(1)} collective-permute-done((bf16[2,2,128,128]{3,2,1,0:T(8,128)(2,1)S(1)}, bf16[2,2,128,128]{3,2,1,0:T(8,128)(2,1)S(1)}, u32[]{:S(2)}, u32[]{:S(2)}) %collective-permute-start.19) | collective-permute-done | bytes 131104 | tf_op jit(solution)/shard_map/ppermute | solution.py:140
  62.7 1.2 %collective-permute-done.29.refs_2_ = bf16[2,128,128]{2,1,0:T(8,128)(2,1)S(1)} collective-permute-done((bf16[2,128,128]{2,1,0:T(8,128)(2,1)S(1)}, bf16[2,128,128]{2,1,0:T(8,128)(2,1)S(1)}, u32[]{:S(2)}, u32[]{:S(2)}) %collective-permute-start.29) | collective-permute-done | bytes 65568 | tf_op jit(solution)/shard_map/ppermute | solution.py:140
  63.9 1.1 %final.1 = bf16[256,512]{1,0:T(8,128)(2,1)} custom-call(bf16[2,128,128]{2,1,0:T(8,128)(2,1)S(1)} %get-tuple-element.57.refs_0_, bf16[2,128,128]{2,1,0:T(8,128)(2,1)S(1)} %get-tuple-element.70.refs_1_, bf16[2,128,128]{2,1,0:T(8,128)(2,1)S(1)} %collective-permute-done.29.refs_2_, bf16[2,128,128]{2,1,0:T(8,128)(2,1)S(1)} %collective-permute-done.30.refs_3_, ...), custom_call_target="tpu_custom_call" | custom-call | flops 1000000000 | bytes 10000000 | tf_op jit(solution)/shard_map/final/pallas_call | solution.py:129
  (37 shorter events, 0.4 us)
Async XLA Ops:
  0.0 20.4 %collective-permute-start.2 = (bf16[1,16,128,128]{3,2,1,0:T(8,128)(2,1)}, bf16[1,16,128,128]{3,2,1,0:T(8,128)(2,1)S(1)}, u32[]{:S(2)}, u32[]{:S(2)}) collective-permute-start(bf16[1,16,128,128]{3,2,1,0:T(8,128)(2,1)} %own_tiles.1), channel_id=1, source_target_pairs={{0,1},{1,0},{2,3},{3,2},{4,5},{5,4},{6,7},{7,6},{8,9},{9,8},{10,11... | collective-permute-start | bytes 1572872 | tf_op jit(solution)/shard_map/ppermute | solution.py:140
  0.5 8.4 %collective-permute-start.7 = (bf16[256,512]{1,0:T(8,128)(2,1)}, bf16[256,512]{1,0:T(8,128)(2,1)S(1)}, u32[]{:S(2)}, u32[]{:S(2)}) collective-permute-start(bf16[256,512]{1,0:T(8,128)(2,1)} %own.1), channel_id=1, source_target_pairs={{0,1},{1,0},{2,3},{3,2},{4,5},{5,4},{6,7},{7,6},{8,9},{9,8},{10,11... | collective-permute-start | bytes 786440 | tf_op jit(solution)/shard_map/ppermute | solution.py:140
  0.5 2.1 %collective-permute-start.3 = (s32[1,4]{1,0:T(1,128)}, s32[1,4]{1,0:T(1,128)S(1)}, u32[]{:S(2)}, u32[]{:S(2)}) collective-permute-start(s32[1,4]{1,0:T(1,128)} %param.11), channel_id=1, source_target_pairs={{0,1},{1,0},{2,3},{3,2},{4,5},{5,4},{6,7},{7,6},{8,9},{9,8},{10,11... | collective-permute-start | bytes 56 | tf_op jit(solution)/shard_map/ppermute | solution.py:140
  3.2 7.9 %collective-permute-start.6 = (s32[2,4]{1,0:T(2,128)S(1)}, s32[2,4]{1,0:T(2,128)S(1)}, u32[]{:S(2)}, u32[]{:S(2)}) collective-permute-start(s32[2,4]{1,0:T(2,128)S(1)} %pad_add_fusion.refs_0_), channel_id=1, source_target_pairs={{0,24},{8,16},{16,8},{24,0},{1,25},{9,17},{17,9},{25,1},{2,26},{10... | collective-permute-start | bytes 104 | tf_op jit(solution)/shard_map/ppermute | solution.py:146
  8.2 4.5 %collective-permute-start.5 = (s32[2,4]{1,0:T(2,128)S(1)}, s32[2,4]{1,0:T(2,128)S(1)}, u32[]{:S(2)}, u32[]{:S(2)}) collective-permute-start(s32[2,4]{1,0:T(2,128)S(1)} %pad_add_fusion.refs_0_), channel_id=1, source_target_pairs={{0,16},{8,24},{16,0},{24,8},{1,17},{9,25},{17,1},{25,9},{2,18},{10... | collective-permute-start | bytes 104 | tf_op jit(solution)/shard_map/ppermute | solution.py:146
  8.2 4.5 %collective-permute-start.4 = (s32[2,4]{1,0:T(2,128)S(1)}, s32[2,4]{1,0:T(2,128)S(1)}, u32[]{:S(2)}, u32[]{:S(2)}) collective-permute-start(s32[2,4]{1,0:T(2,128)S(1)} %pad_add_fusion.refs_0_), channel_id=1, source_target_pairs={{0,8},{8,0},{16,24},{24,16},{1,9},{9,1},{17,25},{25,17},{2,10},{10... | collective-permute-start | bytes 104 | tf_op jit(solution)/shard_map/ppermute | solution.py:146
  8.8 1.0 %copy-start = (bf16[512,512]{1,0:T(8,128)(2,1)S(1)}, bf16[512,512]{1,0:T(8,128)(2,1)}, u32[]{:S(2)}) copy-start(bf16[512,512]{1,0:T(8,128)(2,1)} %weight.1) | copy-start | bytes 1572868
  9.9 0.9 %copy-start.3 = (bf16[256,512]{1,0:T(8,128)(2,1)S(1)}, bf16[256,512]{1,0:T(8,128)(2,1)}, u32[]{:S(2)}) copy-start(bf16[256,512]{1,0:T(8,128)(2,1)} %own.1) | copy-start | bytes 786436
  11.1 6.6 %copy-start.4 = (s32[1,16,2]{1,2,0:T(2,128)S(1)}, s32[1,16,2]{1,2,0:T(2,128)}, u32[]{:S(2)}) copy-start(s32[1,16,2]{1,2,0:T(2,128)} %param.9) | copy-start | bytes 388
  11.2 9.2 %copy-start.1 = (bf16[1,16,128,128]{3,2,1,0:T(8,128)(2,1)S(1)}, bf16[1,16,128,128]{3,2,1,0:T(8,128)(2,1)}, u32[]{:S(2)}) copy-start(bf16[1,16,128,128]{3,2,1,0:T(8,128)(2,1)} %own_tiles.1) | copy-start | bytes 1572868
  13.3 9.3 %collective-permute-start.8 = (bf16[2,128,256]{2,1,0:T(8,128)(2,1)S(1)}, bf16[2,128,256]{2,1,0:T(8,128)(2,1)S(1)}, u32[]{:S(2)}, u32[]{:S(2)}) collective-permute-start(bf16[2,128,256]{2,1,0:T(8,128)(2,1)S(1)} %get-tuple-element.42), channel_id=1, source_target_pairs={{0,24},{8,16},{16,8},{24,0},{1,25},{9,17},{17,9},{25,1},{2,26},{10... | collective-permute-start | bytes 393224 | tf_op jit(solution)/shard_map/ppermute | solution.py:146
  15.7 10.7 %collective-permute-start.9 = (bf16[2,128,256]{2,1,0:T(8,128)(2,1)S(1)}, bf16[2,128,256]{2,1,0:T(8,128)(2,1)S(1)}, u32[]{:S(2)}, u32[]{:S(2)}) collective-permute-start(bf16[2,128,256]{2,1,0:T(8,128)(2,1)S(1)} %get-tuple-element.43), channel_id=1, source_target_pairs={{0,16},{8,24},{16,0},{24,8},{1,17},{9,25},{17,1},{25,9},{2,18},{10... | collective-permute-start | bytes 393224 | tf_op jit(solution)/shard_map/ppermute | solution.py:146
  15.7 10.7 %collective-permute-start.10 = (bf16[2,128,256]{2,1,0:T(8,128)(2,1)S(1)}, bf16[2,128,256]{2,1,0:T(8,128)(2,1)S(1)}, u32[]{:S(2)}, u32[]{:S(2)}) collective-permute-start(bf16[2,128,256]{2,1,0:T(8,128)(2,1)S(1)} %get-tuple-element.44), channel_id=1, source_target_pairs={{0,8},{8,0},{16,24},{24,16},{1,9},{9,1},{17,25},{25,17},{2,10},{10... | collective-permute-start | bytes 393224 | tf_op jit(solution)/shard_map/ppermute | solution.py:146
  17.8 1.4 %collective-permute-start.1 = (s32[1]{0:T(128)}, s32[1]{0:T(128)}, u32[]{:S(2)}, u32[]{:S(2)}) collective-permute-start(s32[1]{0:T(128)} %param.10), channel_id=1, source_target_pairs={{0,1},{1,0},{2,3},{3,2},{4,5},{5,4},{6,7},{7,6},{8,9},{9,8},{10,11... | collective-permute-start | bytes 20 | tf_op jit(solution)/shard_map/ppermute | solution.py:140
  19.2 1.2 %collective-permute-start = (s32[1,16,2]{2,1,0:T(8,128)S(1)}, s32[1,16,2]{2,1,0:T(8,128)S(1)}, u32[]{:S(2)}, u32[]{:S(2)}) collective-permute-start(s32[1,16,2]{2,1,0:T(8,128)S(1)} %copy.9.own_at), channel_id=1, source_target_pairs={{0,1},{1,0},{2,3},{3,2},{4,5},{5,4},{6,7},{7,6},{8,9},{9,8},{10,11... | collective-permute-start | bytes 392 | tf_op jit(solution)/shard_map/ppermute | solution.py:140
  27.6 6.6 %collective-permute-start.20 = (bf16[2,2,128,128]{3,2,1,0:T(8,128)(2,1)S(1)}, bf16[2,2,128,128]{3,2,1,0:T(8,128)(2,1)S(1)}, u32[]{:S(2)}, u32[]{:S(2)}) collective-permute-start(bf16[2,2,128,128]{3,2,1,0:T(8,128)(2,1)S(1)} %get-tuple-element.59), channel_id=1, source_target_pairs={{0,2},{1,3},{2,0},{3,1},{4,6},{5,7},{6,4},{7,5},{8,10},{9,11},{10,... | collective-permute-start | bytes 393224 | tf_op jit(solution)/shard_map/ppermute | solution.py:140
  29.2 9.4 %collective-permute-start.21 = (bf16[2,2,128,128]{3,2,1,0:T(8,128)(2,1)S(1)}, bf16[2,2,128,128]{3,2,1,0:T(8,128)(2,1)S(1)}, u32[]{:S(2)}, u32[]{:S(2)}) collective-permute-start(bf16[2,2,128,128]{3,2,1,0:T(8,128)(2,1)S(1)} %get-tuple-element.60), channel_id=1, source_target_pairs={{0,4},{1,5},{2,6},{3,7},{4,0},{5,1},{6,2},{7,3},{8,12},{9,13},{10,... | collective-permute-start | bytes 393224 | tf_op jit(solution)/shard_map/ppermute | solution.py:140
  30.7 7.9 %collective-permute-start.22 = (bf16[2,2,128,128]{3,2,1,0:T(8,128)(2,1)S(1)}, bf16[2,2,128,128]{3,2,1,0:T(8,128)(2,1)S(1)}, u32[]{:S(2)}, u32[]{:S(2)}) collective-permute-start(bf16[2,2,128,128]{3,2,1,0:T(8,128)(2,1)S(1)} %get-tuple-element.61), channel_id=1, source_target_pairs={{0,6},{1,7},{2,4},{3,5},{4,2},{5,3},{6,0},{7,1},{8,14},{9,15},{10,... | collective-permute-start | bytes 393224 | tf_op jit(solution)/shard_map/ppermute | solution.py:140
  31.2 10.4 %collective-permute-start.11 = (bf16[2,2,128,128]{3,2,1,0:T(8,128)(2,1)S(1)}, bf16[2,2,128,128]{3,2,1,0:T(8,128)(2,1)S(1)}, u32[]{:S(2)}, u32[]{:S(2)}) collective-permute-start(bf16[2,2,128,128]{3,2,1,0:T(8,128)(2,1)S(1)} %get-tuple-element.46), channel_id=1, source_target_pairs={{0,2},{1,3},{2,0},{3,1},{4,6},{5,7},{6,4},{7,5},{8,10},{9,11},{10,... | collective-permute-start | bytes 393224 | tf_op jit(solution)/shard_map/ppermute | solution.py:140
  32.7 11.1 %collective-permute-start.12 = (bf16[2,2,128,128]{3,2,1,0:T(8,128)(2,1)S(1)}, bf16[2,2,128,128]{3,2,1,0:T(8,128)(2,1)S(1)}, u32[]{:S(2)}, u32[]{:S(2)}) collective-permute-start(bf16[2,2,128,128]{3,2,1,0:T(8,128)(2,1)S(1)} %get-tuple-element.47), channel_id=1, source_target_pairs={{0,4},{1,5},{2,6},{3,7},{4,0},{5,1},{6,2},{7,3},{8,12},{9,13},{10,... | collective-permute-start | bytes 393224 | tf_op jit(solution)/shard_map/ppermute | solution.py:140
  34.2 9.6 %collective-permute-start.13 = (bf16[2,2,128,128]{3,2,1,0:T(8,128)(2,1)S(1)}, bf16[2,2,128,128]{3,2,1,0:T(8,128)(2,1)S(1)}, u32[]{:S(2)}, u32[]{:S(2)}) collective-permute-start(bf16[2,2,128,128]{3,2,1,0:T(8,128)(2,1)S(1)} %get-tuple-element.48), channel_id=1, source_target_pairs={{0,6},{1,7},{2,4},{3,5},{4,2},{5,3},{6,0},{7,1},{8,14},{9,15},{10,... | collective-permute-start | bytes 393224 | tf_op jit(solution)/shard_map/ppermute | solution.py:140
  39.3 7.4 %collective-permute-start.23 = (bf16[2,128,128]{2,1,0:T(8,128)(2,1)S(1)}, bf16[2,128,128]{2,1,0:T(8,128)(2,1)S(1)}, u32[]{:S(2)}, u32[]{:S(2)}) collective-permute-start(bf16[2,128,128]{2,1,0:T(8,128)(2,1)S(1)} %get-tuple-element.63), channel_id=1, source_target_pairs={{0,24},{8,16},{16,8},{24,0},{1,25},{9,17},{17,9},{25,1},{2,26},{10... | collective-permute-start | bytes 196616 | tf_op jit(solution)/shard_map/ppermute | solution.py:146
  41.5 7.4 %collective-permute-start.24 = (bf16[2,128,128]{2,1,0:T(8,128)(2,1)S(1)}, bf16[2,128,128]{2,1,0:T(8,128)(2,1)S(1)}, u32[]{:S(2)}, u32[]{:S(2)}) collective-permute-start(bf16[2,128,128]{2,1,0:T(8,128)(2,1)S(1)} %get-tuple-element.64), channel_id=1, source_target_pairs={{0,16},{8,24},{16,0},{24,8},{1,17},{9,25},{17,1},{25,9},{2,18},{10... | collective-permute-start | bytes 196616 | tf_op jit(solution)/shard_map/ppermute | solution.py:146
  41.5 7.4 %collective-permute-start.25 = (bf16[2,128,128]{2,1,0:T(8,128)(2,1)S(1)}, bf16[2,128,128]{2,1,0:T(8,128)(2,1)S(1)}, u32[]{:S(2)}, u32[]{:S(2)}) collective-permute-start(bf16[2,128,128]{2,1,0:T(8,128)(2,1)S(1)} %get-tuple-element.65), channel_id=1, source_target_pairs={{0,8},{8,0},{16,24},{24,16},{1,9},{9,1},{17,25},{25,17},{2,10},{10... | collective-permute-start | bytes 196616 | tf_op jit(solution)/shard_map/ppermute | solution.py:146
  44.4 7.4 %collective-permute-start.14 = (bf16[2,128,128]{2,1,0:T(8,128)(2,1)S(1)}, bf16[2,128,128]{2,1,0:T(8,128)(2,1)S(1)}, u32[]{:S(2)}, u32[]{:S(2)}) collective-permute-start(bf16[2,128,128]{2,1,0:T(8,128)(2,1)S(1)} %get-tuple-element.50), channel_id=1, source_target_pairs={{0,24},{8,16},{16,8},{24,0},{1,25},{9,17},{17,9},{25,1},{2,26},{10... | collective-permute-start | bytes 196616 | tf_op jit(solution)/shard_map/ppermute | solution.py:146
  46.7 7.0 %collective-permute-start.15 = (bf16[2,128,128]{2,1,0:T(8,128)(2,1)S(1)}, bf16[2,128,128]{2,1,0:T(8,128)(2,1)S(1)}, u32[]{:S(2)}, u32[]{:S(2)}) collective-permute-start(bf16[2,128,128]{2,1,0:T(8,128)(2,1)S(1)} %get-tuple-element.51), channel_id=1, source_target_pairs={{0,16},{8,24},{16,0},{24,8},{1,17},{9,25},{17,1},{25,9},{2,18},{10... | collective-permute-start | bytes 196616 | tf_op jit(solution)/shard_map/ppermute | solution.py:146
  46.7 7.0 %collective-permute-start.16 = (bf16[2,128,128]{2,1,0:T(8,128)(2,1)S(1)}, bf16[2,128,128]{2,1,0:T(8,128)(2,1)S(1)}, u32[]{:S(2)}, u32[]{:S(2)}) collective-permute-start(bf16[2,128,128]{2,1,0:T(8,128)(2,1)S(1)} %get-tuple-element.52), channel_id=1, source_target_pairs={{0,8},{8,0},{16,24},{24,16},{1,9},{9,1},{17,25},{25,17},{2,10},{10... | collective-permute-start | bytes 196616 | tf_op jit(solution)/shard_map/ppermute | solution.py:146
  50.2 6.5 %collective-permute-start.26 = (bf16[2,2,128,128]{3,2,1,0:T(8,128)(2,1)S(1)}, bf16[2,2,128,128]{3,2,1,0:T(8,128)(2,1)S(1)}, u32[]{:S(2)}, u32[]{:S(2)}) collective-permute-start(bf16[2,2,128,128]{3,2,1,0:T(8,128)(2,1)S(1)} %get-tuple-element.67), channel_id=1, source_target_pairs={{0,2},{1,3},{2,0},{3,1},{4,6},{5,7},{6,4},{7,5},{8,10},{9,11},{10,... | collective-permute-start | bytes 393224 | tf_op jit(solution)/shard_map/ppermute | solution.py:140
  51.0 7.5 %collective-permute-start.27 = (bf16[2,2,128,128]{3,2,1,0:T(8,128)(2,1)S(1)}, bf16[2,2,128,128]{3,2,1,0:T(8,128)(2,1)S(1)}, u32[]{:S(2)}, u32[]{:S(2)}) collective-permute-start(bf16[2,2,128,128]{3,2,1,0:T(8,128)(2,1)S(1)} %get-tuple-element.68), channel_id=1, source_target_pairs={{0,4},{1,5},{2,6},{3,7},{4,0},{5,1},{6,2},{7,3},{8,12},{9,13},{10,... | collective-permute-start | bytes 393224 | tf_op jit(solution)/shard_map/ppermute | solution.py:140
  51.8 7.3 %collective-permute-start.28 = (bf16[2,2,128,128]{3,2,1,0:T(8,128)(2,1)S(1)}, bf16[2,2,128,128]{3,2,1,0:T(8,128)(2,1)S(1)}, u32[]{:S(2)}, u32[]{:S(2)}) collective-permute-start(bf16[2,2,128,128]{3,2,1,0:T(8,128)(2,1)S(1)} %get-tuple-element.69), channel_id=1, source_target_pairs={{0,6},{1,7},{2,4},{3,5},{4,2},{5,3},{6,0},{7,1},{8,14},{9,15},{10,... | collective-permute-start | bytes 393224 | tf_op jit(solution)/shard_map/ppermute | solution.py:140
  55.0 5.0 %collective-permute-start.17 = (bf16[2,2,128,128]{3,2,1,0:T(8,128)(2,1)S(1)}, bf16[2,2,128,128]{3,2,1,0:T(8,128)(2,1)S(1)}, u32[]{:S(2)}, u32[]{:S(2)}) collective-permute-start(bf16[2,2,128,128]{3,2,1,0:T(8,128)(2,1)S(1)} %get-tuple-element.54), channel_id=1, source_target_pairs={{0,2},{1,3},{2,0},{3,1},{4,6},{5,7},{6,4},{7,5},{8,10},{9,11},{10,... | collective-permute-start | bytes 393224 | tf_op jit(solution)/shard_map/ppermute | solution.py:140
  55.8 5.0 %collective-permute-start.18 = (bf16[2,2,128,128]{3,2,1,0:T(8,128)(2,1)S(1)}, bf16[2,2,128,128]{3,2,1,0:T(8,128)(2,1)S(1)}, u32[]{:S(2)}, u32[]{:S(2)}) collective-permute-start(bf16[2,2,128,128]{3,2,1,0:T(8,128)(2,1)S(1)} %get-tuple-element.55), channel_id=1, source_target_pairs={{0,4},{1,5},{2,6},{3,7},{4,0},{5,1},{6,2},{7,3},{8,12},{9,13},{10,... | collective-permute-start | bytes 393224 | tf_op jit(solution)/shard_map/ppermute | solution.py:140
  56.6 5.9 %collective-permute-start.19 = (bf16[2,2,128,128]{3,2,1,0:T(8,128)(2,1)S(1)}, bf16[2,2,128,128]{3,2,1,0:T(8,128)(2,1)S(1)}, u32[]{:S(2)}, u32[]{:S(2)}) collective-permute-start(bf16[2,2,128,128]{3,2,1,0:T(8,128)(2,1)S(1)} %get-tuple-element.56), channel_id=1, source_target_pairs={{0,6},{1,7},{2,4},{3,5},{4,2},{5,3},{6,0},{7,1},{8,14},{9,15},{10,... | collective-permute-start | bytes 393224 | tf_op jit(solution)/shard_map/ppermute | solution.py:140
  59.2 4.7 %copy-start.2 = (bf16[512,512]{1,0:T(8,128)(2,1)S(1)}, bf16[512,512]{1,0:T(8,128)(2,1)}, u32[]{:S(2)}) copy-start(bf16[512,512]{1,0:T(8,128)(2,1)} %refs_4_.1) | copy-start | bytes 1572868
  59.2 3.5 %collective-permute-start.30 = (bf16[2,128,128]{2,1,0:T(8,128)(2,1)S(1)}, bf16[2,128,128]{2,1,0:T(8,128)(2,1)S(1)}, u32[]{:S(2)}, u32[]{:S(2)}) collective-permute-start(bf16[2,128,128]{2,1,0:T(8,128)(2,1)S(1)} %get-tuple-element.72), channel_id=1, source_target_pairs={{0,1},{1,0},{2,3},{3,2},{4,5},{5,4},{6,7},{7,6},{8,9},{9,8},{10,11... | collective-permute-start | bytes 196616 | tf_op jit(solution)/shard_map/ppermute | solution.py:140
  62.6 1.3 %collective-permute-start.29 = (bf16[2,128,128]{2,1,0:T(8,128)(2,1)S(1)}, bf16[2,128,128]{2,1,0:T(8,128)(2,1)S(1)}, u32[]{:S(2)}, u32[]{:S(2)}) collective-permute-start(bf16[2,128,128]{2,1,0:T(8,128)(2,1)S(1)} %get-tuple-element.71), channel_id=1, source_target_pairs={{0,1},{1,0},{2,3},{3,2},{4,5},{5,4},{6,7},{7,6},{8,9},{9,8},{10,11... | collective-permute-start | bytes 196616 | tf_op jit(solution)/shard_map/ppermute | solution.py:140

commit v4 on v3

--- a/solution.py
+++ b/solution.py
@@ -8,54 +8,67 @@
 from jax.sharding import PartitionSpec as P
 
 CHUNKS = 2
+FLOPS = 1_000_000_000
 SMEM = pl.BlockSpec(memory_space=pltpu.SMEM)
 VMEM = pl.BlockSpec(memory_space=pltpu.VMEM)
 HALF = jnp.bfloat16
 FULL = jnp.float32
 
 
-def build_kernel(own_at, peer_at, own_count, peer_count, own_tiles, peer_tiles, dense, picks):
+def build_kernel(own_table, peer_table, own_tiles, peer_tiles, dense, picks):
     _, owners, tile, _ = dense.shape
+    slots = own_tiles.shape[1]
     per_device = 2
     rows = dense.shape[3] // tile
     row_pos = lax.axis_index("row")
     col_pos = lax.axis_index("col")
     dense[...] = jnp.zeros_like(dense)
-    for r, at, count, tiles in ((0, own_at, own_count, own_tiles), (1, peer_at, peer_count, peer_tiles)):
-        for e in range(owners):
-            picks[r, e] = 0
-
-        def add(t, carry, r=r, at=at, tiles=tiles):
-            block = at[0, t, 0]
+    picks[...] = jnp.zeros_like(picks)
+    for r, table, tiles in ((0, own_table, own_tiles), (1, peer_table, peer_tiles)):
+
+        def add(t, carry, r=r, table=table, tiles=tiles):
+            block = table[2 * t]
             e = ((block // per_device) % owners) ^ col_pos
-            s = (at[0, t, 1] % rows) ^ row_pos
-            picks[r, e] = block % per_device
+            s = (table[2 * t + 1] % rows) ^ row_pos
+            picks[r * owners + e] = jnp.full(picks.shape[1:], block % per_device, jnp.int32)
             cols = pl.ds(pl.multiple_of(s * tile, tile), tile)
             dense[r, e, :, cols] = (dense[r, e, :, cols].astype(FULL) + tiles[0, t].astype(FULL)).astype(HALF)
             return carry
 
-        lax.fori_loop(0, count[0], add, 0)
-
-
-def project_kernel(own, peer, weight, out):
-    width = weight.shape[1] // 2
+        lax.fori_loop(0, table[2 * slots], add, 0)
+
+
+def project_kernel(own_hbm, peer_hbm, weight_hbm, out, own, peer, weight, sems):
+    width = weight.shape[1]
     core = lax.axis_index("col") % 2
-    columns = weight[:, pl.ds(pl.multiple_of(core * width, width), width)]
+    columns = pl.ds(pl.multiple_of(core * width, width), width)
+    copies = [
+        pltpu.make_async_copy(weight_hbm.at[:, columns], weight, sems.at[0]),
+        pltpu.make_async_copy(own_hbm, own, sems.at[1]),
+        pltpu.make_async_copy(peer_hbm, peer, sems.at[2]),
+    ]
+    for copy in copies:
+        copy.start()
+    for copy in copies:
+        copy.wait()
     for r, x in enumerate((own, peer)):
-        product = jnp.dot(x[...], columns, preferred_element_type=FULL).astype(HALF)
+        product = jnp.dot(x[...], weight[...], preferred_element_type=FULL).astype(HALF)
         out[r] = product.reshape(out.shape[1:])
 
 
-def select(wanted, values, outs):
+def farthest_last(items):
+    return [items[0], *items[:0:-1]]
+
+
+def select_kernel(*refs, rows):
+    needed, values, outs = farthest_last(refs[:rows]), refs[rows], refs[rows + 1 :]
     row_pos = lax.axis_index("row")
-    for s, out in enumerate(outs):
+    columns = outs[0].shape[-1]
+    for s in range(rows):
         for r in range(2):
-            out[r] = values[r, wanted[s][r, row_pos]]
-
-
-def select_kernel(*refs):
-    rows = (len(refs) - 1) // 2
-    select(refs[:rows], refs[rows], refs[rows + 1 :])
+            block = needed[s][r, row_pos]
+            for j in range(len(outs) // rows):
+                outs[j * rows + s][r] = values[r, block, :, j * columns : (j + 1) * columns]
 
 
 def multiply_kernel(*refs):
@@ -65,13 +78,12 @@
     pieces, outs = refs[2 : 2 + rows], refs[2 + rows :]
     chips = owners // 2
     columns = outs[0].shape[-1]
-    ordered = pieces[:1] + pieces[:0:-1]
-    operands = [jnp.concatenate([piece[r] for piece in ordered], axis=0) for r in range(2)]
+    operands = [jnp.concatenate([piece[r] for piece in farthest_last(pieces)], axis=0) for r in range(2)]
+    products = [jnp.dot(dense[r].reshape(owners * tile, depth), operands[r], preferred_element_type=FULL) for r in range(2)]
     for e in range(owners):
-        own = jnp.dot(dense[0, e], operands[0], preferred_element_type=FULL)
-        peer = jnp.dot(dense[1, e], operands[1], preferred_element_type=FULL)
+        own, peer = (product[e * tile : (e + 1) * tile] for product in products)
         for b in range(2):
-            total = jnp.where(picks[0, e] == b, own, 0.0) + jnp.where(picks[1, e] == b, peer, 0.0)
+            total = jnp.where(picks[e, :, :1] == b, own, 0.0) + jnp.where(picks[owners + e, :, :1] == b, peer, 0.0)
             for j in range(len(outs) // chips):
                 outs[j * chips + e // 2][e % 2, b] = total[:, j * columns : (j + 1) * columns].astype(HALF)
 
@@ -85,11 +97,14 @@
 
 def hidden_kernel(*refs, rows):
     values = refs[-1]
-    wanted, parts, outs = refs[:rows], refs[rows : -1 - rows], refs[-1 - rows : -1]
+    needed, parts, outs = farthest_last(refs[:rows]), refs[rows : -1 - rows], refs[-1 - rows : -1]
+    row_pos = lax.axis_index("row")
     for r in range(2):
         for b in range(2):
             values[r, b] = jnp.maximum(added(parts, r, b), 0.0).astype(HALF)
-    select(wanted, values, outs)
+    for s, out in enumerate(outs):
+        for r in range(2):
+            out[r] = values[r, needed[s][r, row_pos]]
 
 
 def mixed_kernel(*refs):
@@ -132,10 +147,13 @@
             out_specs=out_specs or ([VMEM] * len(out_shape) if many else VMEM),
             out_shape=out_shape,
             compiler_params=pltpu.CompilerParams(vmem_limit_bytes=limit),
-            cost_estimate=pl.CostEstimate(flops=1_000_000_000, bytes_accessed=10_000_000, transcendentals=0),
+            cost_estimate=pl.CostEstimate(flops=FLOPS, bytes_accessed=FLOPS // 100, transcendentals=0),
             **options,
         )(*args)
 
+    def in_hbm(x):
+        return pltpu.with_memory_space_constraint(x, pltpu.HBM)
+
     def by_col(x, masks):
         return lax.ppermute(x, "col", [(i, i ^ masks[i % 2]) for i in range(col_count)])
 
@@ -148,18 +166,32 @@
     def shape(*dims, dtype=HALF):
         return jax.ShapeDtypeStruct(dims, dtype)
 
-    both_needed = jnp.concatenate([needed, swap(needed)], axis=0)
-    wanted = [both_needed] + [by_row(both_needed, s) for s in range(1, row_count)]
-    projected = call(project_kernel, shape(2, 2, tile, width), [features, swap(features), weight_one], name="project")
+    needs = jnp.concatenate([needed, swap(needed)], axis=0)
+    features, tile_values, needs = lax.optimization_barrier((features, tile_values, needs))
+    needs = [needs] + [by_row(needs, s) for s in range(row_count - 1, 0, -1)]
+    peer_features = swap(features)
+    projected = call(
+        project_kernel,
+        shape(2, 2, tile, width),
+        [in_hbm(features), peer_features, in_hbm(weight_one)],
+        in_specs=[pl.BlockSpec(memory_space=pltpu.HBM)] * 3,
+        scratch_shapes=[
+            pltpu.VMEM(features.shape, HALF),
+            pltpu.VMEM(features.shape, HALF),
+            pltpu.VMEM((features.shape[1], width), HALF),
+            pltpu.SemaphoreType.DMA((3,)),
+        ],
+        name="project",
+    )
+    tile_blocks, tile_count, projected = lax.optimization_barrier((tile_blocks, tile_count, projected))
+    table = jnp.concatenate([tile_blocks.reshape(-1), tile_count])
     dense, picks = call(
         build_kernel,
-        [shape(2, col_count, tile, row_count * tile), shape(2, col_count, dtype=jnp.int32)],
-        [tile_blocks, swap(tile_blocks), tile_count, swap(tile_count), tile_values, swap(tile_values)],
-        in_specs=[SMEM] * 4 + [VMEM] * 2,
-        out_specs=[VMEM, SMEM],
+        [shape(2, col_count, tile, row_count * tile), shape(2 * col_count, 1, tile, dtype=jnp.int32)],
+        [table, swap(table), tile_values, swap(tile_values)],
+        in_specs=[SMEM] * 2 + [VMEM] * 2,
         name="build",
     )
-
     columns = width // CHUNKS
 
     def to_readers(pieces):
@@ -171,26 +203,26 @@
             multiply_kernel,
             [shape(2, 2, tile, columns)] * (chips * chunks),
             [picks, dense, *pieces],
-            in_specs=[SMEM] + [VMEM] * (1 + row_count),
             name="multiply",
         )
         parts = [parts[j * chips : (j + 1) * chips] for j in range(chunks)]
         return [[x[0]] + [by_col(x[c], (2 * c, 2 * c)) for c in range(1, chips)] for x in parts]
 
     selected = call(
-        select_kernel,
-        [shape(2, tile, width)] * row_count,
-        [*wanted, projected],
+        functools.partial(select_kernel, rows=row_count),
+        [shape(2, tile, columns)] * (row_count * CHUNKS),
+        [*needs, projected],
         in_specs=[SMEM] * row_count + [VMEM],
         name="select",
     )
-    arrived = to_owners(to_readers(selected))
+    panels = [to_readers(selected[j * row_count : (j + 1) * row_count]) for j in range(CHUNKS)]
+    arrived = [parts for panel in panels for parts in to_owners(panel)]
     panels = []
     for parts in arrived:
         selected = call(
             functools.partial(hidden_kernel, rows=row_count),
             [shape(2, tile, columns)] * row_count,
-            [*wanted, *parts],
+            [*needs, *parts],
             in_specs=[SMEM] * row_count + [VMEM] * len(parts),
             scratch_shapes=[pltpu.VMEM((2, 2, tile, columns), HALF)],
             name="hidden",

time: 65.2 us -> 61.5 us (0.943)
  waiting for transfers between devices: 15.6 us -> 12 us
  starting transfers between devices: 36.2 us -> 38.9 us
  local copies, waits for them, and re-layouts: 2.09 us -> 0.19 us
  Pallas kernels: 9.67 us -> 8.77 us
    ppermute x12 -> x15, starting transfers between devices: 19 us -> 23.6 us  [by_row(): return lax.ppermute(x, 'row', [(i, i ^ s) for i in range(row_count)])]
    ppermute x12 -> x15, waiting for transfers between devices: 5.18 us -> 2.79 us  [by_row(): return lax.ppermute(x, 'row', [(i, i ^ s) for i in range(row_count)])]
    unnamed x11 -> x6, local copies, waits for them, and re-layouts: 2.09 us -> 0.02 us
    ppermute x19 -> x18, starting transfers between devices: 17.3 us -> 15.3 us  [by_col(): lax.ppermute(x, 'col', [(i, i ^ masks[i % 2]) for i in range(col_count)])]
    ppermute x19 -> x18, waiting for transfers between devices: 10.4 us -> 9.23 us  [by_col(): lax.ppermute(x, 'col', [(i, i ^ masks[i % 2]) for i in range(col_count)])]
    pallas_call x11 -> x12, Pallas kernels: 9.67 us -> 8.77 us  [call(): pl.pallas_call(kernel, in_specs=in_specs or [VMEM] * len(args), out_specs...]
  transfers between devices with their start and end apart: 31 -> 33, of which waited for: 11 -> 7; matrix products, arithmetic and copies ran while one was open for 1% -> 0% of each run, Pallas kernels for 11% -> 12%
where the time goes in v4:
time: 61.5 us
  starting transfers between devices  38.9 us (63%)
  waiting for transfers between devices  12 us (20%)
  Pallas kernels  8.77 us (14%)
  between operations  0.84 us (1%)
  other arithmetic  0.74 us (1%)
    ppermute x15, starting transfers between devices, by_row(): return lax.ppermute(x, 'row', [(i, i ^ s) for i in range(row_count)])  23.6 us
    ppermute x18, starting transfers between devices, by_col(): lax.ppermute(x, 'col', [(i, i ^ masks[i % 2]) for i in range(col_count)])  15.3 us
    ppermute x18, waiting for transfers between devices, by_col(): lax.ppermute(x, 'col', [(i, i ^ masks[i % 2]) for i in range(col_count)])  9.23 us
    pallas_call x12, Pallas kernels, call(): pl.pallas_call(kernel, in_specs=in_specs or [VMEM] * len(args), out_specs...  8.77 us
    ppermute x15, waiting for transfers between devices, by_row(): return lax.ppermute(x, 'row', [(i, i ^ s) for i in range(row_count)])  2.79 us
  transfers between devices with their start and end apart: 33, of which 7 were waited for; matrix products, arithmetic and copies ran while one was open for 0% of the time, Pallas kernels for 12%

profile of v4, /device:TPU:0, one launch (start us, length us, event | category | flops | bytes accessed | tf_op | source)
XLA Modules:
  0.0 61.5 jit_solution(14757337924743721141)
XLA Ops:
  0.0 0.5 collective-permute-start
  0.5 1.0 %collective-permute-done = s32[1,4]{1,0:T(1,128)S(1)} collective-permute-done((s32[1,4]{1,0:T(1,128)}, s32[1,4]{1,0:T(1,128)S(1)}, u32[]{:S(2)}, u32[]{:S(2)}) %collective-permute-start) | collective-permute-done | bytes 48 | tf_op jit(solution)/shard_map/ppermute | solution.py:158
  1.4 0.7 %pad_add_fusion.refs_0_ = s32[2,4]{1,0:T(2,128)S(1)} fusion(s32[1,4]{1,0:T(1,128)S(1)} %collective-permute-done, s32[1,4]{1,0:T(1,128)} %param.11), kind=kLoop, calls=%fused_computation | loop fusion | flops 8 | bytes 64 | tf_op jit(solution)/shard_map/concatenate | solution.py:169
  2.1 0.3 collective-permute-start.1
  2.4 0.2 collective-permute-start.3
  3.2 5.0 %collective-permute-start.4 = (s32[2,4]{1,0:T(2,128)S(1)}, s32[2,4]{1,0:T(2,128)S(1)}, u32[]{:S(2)}, u32[]{:S(2)}) collective-permute-start(s32[2,4]{1,0:T(2,128)S(1)} %pad_add_fusion.refs_0_), channel_id=1, source_target_pairs={{0,24},{8,16},{16,8},{24,0},{1,25},{9,17},{17,9},{25,1},{2,26},{10... | collective-permute-start | bytes 104 | tf_op jit(solution)/shard_map/ppermute | solution.py:164
  8.2 0.6 %collective-permute-start.6 = (s32[2,4]{1,0:T(2,128)S(1)}, s32[2,4]{1,0:T(2,128)S(1)}, u32[]{:S(2)}, u32[]{:S(2)}) collective-permute-start(s32[2,4]{1,0:T(2,128)S(1)} %pad_add_fusion.refs_0_), channel_id=1, source_target_pairs={{0,8},{8,0},{16,24},{24,16},{1,9},{9,1},{17,25},{25,17},{2,10},{10... | collective-permute-start | bytes 104 | tf_op jit(solution)/shard_map/ppermute | solution.py:164
  8.8 1.4 %project.1.refs_4_ = bf16[2,2,128,256]{3,2,1,0:T(8,128)(2,1)S(1)} custom-call(bf16[256,512]{1,0:T(8,128)(2,1)} %own_hbm, bf16[256,512]{1,0:T(8,128)(2,1)S(1)} %collective-permute-done.1.peer_hbm, bf16[512,512]{1,0:T(8,128)(2,1)} %weight_hbm.1), custom_call_target="tpu_custom_call" | custom-call | flops 1000000000 | bytes 10000000 | tf_op jit(solution)/shard_map/project/pallas_call | solution.py:144
  10.2 0.1 copy.9
  10.3 0.1 reshape.3
  10.4 0.1 pad_add_fusion.1.own_table
  10.5 2.2 %collective-permute-done.5.refs_2_ = s32[2,4]{1,0:T(2,128)S(1)} collective-permute-done((s32[2,4]{1,0:T(2,128)S(1)}, s32[2,4]{1,0:T(2,128)S(1)}, u32[]{:S(2)}, u32[]{:S(2)}) %collective-permute-start.5) | collective-permute-done | bytes 64 | tf_op jit(solution)/shard_map/ppermute | solution.py:164
  12.7 0.7 %select.1 = (bf16[2,128,128]{2,1,0:T(8,128)(2,1)S(1)}, bf16[2,128,128]{2,1,0:T(8,128)(2,1)S(1)}, bf16[2,128,128]{2,1,0:T(8,128)(2,1)S(1)}, bf16[2,128,128]{2,1,0...) custom-call(s32[2,4]{1,0:T(2,128)S(1)} %pad_add_fusion.refs_0_, ...), custom_call_target="tpu_custom_call" | custom-call | flops 1000000000 | bytes 10000000 | tf_op jit(solution)/shard_map/select/pallas_call | solution.py:144
  13.4 1.7 %collective-permute-start.7 = (bf16[2,128,128]{2,1,0:T(8,128)(2,1)S(1)}, bf16[2,128,128]{2,1,0:T(8,128)(2,1)S(1)}, u32[]{:S(2)}, u32[]{:S(2)}) collective-permute-start(bf16[2,128,128]{2,1,0:T(8,128)(2,1)S(1)} %get-tuple-element.58), channel_id=1, source_target_pairs={{0,24},{8,16},{16,8},{24,0},{1,25},{9,17},{17,9},{25,1},{2,26},{10... | collective-permute-start | bytes 196616 | tf_op jit(solution)/shard_map/ppermute | solution.py:164
  15.1 0.5 collective-permute-start.8
  15.5 2.3 %collective-permute-start.9 = (bf16[2,128,128]{2,1,0:T(8,128)(2,1)S(1)}, bf16[2,128,128]{2,1,0:T(8,128)(2,1)S(1)}, u32[]{:S(2)}, u32[]{:S(2)}) collective-permute-start(bf16[2,128,128]{2,1,0:T(8,128)(2,1)S(1)} %get-tuple-element.60), channel_id=1, source_target_pairs={{0,8},{8,0},{16,24},{24,16},{1,9},{9,1},{17,25},{25,17},{2,10},{10... | collective-permute-start | bytes 196616 | tf_op jit(solution)/shard_map/ppermute | solution.py:164
  17.8 1.6 %collective-permute-start.19 = (bf16[2,128,128]{2,1,0:T(8,128)(2,1)S(1)}, bf16[2,128,128]{2,1,0:T(8,128)(2,1)S(1)}, u32[]{:S(2)}, u32[]{:S(2)}) collective-permute-start(bf16[2,128,128]{2,1,0:T(8,128)(2,1)S(1)} %get-tuple-element.75), channel_id=1, source_target_pairs={{0,24},{8,16},{16,8},{24,0},{1,25},{9,17},{17,9},{25,1},{2,26},{10... | collective-permute-start | bytes 196616 | tf_op jit(solution)/shard_map/ppermute | solution.py:164
  19.5 1.2 %build.1 = (bf16[2,8,128,512]{3,2,1,0:T(8,128)(2,1)S(1)}, s32[16,1,128]{2,1,0:T(1,128)S(1)}) custom-call(s32[33]{0:T(128)S(1)} %pad_add_fusion.1.own_table, s32[33]{0:T(128)S(1)} %collective-permute-done.2.peer_table, bf16[1,16,128,128]{3,2,1,0:T(8,128)(2,1)S(1)} %copy-done, bf16[1,16,128,128]{3,2,1,0:T(8,128)(2,1)S(1)} %collective-permute-done.3.peer_tiles), custom_call_target="tpu_custom_call" | custom-call | flops 1000000000 | bytes 10000000 | tf_op jit(solution)/shard_map/build/pallas_call | solution.py:144
  20.7 2.6 %collective-permute-start.21 = (bf16[2,128,128]{2,1,0:T(8,128)(2,1)S(1)}, bf16[2,128,128]{2,1,0:T(8,128)(2,1)S(1)}, u32[]{:S(2)}, u32[]{:S(2)}) collective-permute-start(bf16[2,128,128]{2,1,0:T(8,128)(2,1)S(1)} %get-tuple-element.77), channel_id=1, source_target_pairs={{0,8},{8,0},{16,24},{24,16},{1,9},{9,1},{17,25},{25,17},{2,10},{10... | collective-permute-start | bytes 196616 | tf_op jit(solution)/shard_map/ppermute | solution.py:164
  23.3 0.7 %multiply.4 = (bf16[2,2,128,128]{3,2,1,0:T(8,128)(2,1)S(1)}, bf16[2,2,128,128]{3,2,1,0:T(8,128)(2,1)S(1)}, bf16[2,2,128,128]{3,2,1,0:T(8,128)(2,1)S(1)}, bf16[2,2,128,128]{3,2,1,0:T(8,128)(2,1)S(1)}) custom-call(s32[16,1,128]{2,1,0:T(1,128)S(1)} %get-tuple-element.53.refs_0_, bf16[2,8,128,512]{3,2,1,0:T(8,128)(2,1)S(1)} %get-tuple-element.54.refs_1_, ...), custom_call_target="tpu_custom_call" | custom-call | flops 1000000000 | bytes 10000000 | tf_op jit(solution)/shard_map/multiply/pallas_call | solution.py:144
  24.0 1.5 %collective-permute-start.10 = (bf16[2,2,128,128]{3,2,1,0:T(8,128)(2,1)S(1)}, bf16[2,2,128,128]{3,2,1,0:T(8,128)(2,1)S(1)}, u32[]{:S(2)}, u32[]{:S(2)}) collective-permute-start(bf16[2,2,128,128]{3,2,1,0:T(8,128)(2,1)S(1)} %get-tuple-element.62), channel_id=1, source_target_pairs={{0,2},{1,3},{2,0},{3,1},{4,6},{5,7},{6,4},{7,5},{8,10},{9,11},{10,... | collective-permute-start | bytes 393224 | tf_op jit(solution)/shard_map/ppermute | solution.py:158
  25.5 1.6 %collective-permute-start.11 = (bf16[2,2,128,128]{3,2,1,0:T(8,128)(2,1)S(1)}, bf16[2,2,128,128]{3,2,1,0:T(8,128)(2,1)S(1)}, u32[]{:S(2)}, u32[]{:S(2)}) collective-permute-start(bf16[2,2,128,128]{3,2,1,0:T(8,128)(2,1)S(1)} %get-tuple-element.63), channel_id=1, source_target_pairs={{0,4},{1,5},{2,6},{3,7},{4,0},{5,1},{6,2},{7,3},{8,12},{9,13},{10,... | collective-permute-start | bytes 393224 | tf_op jit(solution)/shard_map/ppermute | solution.py:158
  27.1 0.5 collective-permute-start.12
  27.6 0.7 %multiply.6 = (bf16[2,2,128,128]{3,2,1,0:T(8,128)(2,1)S(1)}, bf16[2,2,128,128]{3,2,1,0:T(8,128)(2,1)S(1)}, bf16[2,2,128,128]{3,2,1,0:T(8,128)(2,1)S(1)}, bf16[2,2,128,128]{3,2,1,0:T(8,128)(2,1)S(1)}) custom-call(s32[16,1,128]{2,1,0:T(1,128)S(1)} %get-tuple-element.53.refs_0_, bf16[2,8,128,512]{3,2,1,0:T(8,128)(2,1)S(1)} %get-tuple-element.54.refs_1_, ...), custom_call_target="tpu_custom_call" | custom-call | flops 1000000000 | bytes 10000000 | tf_op jit(solution)/shard_map/multiply/pallas_call | solution.py:144
  28.3 1.5 %collective-permute-start.22 = (bf16[2,2,128,128]{3,2,1,0:T(8,128)(2,1)S(1)}, bf16[2,2,128,128]{3,2,1,0:T(8,128)(2,1)S(1)}, u32[]{:S(2)}, u32[]{:S(2)}) collective-permute-start(bf16[2,2,128,128]{3,2,1,0:T(8,128)(2,1)S(1)} %get-tuple-element.79), channel_id=1, source_target_pairs={{0,2},{1,3},{2,0},{3,1},{4,6},{5,7},{6,4},{7,5},{8,10},{9,11},{10,... | collective-permute-start | bytes 393224 | tf_op jit(solution)/shard_map/ppermute | solution.py:158
  29.7 1.6 %collective-permute-start.23 = (bf16[2,2,128,128]{3,2,1,0:T(8,128)(2,1)S(1)}, bf16[2,2,128,128]{3,2,1,0:T(8,128)(2,1)S(1)}, u32[]{:S(2)}, u32[]{:S(2)}) collective-permute-start(bf16[2,2,128,128]{3,2,1,0:T(8,128)(2,1)S(1)} %get-tuple-element.80), channel_id=1, source_target_pairs={{0,4},{1,5},{2,6},{3,7},{4,0},{5,1},{6,2},{7,3},{8,12},{9,13},{10,... | collective-permute-start | bytes 393224 | tf_op jit(solution)/shard_map/ppermute | solution.py:158
  31.4 0.5 collective-permute-start.24
  31.9 2.6 %collective-permute-done.12.refs_7_ = bf16[2,2,128,128]{3,2,1,0:T(8,128)(2,1)S(1)} collective-permute-done((bf16[2,2,128,128]{3,2,1,0:T(8,128)(2,1)S(1)}, bf16[2,2,128,128]{3,2,1,0:T(8,128)(2,1)S(1)}, u32[]{:S(2)}, u32[]{:S(2)}) %collective-permute-start.12) | collective-permute-done | bytes 131104 | tf_op jit(solution)/shard_map/ppermute | solution.py:158
  34.5 0.7 %hidden.2 = (bf16[2,128,128]{2,1,0:T(8,128)(2,1)S(1)}, bf16[2,128,128]{2,1,0:T(8,128)(2,1)S(1)}, bf16[2,128,128]{2,1,0:T(8,128)(2,1)S(1)}, bf16[2,128,128]{2,1,0:T(8,128)(2,1)S(1)}) custom-call(s32[2,4]{1,0:T(2,128)S(1)} %pad_add_fusion.refs_0_, s32[2,4]{1,0:T(2,128)S(1)} %collective-permute-done.4.refs_1_, s32[2,4]{1,0:T(2,128)S(1)} %collective-permute-done.5.refs_2_, ...), custom_call_target="tpu_custom_call" | custom-call | flops 1000000000 | bytes 10000000 | tf_op jit(solution)/shard_map/hidden/pallas_call | solution.py:144
  35.2 4.2 %collective-permute-start.13 = (bf16[2,128,128]{2,1,0:T(8,128)(2,1)S(1)}, bf16[2,128,128]{2,1,0:T(8,128)(2,1)S(1)}, u32[]{:S(2)}, u32[]{:S(2)}) collective-permute-start(bf16[2,128,128]{2,1,0:T(8,128)(2,1)S(1)} %get-tuple-element.66), channel_id=1, source_target_pairs={{0,24},{8,16},{16,8},{24,0},{1,25},{9,17},{17,9},{25,1},{2,26},{10... | collective-permute-start | bytes 196616 | tf_op jit(solution)/shard_map/ppermute | solution.py:164
  39.4 0.6 %collective-permute-start.15 = (bf16[2,128,128]{2,1,0:T(8,128)(2,1)S(1)}, bf16[2,128,128]{2,1,0:T(8,128)(2,1)S(1)}, u32[]{:S(2)}, u32[]{:S(2)}) collective-permute-start(bf16[2,128,128]{2,1,0:T(8,128)(2,1)S(1)} %get-tuple-element.68), channel_id=1, source_target_pairs={{0,8},{8,0},{16,24},{24,16},{1,9},{9,1},{17,25},{25,17},{2,10},{10... | collective-permute-start | bytes 196616 | tf_op jit(solution)/shard_map/ppermute | solution.py:164
  40.0 0.7 %hidden.3 = (bf16[2,128,128]{2,1,0:T(8,128)(2,1)S(1)}, bf16[2,128,128]{2,1,0:T(8,128)(2,1)S(1)}, bf16[2,128,128]{2,1,0:T(8,128)(2,1)S(1)}, bf16[2,128,128]{2,1,0:T(8,128)(2,1)S(1)}) custom-call(s32[2,4]{1,0:T(2,128)S(1)} %pad_add_fusion.refs_0_, s32[2,4]{1,0:T(2,128)S(1)} %collective-permute-done.4.refs_1_, s32[2,4]{1,0:T(2,128)S(1)} %collective-permute-done.5.refs_2_, ...), custom_call_target="tpu_custom_call" | custom-call | flops 1000000000 | bytes 10000000 | tf_op jit(solution)/shard_map/hidden/pallas_call | solution.py:144
  40.7 3.8 %collective-permute-start.25 = (bf16[2,128,128]{2,1,0:T(8,128)(2,1)S(1)}, bf16[2,128,128]{2,1,0:T(8,128)(2,1)S(1)}, u32[]{:S(2)}, u32[]{:S(2)}) collective-permute-start(bf16[2,128,128]{2,1,0:T(8,128)(2,1)S(1)} %get-tuple-element.83), channel_id=1, source_target_pairs={{0,24},{8,16},{16,8},{24,0},{1,25},{9,17},{17,9},{25,1},{2,26},{10... | collective-permute-start | bytes 196616 | tf_op jit(solution)/shard_map/ppermute | solution.py:164
  44.5 0.6 %collective-permute-start.27 = (bf16[2,128,128]{2,1,0:T(8,128)(2,1)S(1)}, bf16[2,128,128]{2,1,0:T(8,128)(2,1)S(1)}, u32[]{:S(2)}, u32[]{:S(2)}) collective-permute-start(bf16[2,128,128]{2,1,0:T(8,128)(2,1)S(1)} %get-tuple-element.85), channel_id=1, source_target_pairs={{0,8},{8,0},{16,24},{24,16},{1,9},{9,1},{17,25},{25,17},{2,10},{10... | collective-permute-start | bytes 196616 | tf_op jit(solution)/shard_map/ppermute | solution.py:164
  45.2 0.6 collective-permute-done.14.refs_4_
  45.8 0.7 %multiply.5 = (bf16[2,2,128,128]{3,2,1,0:T(8,128)(2,1)S(1)}, bf16[2,2,128,128]{3,2,1,0:T(8,128)(2,1)S(1)}, bf16[2,2,128,128]{3,2,1,0:T(8,128)(2,1)S(1)}, bf16[2,2,128,128]{3,2,1,0:T(8,128)(2,1)S(1)}) custom-call(s32[16,1,128]{2,1,0:T(1,128)S(1)} %get-tuple-element.53.refs_0_, bf16[2,8,128,512]{3,2,1,0:T(8,128)(2,1)S(1)} %get-tuple-element.54.refs_1_, ...), custom_call_target="tpu_custom_call" | custom-call | flops 1000000000 | bytes 10000000 | tf_op jit(solution)/shard_map/multiply/pallas_call | solution.py:144
  46.5 1.6 %collective-permute-start.16 = (bf16[2,2,128,128]{3,2,1,0:T(8,128)(2,1)S(1)}, bf16[2,2,128,128]{3,2,1,0:T(8,128)(2,1)S(1)}, u32[]{:S(2)}, u32[]{:S(2)}) collective-permute-start(bf16[2,2,128,128]{3,2,1,0:T(8,128)(2,1)S(1)} %get-tuple-element.70), channel_id=1, source_target_pairs={{0,2},{1,3},{2,0},{3,1},{4,6},{5,7},{6,4},{7,5},{8,10},{9,11},{10,... | collective-permute-start | bytes 393224 | tf_op jit(solution)/shard_map/ppermute | solution.py:158
  48.1 0.3 collective-permute-start.17
  48.4 1.6 %collective-permute-start.18 = (bf16[2,2,128,128]{3,2,1,0:T(8,128)(2,1)S(1)}, bf16[2,2,128,128]{3,2,1,0:T(8,128)(2,1)S(1)}, u32[]{:S(2)}, u32[]{:S(2)}) collective-permute-start(bf16[2,2,128,128]{3,2,1,0:T(8,128)(2,1)S(1)} %get-tuple-element.72), channel_id=1, source_target_pairs={{0,6},{1,7},{2,4},{3,5},{4,2},{5,3},{6,0},{7,1},{8,14},{9,15},{10,... | collective-permute-start | bytes 393224 | tf_op jit(solution)/shard_map/ppermute | solution.py:158
  50.1 0.7 %multiply.7 = (bf16[2,2,128,128]{3,2,1,0:T(8,128)(2,1)S(1)}, bf16[2,2,128,128]{3,2,1,0:T(8,128)(2,1)S(1)}, bf16[2,2,128,128]{3,2,1,0:T(8,128)(2,1)S(1)}, bf16[2,2,128,128]{3,2,1,0:T(8,128)(2,1)S(1)}) custom-call(s32[16,1,128]{2,1,0:T(1,128)S(1)} %get-tuple-element.53.refs_0_, bf16[2,8,128,512]{3,2,1,0:T(8,128)(2,1)S(1)} %get-tuple-element.54.refs_1_, ...), custom_call_target="tpu_custom_call" | custom-call | flops 1000000000 | bytes 10000000 | tf_op jit(solution)/shard_map/multiply/pallas_call | solution.py:144
  50.8 1.6 %collective-permute-start.28 = (bf16[2,2,128,128]{3,2,1,0:T(8,128)(2,1)S(1)}, bf16[2,2,128,128]{3,2,1,0:T(8,128)(2,1)S(1)}, u32[]{:S(2)}, u32[]{:S(2)}) collective-permute-start(bf16[2,2,128,128]{3,2,1,0:T(8,128)(2,1)S(1)} %get-tuple-element.87), channel_id=1, source_target_pairs={{0,2},{1,3},{2,0},{3,1},{4,6},{5,7},{6,4},{7,5},{8,10},{9,11},{10,... | collective-permute-start | bytes 393224 | tf_op jit(solution)/shard_map/ppermute | solution.py:158
  52.4 0.3 collective-permute-start.29
  52.7 1.6 %collective-permute-start.30 = (bf16[2,2,128,128]{3,2,1,0:T(8,128)(2,1)S(1)}, bf16[2,2,128,128]{3,2,1,0:T(8,128)(2,1)S(1)}, u32[]{:S(2)}, u32[]{:S(2)}) collective-permute-start(bf16[2,2,128,128]{3,2,1,0:T(8,128)(2,1)S(1)} %get-tuple-element.89), channel_id=1, source_target_pairs={{0,6},{1,7},{2,4},{3,5},{4,2},{5,3},{6,0},{7,1},{8,14},{9,15},{10,... | collective-permute-start | bytes 393224 | tf_op jit(solution)/shard_map/ppermute | solution.py:158
  54.3 1.8 %collective-permute-done.17.refs_2_ = bf16[2,2,128,128]{3,2,1,0:T(8,128)(2,1)S(1)} collective-permute-done((bf16[2,2,128,128]{3,2,1,0:T(8,128)(2,1)S(1)}, bf16[2,2,128,128]{3,2,1,0:T(8,128)(2,1)S(1)}, u32[]{:S(2)}, u32[]{:S(2)}) %collective-permute-start.17) | collective-permute-done | bytes 131104 | tf_op jit(solution)/shard_map/ppermute | solution.py:158
  56.2 0.1 collective-permute-start.31
  56.3 2.6 %collective-permute-done.29.refs_2_ = bf16[2,2,128,128]{3,2,1,0:T(8,128)(2,1)S(1)} collective-permute-done((bf16[2,2,128,128]{3,2,1,0:T(8,128)(2,1)S(1)}, bf16[2,2,128,128]{3,2,1,0:T(8,128)(2,1)S(1)}, u32[]{:S(2)}, u32[]{:S(2)}) %collective-permute-start.29) | collective-permute-done | bytes 131104 | tf_op jit(solution)/shard_map/ppermute | solution.py:158
  59.1 1.2 %collective-permute-done.32.refs_3_ = bf16[2,128,128]{2,1,0:T(8,128)(2,1)S(1)} collective-permute-done((bf16[2,128,128]{2,1,0:T(8,128)(2,1)S(1)}, bf16[2,128,128]{2,1,0:T(8,128)(2,1)S(1)}, u32[]{:S(2)}, u32[]{:S(2)}) %collective-permute-start.32) | collective-permute-done | bytes 65568 | tf_op jit(solution)/shard_map/ppermute | solution.py:158
  60.3 1.1 %final.1 = bf16[256,512]{1,0:T(8,128)(2,1)} custom-call(bf16[2,128,128]{2,1,0:T(8,128)(2,1)S(1)} %get-tuple-element.73.refs_0_, bf16[2,128,128]{2,1,0:T(8,128)(2,1)S(1)} %get-tuple-element.90.refs_1_, bf16[2,128,128]{2,1,0:T(8,128)(2,1)S(1)} %collective-permute-done.31.refs_2_, bf16[2,128,128]{2,1,0:T(8,128)(2,1)S(1)} %collective-permute-done.32.refs_3_, ...), custom_call_target="tpu_custom_call" | custom-call | flops 1000000000 | bytes 10000000 | tf_op jit(solution)/shard_map/final/pallas_call | solution.py:144
  (40 shorter events, 0.3 us)
Async XLA Ops:
  0.0 10.2 %copy-start.2 = (s32[1,16,2]{1,2,0:T(2,128)S(1)}, s32[1,16,2]{1,2,0:T(2,128)}, u32[]{:S(2)}) copy-start(s32[1,16,2]{1,2,0:T(2,128)} %param.9) | copy-start | bytes 388
  0.0 1.4 %collective-permute-start = (s32[1,4]{1,0:T(1,128)}, s32[1,4]{1,0:T(1,128)S(1)}, u32[]{:S(2)}, u32[]{:S(2)}) collective-permute-start(s32[1,4]{1,0:T(1,128)} %param.11), channel_id=1, source_target_pairs={{0,1},{1,0},{2,3},{3,2},{4,5},{5,4},{6,7},{7,6},{8,9},{9,8},{10,11... | collective-permute-start | bytes 56 | tf_op jit(solution)/shard_map/ppermute | solution.py:158
  2.1 6.8 %collective-permute-start.1 = (bf16[256,512]{1,0:T(8,128)(2,1)}, bf16[256,512]{1,0:T(8,128)(2,1)S(1)}, u32[]{:S(2)}, u32[]{:S(2)}) collective-permute-start(bf16[256,512]{1,0:T(8,128)(2,1)} %own_hbm), channel_id=1, source_target_pairs={{0,1},{1,0},{2,3},{3,2},{4,5},{5,4},{6,7},{7,6},{8,9},{9,8},{10,11... | collective-permute-start | bytes 786440 | tf_op jit(solution)/shard_map/ppermute | solution.py:158
  2.4 17.1 %collective-permute-start.3 = (bf16[1,16,128,128]{3,2,1,0:T(8,128)(2,1)}, bf16[1,16,128,128]{3,2,1,0:T(8,128)(2,1)S(1)}, u32[]{:S(2)}, u32[]{:S(2)}) collective-permute-start(bf16[1,16,128,128]{3,2,1,0:T(8,128)(2,1)} %own_tiles), channel_id=1, source_target_pairs={{0,1},{1,0},{2,3},{3,2},{4,5},{5,4},{6,7},{7,6},{8,9},{9,8},{10,11... | collective-permute-start | bytes 1572872 | tf_op jit(solution)/shard_map/ppermute | solution.py:158
  3.2 7.3 %collective-permute-start.4 = (s32[2,4]{1,0:T(2,128)S(1)}, s32[2,4]{1,0:T(2,128)S(1)}, u32[]{:S(2)}, u32[]{:S(2)}) collective-permute-start(s32[2,4]{1,0:T(2,128)S(1)} %pad_add_fusion.refs_0_), channel_id=1, source_target_pairs={{0,24},{8,16},{16,8},{24,0},{1,25},{9,17},{17,9},{25,1},{2,26},{10... | collective-permute-start | bytes 104 | tf_op jit(solution)/shard_map/ppermute | solution.py:164
  8.2 4.5 %collective-permute-start.5 = (s32[2,4]{1,0:T(2,128)S(1)}, s32[2,4]{1,0:T(2,128)S(1)}, u32[]{:S(2)}, u32[]{:S(2)}) collective-permute-start(s32[2,4]{1,0:T(2,128)S(1)} %pad_add_fusion.refs_0_), channel_id=1, source_target_pairs={{0,16},{8,24},{16,0},{24,8},{1,17},{9,25},{17,1},{25,9},{2,18},{10... | collective-permute-start | bytes 104 | tf_op jit(solution)/shard_map/ppermute | solution.py:164
  8.2 4.5 %collective-permute-start.6 = (s32[2,4]{1,0:T(2,128)S(1)}, s32[2,4]{1,0:T(2,128)S(1)}, u32[]{:S(2)}, u32[]{:S(2)}) collective-permute-start(s32[2,4]{1,0:T(2,128)S(1)} %pad_add_fusion.refs_0_), channel_id=1, source_target_pairs={{0,8},{8,0},{16,24},{24,16},{1,9},{9,1},{17,25},{25,17},{2,10},{10... | collective-permute-start | bytes 104 | tf_op jit(solution)/shard_map/ppermute | solution.py:164
  10.2 9.2 %copy-start = (bf16[1,16,128,128]{3,2,1,0:T(8,128)(2,1)S(1)}, bf16[1,16,128,128]{3,2,1,0:T(8,128)(2,1)}, u32[]{:S(2)}) copy-start(bf16[1,16,128,128]{3,2,1,0:T(8,128)(2,1)} %own_tiles) | copy-start | bytes 1572868
  10.5 7.3 %collective-permute-start.2 = (s32[33]{0:T(128)S(1)}, s32[33]{0:T(128)S(1)}, u32[]{:S(2)}, u32[]{:S(2)}) collective-permute-start(s32[33]{0:T(128)S(1)} %pad_add_fusion.1.own_table), channel_id=1, source_target_pairs={{0,1},{1,0},{2,3},{3,2},{4,5},{5,4},{6,7},{7,6},{8,9},{9,8},{10,11... | collective-permute-start | bytes 404 | tf_op jit(solution)/shard_map/ppermute | solution.py:158
  13.4 7.3 %collective-permute-start.7 = (bf16[2,128,128]{2,1,0:T(8,128)(2,1)S(1)}, bf16[2,128,128]{2,1,0:T(8,128)(2,1)S(1)}, u32[]{:S(2)}, u32[]{:S(2)}) collective-permute-start(bf16[2,128,128]{2,1,0:T(8,128)(2,1)S(1)} %get-tuple-element.58), channel_id=1, source_target_pairs={{0,24},{8,16},{16,8},{24,0},{1,25},{9,17},{17,9},{25,1},{2,26},{10... | collective-permute-start | bytes 196616 | tf_op jit(solution)/shard_map/ppermute | solution.py:164
  15.1 8.2 %collective-permute-start.8 = (bf16[2,128,128]{2,1,0:T(8,128)(2,1)S(1)}, bf16[2,128,128]{2,1,0:T(8,128)(2,1)S(1)}, u32[]{:S(2)}, u32[]{:S(2)}) collective-permute-start(bf16[2,128,128]{2,1,0:T(8,128)(2,1)S(1)} %get-tuple-element.59), channel_id=1, source_target_pairs={{0,16},{8,24},{16,0},{24,8},{1,17},{9,25},{17,1},{25,9},{2,18},{10... | collective-permute-start | bytes 196616 | tf_op jit(solution)/shard_map/ppermute | solution.py:164
  15.5 7.8 %collective-permute-start.9 = (bf16[2,128,128]{2,1,0:T(8,128)(2,1)S(1)}, bf16[2,128,128]{2,1,0:T(8,128)(2,1)S(1)}, u32[]{:S(2)}, u32[]{:S(2)}) collective-permute-start(bf16[2,128,128]{2,1,0:T(8,128)(2,1)S(1)} %get-tuple-element.60), channel_id=1, source_target_pairs={{0,8},{8,0},{16,24},{24,16},{1,9},{9,1},{17,25},{25,17},{2,10},{10... | collective-permute-start | bytes 196616 | tf_op jit(solution)/shard_map/ppermute | solution.py:164
  17.8 9.3 %collective-permute-start.19 = (bf16[2,128,128]{2,1,0:T(8,128)(2,1)S(1)}, bf16[2,128,128]{2,1,0:T(8,128)(2,1)S(1)}, u32[]{:S(2)}, u32[]{:S(2)}) collective-permute-start(bf16[2,128,128]{2,1,0:T(8,128)(2,1)S(1)} %get-tuple-element.75), channel_id=1, source_target_pairs={{0,24},{8,16},{16,8},{24,0},{1,25},{9,17},{17,9},{25,1},{2,26},{10... | collective-permute-start | bytes 196616 | tf_op jit(solution)/shard_map/ppermute | solution.py:164
  19.5 8.1 %collective-permute-start.20 = (bf16[2,128,128]{2,1,0:T(8,128)(2,1)S(1)}, bf16[2,128,128]{2,1,0:T(8,128)(2,1)S(1)}, u32[]{:S(2)}, u32[]{:S(2)}) collective-permute-start(bf16[2,128,128]{2,1,0:T(8,128)(2,1)S(1)} %get-tuple-element.76), channel_id=1, source_target_pairs={{0,16},{8,24},{16,0},{24,8},{1,17},{9,25},{17,1},{25,9},{2,18},{10... | collective-permute-start | bytes 196616 | tf_op jit(solution)/shard_map/ppermute | solution.py:164
  20.7 6.9 %collective-permute-start.21 = (bf16[2,128,128]{2,1,0:T(8,128)(2,1)S(1)}, bf16[2,128,128]{2,1,0:T(8,128)(2,1)S(1)}, u32[]{:S(2)}, u32[]{:S(2)}) collective-permute-start(bf16[2,128,128]{2,1,0:T(8,128)(2,1)S(1)} %get-tuple-element.77), channel_id=1, source_target_pairs={{0,8},{8,0},{16,24},{24,16},{1,9},{9,1},{17,25},{25,17},{2,10},{10... | collective-permute-start | bytes 196616 | tf_op jit(solution)/shard_map/ppermute | solution.py:164
  24.0 7.4 %collective-permute-start.10 = (bf16[2,2,128,128]{3,2,1,0:T(8,128)(2,1)S(1)}, bf16[2,2,128,128]{3,2,1,0:T(8,128)(2,1)S(1)}, u32[]{:S(2)}, u32[]{:S(2)}) collective-permute-start(bf16[2,2,128,128]{3,2,1,0:T(8,128)(2,1)S(1)} %get-tuple-element.62), channel_id=1, source_target_pairs={{0,2},{1,3},{2,0},{3,1},{4,6},{5,7},{6,4},{7,5},{8,10},{9,11},{10,... | collective-permute-start | bytes 393224 | tf_op jit(solution)/shard_map/ppermute | solution.py:158
  25.5 6.4 %collective-permute-start.11 = (bf16[2,2,128,128]{3,2,1,0:T(8,128)(2,1)S(1)}, bf16[2,2,128,128]{3,2,1,0:T(8,128)(2,1)S(1)}, u32[]{:S(2)}, u32[]{:S(2)}) collective-permute-start(bf16[2,2,128,128]{3,2,1,0:T(8,128)(2,1)S(1)} %get-tuple-element.63), channel_id=1, source_target_pairs={{0,4},{1,5},{2,6},{3,7},{4,0},{5,1},{6,2},{7,3},{8,12},{9,13},{10,... | collective-permute-start | bytes 393224 | tf_op jit(solution)/shard_map/ppermute | solution.py:158
  27.1 7.4 %collective-permute-start.12 = (bf16[2,2,128,128]{3,2,1,0:T(8,128)(2,1)S(1)}, bf16[2,2,128,128]{3,2,1,0:T(8,128)(2,1)S(1)}, u32[]{:S(2)}, u32[]{:S(2)}) collective-permute-start(bf16[2,2,128,128]{3,2,1,0:T(8,128)(2,1)S(1)} %get-tuple-element.64), channel_id=1, source_target_pairs={{0,6},{1,7},{2,4},{3,5},{4,2},{5,3},{6,0},{7,1},{8,14},{9,15},{10,... | collective-permute-start | bytes 393224 | tf_op jit(solution)/shard_map/ppermute | solution.py:158
  28.3 11.1 %collective-permute-start.22 = (bf16[2,2,128,128]{3,2,1,0:T(8,128)(2,1)S(1)}, bf16[2,2,128,128]{3,2,1,0:T(8,128)(2,1)S(1)}, u32[]{:S(2)}, u32[]{:S(2)}) collective-permute-start(bf16[2,2,128,128]{3,2,1,0:T(8,128)(2,1)S(1)} %get-tuple-element.79), channel_id=1, source_target_pairs={{0,2},{1,3},{2,0},{3,1},{4,6},{5,7},{6,4},{7,5},{8,10},{9,11},{10,... | collective-permute-start | bytes 393224 | tf_op jit(solution)/shard_map/ppermute | solution.py:158
  29.7 10.3 %collective-permute-start.23 = (bf16[2,2,128,128]{3,2,1,0:T(8,128)(2,1)S(1)}, bf16[2,2,128,128]{3,2,1,0:T(8,128)(2,1)S(1)}, u32[]{:S(2)}, u32[]{:S(2)}) collective-permute-start(bf16[2,2,128,128]{3,2,1,0:T(8,128)(2,1)S(1)} %get-tuple-element.80), channel_id=1, source_target_pairs={{0,4},{1,5},{2,6},{3,7},{4,0},{5,1},{6,2},{7,3},{8,12},{9,13},{10,... | collective-permute-start | bytes 393224 | tf_op jit(solution)/shard_map/ppermute | solution.py:158
  31.4 8.7 %collective-permute-start.24 = (bf16[2,2,128,128]{3,2,1,0:T(8,128)(2,1)S(1)}, bf16[2,2,128,128]{3,2,1,0:T(8,128)(2,1)S(1)}, u32[]{:S(2)}, u32[]{:S(2)}) collective-permute-start(bf16[2,2,128,128]{3,2,1,0:T(8,128)(2,1)S(1)} %get-tuple-element.81), channel_id=1, source_target_pairs={{0,6},{1,7},{2,4},{3,5},{4,2},{5,3},{6,0},{7,1},{8,14},{9,15},{10,... | collective-permute-start | bytes 393224 | tf_op jit(solution)/shard_map/ppermute | solution.py:158
  35.2 9.4 %collective-permute-start.13 = (bf16[2,128,128]{2,1,0:T(8,128)(2,1)S(1)}, bf16[2,128,128]{2,1,0:T(8,128)(2,1)S(1)}, u32[]{:S(2)}, u32[]{:S(2)}) collective-permute-start(bf16[2,128,128]{2,1,0:T(8,128)(2,1)S(1)} %get-tuple-element.66), channel_id=1, source_target_pairs={{0,24},{8,16},{16,8},{24,0},{1,25},{9,17},{17,9},{25,1},{2,26},{10... | collective-permute-start | bytes 196616 | tf_op jit(solution)/shard_map/ppermute | solution.py:164
  39.4 6.4 %collective-permute-start.14 = (bf16[2,128,128]{2,1,0:T(8,128)(2,1)S(1)}, bf16[2,128,128]{2,1,0:T(8,128)(2,1)S(1)}, u32[]{:S(2)}, u32[]{:S(2)}) collective-permute-start(bf16[2,128,128]{2,1,0:T(8,128)(2,1)S(1)} %get-tuple-element.67), channel_id=1, source_target_pairs={{0,16},{8,24},{16,0},{24,8},{1,17},{9,25},{17,1},{25,9},{2,18},{10... | collective-permute-start | bytes 196616 | tf_op jit(solution)/shard_map/ppermute | solution.py:164
  39.4 6.4 %collective-permute-start.15 = (bf16[2,128,128]{2,1,0:T(8,128)(2,1)S(1)}, bf16[2,128,128]{2,1,0:T(8,128)(2,1)S(1)}, u32[]{:S(2)}, u32[]{:S(2)}) collective-permute-start(bf16[2,128,128]{2,1,0:T(8,128)(2,1)S(1)} %get-tuple-element.68), channel_id=1, source_target_pairs={{0,8},{8,0},{16,24},{24,16},{1,9},{9,1},{17,25},{25,17},{2,10},{10... | collective-permute-start | bytes 196616 | tf_op jit(solution)/shard_map/ppermute | solution.py:164
  40.7 7.7 %collective-permute-start.25 = (bf16[2,128,128]{2,1,0:T(8,128)(2,1)S(1)}, bf16[2,128,128]{2,1,0:T(8,128)(2,1)S(1)}, u32[]{:S(2)}, u32[]{:S(2)}) collective-permute-start(bf16[2,128,128]{2,1,0:T(8,128)(2,1)S(1)} %get-tuple-element.83), channel_id=1, source_target_pairs={{0,24},{8,16},{16,8},{24,0},{1,25},{9,17},{17,9},{25,1},{2,26},{10... | collective-permute-start | bytes 196616 | tf_op jit(solution)/shard_map/ppermute | solution.py:164
  44.5 5.5 %collective-permute-start.26 = (bf16[2,128,128]{2,1,0:T(8,128)(2,1)S(1)}, bf16[2,128,128]{2,1,0:T(8,128)(2,1)S(1)}, u32[]{:S(2)}, u32[]{:S(2)}) collective-permute-start(bf16[2,128,128]{2,1,0:T(8,128)(2,1)S(1)} %get-tuple-element.84), channel_id=1, source_target_pairs={{0,16},{8,24},{16,0},{24,8},{1,17},{9,25},{17,1},{25,9},{2,18},{10... | collective-permute-start | bytes 196616 | tf_op jit(solution)/shard_map/ppermute | solution.py:164
  44.5 5.5 %collective-permute-start.27 = (bf16[2,128,128]{2,1,0:T(8,128)(2,1)S(1)}, bf16[2,128,128]{2,1,0:T(8,128)(2,1)S(1)}, u32[]{:S(2)}, u32[]{:S(2)}) collective-permute-start(bf16[2,128,128]{2,1,0:T(8,128)(2,1)S(1)} %get-tuple-element.85), channel_id=1, source_target_pairs={{0,8},{8,0},{16,24},{24,16},{1,9},{9,1},{17,25},{25,17},{2,10},{10... | collective-permute-start | bytes 196616 | tf_op jit(solution)/shard_map/ppermute | solution.py:164
  46.5 6.2 %collective-permute-start.16 = (bf16[2,2,128,128]{3,2,1,0:T(8,128)(2,1)S(1)}, bf16[2,2,128,128]{3,2,1,0:T(8,128)(2,1)S(1)}, u32[]{:S(2)}, u32[]{:S(2)}) collective-permute-start(bf16[2,2,128,128]{3,2,1,0:T(8,128)(2,1)S(1)} %get-tuple-element.70), channel_id=1, source_target_pairs={{0,2},{1,3},{2,0},{3,1},{4,6},{5,7},{6,4},{7,5},{8,10},{9,11},{10,... | collective-permute-start | bytes 393224 | tf_op jit(solution)/shard_map/ppermute | solution.py:158
  48.1 8.0 %collective-permute-start.17 = (bf16[2,2,128,128]{3,2,1,0:T(8,128)(2,1)S(1)}, bf16[2,2,128,128]{3,2,1,0:T(8,128)(2,1)S(1)}, u32[]{:S(2)}, u32[]{:S(2)}) collective-permute-start(bf16[2,2,128,128]{3,2,1,0:T(8,128)(2,1)S(1)} %get-tuple-element.71), channel_id=1, source_target_pairs={{0,4},{1,5},{2,6},{3,7},{4,0},{5,1},{6,2},{7,3},{8,12},{9,13},{10,... | collective-permute-start | bytes 393224 | tf_op jit(solution)/shard_map/ppermute | solution.py:158
  48.4 7.7 %collective-permute-start.18 = (bf16[2,2,128,128]{3,2,1,0:T(8,128)(2,1)S(1)}, bf16[2,2,128,128]{3,2,1,0:T(8,128)(2,1)S(1)}, u32[]{:S(2)}, u32[]{:S(2)}) collective-permute-start(bf16[2,2,128,128]{3,2,1,0:T(8,128)(2,1)S(1)} %get-tuple-element.72), channel_id=1, source_target_pairs={{0,6},{1,7},{2,4},{3,5},{4,2},{5,3},{6,0},{7,1},{8,14},{9,15},{10,... | collective-permute-start | bytes 393224 | tf_op jit(solution)/shard_map/ppermute | solution.py:158
  50.8 5.5 %collective-permute-start.28 = (bf16[2,2,128,128]{3,2,1,0:T(8,128)(2,1)S(1)}, bf16[2,2,128,128]{3,2,1,0:T(8,128)(2,1)S(1)}, u32[]{:S(2)}, u32[]{:S(2)}) collective-permute-start(bf16[2,2,128,128]{3,2,1,0:T(8,128)(2,1)S(1)} %get-tuple-element.87), channel_id=1, source_target_pairs={{0,2},{1,3},{2,0},{3,1},{4,6},{5,7},{6,4},{7,5},{8,10},{9,11},{10,... | collective-permute-start | bytes 393224 | tf_op jit(solution)/shard_map/ppermute | solution.py:158
  52.4 6.6 %collective-permute-start.29 = (bf16[2,2,128,128]{3,2,1,0:T(8,128)(2,1)S(1)}, bf16[2,2,128,128]{3,2,1,0:T(8,128)(2,1)S(1)}, u32[]{:S(2)}, u32[]{:S(2)}) collective-permute-start(bf16[2,2,128,128]{3,2,1,0:T(8,128)(2,1)S(1)} %get-tuple-element.88), channel_id=1, source_target_pairs={{0,4},{1,5},{2,6},{3,7},{4,0},{5,1},{6,2},{7,3},{8,12},{9,13},{10,... | collective-permute-start | bytes 393224 | tf_op jit(solution)/shard_map/ppermute | solution.py:158
  52.7 6.2 %collective-permute-start.30 = (bf16[2,2,128,128]{3,2,1,0:T(8,128)(2,1)S(1)}, bf16[2,2,128,128]{3,2,1,0:T(8,128)(2,1)S(1)}, u32[]{:S(2)}, u32[]{:S(2)}) collective-permute-start(bf16[2,2,128,128]{3,2,1,0:T(8,128)(2,1)S(1)} %get-tuple-element.89), channel_id=1, source_target_pairs={{0,6},{1,7},{2,4},{3,5},{4,2},{5,3},{6,0},{7,1},{8,14},{9,15},{10,... | collective-permute-start | bytes 393224 | tf_op jit(solution)/shard_map/ppermute | solution.py:158
  56.2 4.1 %copy-start.1 = (bf16[512,512]{1,0:T(8,128)(2,1)S(1)}, bf16[512,512]{1,0:T(8,128)(2,1)}, u32[]{:S(2)}) copy-start(bf16[512,512]{1,0:T(8,128)(2,1)} %refs_4_.1) | copy-start | bytes 1572868
  56.2 2.9 %collective-permute-start.31 = (bf16[2,128,128]{2,1,0:T(8,128)(2,1)S(1)}, bf16[2,128,128]{2,1,0:T(8,128)(2,1)S(1)}, u32[]{:S(2)}, u32[]{:S(2)}) collective-permute-start(bf16[2,128,128]{2,1,0:T(8,128)(2,1)S(1)} %get-tuple-element.91), channel_id=1, source_target_pairs={{0,1},{1,0},{2,3},{3,2},{4,5},{5,4},{6,7},{7,6},{8,9},{9,8},{10,11... | collective-permute-start | bytes 196616 | tf_op jit(solution)/shard_map/ppermute | solution.py:158
  59.0 1.3 %collective-permute-start.32 = (bf16[2,128,128]{2,1,0:T(8,128)(2,1)S(1)}, bf16[2,128,128]{2,1,0:T(8,128)(2,1)S(1)}, u32[]{:S(2)}, u32[]{:S(2)}) collective-permute-start(bf16[2,128,128]{2,1,0:T(8,128)(2,1)S(1)} %get-tuple-element.92), channel_id=1, source_target_pairs={{0,1},{1,0},{2,3},{3,2},{4,5},{5,4},{6,7},{7,6},{8,9},{9,8},{10,11... | collective-permute-start | bytes 196616 | tf_op jit(solution)/shard_map/ppermute | solution.py:158

commit v5 on v4

--- a/solution.py
+++ b/solution.py
@@ -27,15 +27,15 @@
     for r, table, tiles in ((0, own_table, own_tiles), (1, peer_table, peer_tiles)):
 
         def add(t, carry, r=r, table=table, tiles=tiles):
-            block = table[2 * t]
+            block = table[0, 2 * t]
             e = ((block // per_device) % owners) ^ col_pos
-            s = (table[2 * t + 1] % rows) ^ row_pos
+            s = (table[0, 2 * t + 1] % rows) ^ row_pos
             picks[r * owners + e] = jnp.full(picks.shape[1:], block % per_device, jnp.int32)
             cols = pl.ds(pl.multiple_of(s * tile, tile), tile)
             dense[r, e, :, cols] = (dense[r, e, :, cols].astype(FULL) + tiles[0, t].astype(FULL)).astype(HALF)
             return carry
 
-        lax.fori_loop(0, table[2 * slots], add, 0)
+        lax.fori_loop(0, table[0, 2 * slots], add, 0)
 
 
 def project_kernel(own_hbm, peer_hbm, weight_hbm, out, own, peer, weight, sems):
@@ -56,19 +56,30 @@
         out[r] = product.reshape(out.shape[1:])
 
 
-def farthest_last(items):
-    return [items[0], *items[:0:-1]]
+def distances(rows):
+    return [0] + sorted(range(1, rows), key=lambda s: s ^ rows // 2)
+
+
+def by_distance(items):
+    order = distances(len(items))
+    return [items[order.index(s)] for s in range(len(items))]
+
+
+def reads_first(needed):
+    lane = lax.broadcasted_iota(jnp.int32, needed.shape, 1)
+    here = jnp.where(lane == lax.axis_index("row"), needed[...], 0).astype(FULL)
+    return jnp.sum(here, axis=1, keepdims=True) < 0.5
 
 
 def select_kernel(*refs, rows):
-    needed, values, outs = farthest_last(refs[:rows]), refs[rows], refs[rows + 1 :]
-    row_pos = lax.axis_index("row")
+    needed, values, outs = by_distance(refs[:rows]), refs[rows], refs[rows + 1 :]
     columns = outs[0].shape[-1]
     for s in range(rows):
+        first = reads_first(needed[s])
         for r in range(2):
-            block = needed[s][r, row_pos]
+            block = jnp.where(first[r : r + 1], values[r, 0].astype(FULL), values[r, 1].astype(FULL)).astype(HALF)
             for j in range(len(outs) // rows):
-                outs[j * rows + s][r] = values[r, block, :, j * columns : (j + 1) * columns]
+                outs[j * rows + s][r] = block[:, j * columns : (j + 1) * columns]
 
 
 def multiply_kernel(*refs):
@@ -78,7 +89,7 @@
     pieces, outs = refs[2 : 2 + rows], refs[2 + rows :]
     chips = owners // 2
     columns = outs[0].shape[-1]
-    operands = [jnp.concatenate([piece[r] for piece in farthest_last(pieces)], axis=0) for r in range(2)]
+    operands = [jnp.concatenate([piece[r] for piece in by_distance(pieces)], axis=0) for r in range(2)]
     products = [jnp.dot(dense[r].reshape(owners * tile, depth), operands[r], preferred_element_type=FULL) for r in range(2)]
     for e in range(owners):
         own, peer = (product[e * tile : (e + 1) * tile] for product in products)
@@ -96,15 +107,12 @@
 
 
 def hidden_kernel(*refs, rows):
-    values = refs[-1]
-    needed, parts, outs = farthest_last(refs[:rows]), refs[rows : -1 - rows], refs[-1 - rows : -1]
-    row_pos = lax.axis_index("row")
+    needed, parts, outs = by_distance(refs[:rows]), refs[rows:-rows], refs[-rows:]
+    firsts = [reads_first(x) for x in needed]
     for r in range(2):
-        for b in range(2):
-            values[r, b] = jnp.maximum(added(parts, r, b), 0.0).astype(HALF)
-    for s, out in enumerate(outs):
-        for r in range(2):
-            out[r] = values[r, needed[s][r, row_pos]]
+        blocks = [jnp.maximum(added(parts, r, b), 0.0) for b in range(2)]
+        for first, out in zip(firsts, outs):
+            out[r] = jnp.where(first[r : r + 1], *blocks).astype(HALF)
 
 
 def mixed_kernel(*refs):
@@ -114,21 +122,31 @@
         peer[b] = added(parts, 1, b).astype(HALF)
 
 
-def final_kernel(*refs):
+def weighted(chunks, weight, side, start):
+    core = lax.axis_index("col") % 2
+    at = (core ^ side) * (weight.shape[0] // 2) + start
+    total = None
+    for x in chunks:
+        _, tile, width = x.shape
+        rows = weight[pl.ds(pl.multiple_of(at, width), width), :]
+        product = jnp.dot(x[...].reshape(2 * tile, width), rows, preferred_element_type=FULL)
+        total = product if total is None else total + product
+        at = at + width
+    return total
+
+
+def partial_kernel(*refs):
     weight, out = refs[-2:]
-    sides = refs[: len(refs) // 2 - 1], refs[len(refs) // 2 - 1 : -2]
-    core = lax.axis_index("col") % 2
-    total = None
-    for side, chunks in enumerate(sides):
-        at = (core ^ side) * (weight.shape[0] // 2)
-        for x in chunks:
-            width = x.shape[-1]
-            rows = x[...].reshape(out.shape[0], width)
-            columns = weight[pl.ds(pl.multiple_of(at, width), width), :]
-            product = jnp.dot(rows, columns, preferred_element_type=FULL)
-            total = product if total is None else total + product
-            at = at + width
-    out[...] = total.astype(HALF)
+    chunks = len(refs) // 2 - 1
+    total = weighted(refs[: chunks + 1], weight, 0, 0)
+    if chunks:
+        total = total + weighted(refs[chunks + 1 : -2], weight, 1, 0)
+    out[...] = total
+
+
+def final_kernel(partial, last, weight, out):
+    start = weight.shape[0] // 2 - last.shape[-1]
+    out[...] = (partial[...] + weighted([last], weight, 1, start)).astype(HALF)
 
 
 def body(features, tile_values, tile_blocks, tile_count, needed, weight_one, weight_two):
@@ -168,7 +186,7 @@
 
     needs = jnp.concatenate([needed, swap(needed)], axis=0)
     features, tile_values, needs = lax.optimization_barrier((features, tile_values, needs))
-    needs = [needs] + [by_row(needs, s) for s in range(row_count - 1, 0, -1)]
+    needs = [needs] + [by_row(needs, s) for s in distances(row_count)[1:]]
     peer_features = swap(features)
     projected = call(
         project_kernel,
@@ -184,7 +202,7 @@
         name="project",
     )
     tile_blocks, tile_count, projected = lax.optimization_barrier((tile_blocks, tile_count, projected))
-    table = jnp.concatenate([tile_blocks.reshape(-1), tile_count])
+    table = jnp.concatenate([tile_blocks.reshape(1, -1), tile_count.reshape(1, 1)], axis=1)
     dense, picks = call(
         build_kernel,
         [shape(2, col_count, tile, row_count * tile), shape(2 * col_count, 1, tile, dtype=jnp.int32)],
@@ -195,7 +213,7 @@
     columns = width // CHUNKS
 
     def to_readers(pieces):
-        return [pieces[0]] + [by_row(pieces[s], s) for s in range(row_count - 1, 0, -1)]
+        return [pieces[0]] + [by_row(pieces[s], s) for s in distances(row_count)[1:]]
 
     def to_owners(pieces):
         chunks = pieces[0].shape[-1] // columns
@@ -212,7 +230,6 @@
         functools.partial(select_kernel, rows=row_count),
         [shape(2, tile, columns)] * (row_count * CHUNKS),
         [*needs, projected],
-        in_specs=[SMEM] * row_count + [VMEM],
         name="select",
     )
     panels = [to_readers(selected[j * row_count : (j + 1) * row_count]) for j in range(CHUNKS)]
@@ -223,8 +240,6 @@
             functools.partial(hidden_kernel, rows=row_count),
             [shape(2, tile, columns)] * row_count,
             [*needs, *parts],
-            in_specs=[SMEM] * row_count + [VMEM] * len(parts),
-            scratch_shapes=[pltpu.VMEM((2, 2, tile, columns), HALF)],
             name="hidden",
         )
         panels.append(to_readers(selected))
@@ -234,7 +249,10 @@
         own, other = call(mixed_kernel, [shape(2, tile, columns)] * 2, parts, name="mixed")
         mine.append(own)
         theirs.append(swap(other))
-    return call(final_kernel, shape(*features.shape), [*mine, *theirs, weight_two], name="final")
+    partial = call(
+        partial_kernel, shape(*features.shape, dtype=FULL), [*mine, *theirs[:-1], weight_two], name="partial"
+    )
+    return call(final_kernel, shape(*features.shape), [partial, theirs[-1], weight_two], name="final")
 
 
 def solution(mesh):

time: 61.5 us -> 60 us (0.976)
  Pallas kernels: 8.77 us -> 6.95 us
    ppermute x18, starting transfers between devices: 15.3 us -> 17.8 us  [by_col(): lax.ppermute(x, 'col', [(i, i ^ masks[i % 2]) for i in range(col_count)])]
    ppermute x15, starting transfers between devices: 23.6 us -> 21.5 us  [by_row(): return lax.ppermute(x, 'row', [(i, i ^ s) for i in range(row_count)])]
    ppermute x18, waiting for transfers between devices: 9.23 us -> 7.23 us  [by_col(): lax.ppermute(x, 'col', [(i, i ^ masks[i % 2]) for i in range(col_count)])]
    pallas_call x12 -> x13, Pallas kernels: 8.77 us -> 6.95 us  [call(): pl.pallas_call(kernel, in_specs=in_specs or [VMEM] * len(args), out_specs...]
    ppermute x15, waiting for transfers between devices: 2.79 us -> 4.59 us  [by_row(): return lax.ppermute(x, 'row', [(i, i ^ s) for i in range(row_count)])]
  transfers between devices with their start and end apart: 33 -> 33, of which waited for: 7 -> 14; matrix products, arithmetic and copies ran while one was open for 0% -> 0% of each run, Pallas kernels for 12% -> 10%
where the time goes in v5:
time: 60 us; the launch traced here: 59.9 us
  starting transfers between devices  39.3 us (65%)
  waiting for transfers between devices  11.8 us (20%)
  Pallas kernels  6.95 us (12%)
  between operations  0.85 us (1%)
  other arithmetic  0.74 us (1%)
    ppermute x15, starting transfers between devices, by_row(): return lax.ppermute(x, 'row', [(i, i ^ s) for i in range(row_count)])  21.5 us
    ppermute x18, starting transfers between devices, by_col(): lax.ppermute(x, 'col', [(i, i ^ masks[i % 2]) for i in range(col_count)])  17.8 us
    ppermute x18, waiting for transfers between devices, by_col(): lax.ppermute(x, 'col', [(i, i ^ masks[i % 2]) for i in range(col_count)])  7.23 us
    pallas_call x13, Pallas kernels, call(): pl.pallas_call(kernel, in_specs=in_specs or [VMEM] * len(args), out_specs...  6.95 us
    ppermute x15, waiting for transfers between devices, by_row(): return lax.ppermute(x, 'row', [(i, i ^ s) for i in range(row_count)])  4.59 us
  transfers between devices with their start and end apart: 33, of which 14 were waited for; matrix products, arithmetic and copies ran while one was open for 0% of the time, Pallas kernels for 10%

profile of v5, /device:TPU:0, one launch (start us, length us, event | category | flops | bytes accessed | tf_op | source)
XLA Modules:
  0.0 59.9 jit_solution(10225658305359010275)
XLA Ops:
  0.0 0.5 collective-permute-start
  0.5 1.0 %collective-permute-done = s32[1,4]{1,0:T(1,128)S(1)} collective-permute-done((s32[1,4]{1,0:T(1,128)}, s32[1,4]{1,0:T(1,128)S(1)}, u32[]{:S(2)}, u32[]{:S(2)}) %collective-permute-start) | collective-permute-done | bytes 48 | tf_op jit(solution)/shard_map/ppermute | solution.py:176
  1.4 0.7 %pad_add_fusion.refs_0_ = s32[2,4]{1,0:T(2,128)S(1)} fusion(s32[1,4]{1,0:T(1,128)S(1)} %collective-permute-done, s32[1,4]{1,0:T(1,128)} %param.11), kind=kLoop, calls=%fused_computation | loop fusion | flops 8 | bytes 64 | tf_op jit(solution)/shard_map/concatenate | solution.py:187
  2.1 0.3 collective-permute-start.1
  2.4 0.2 collective-permute-start.3
  3.2 4.0 %collective-permute-start.4 = (s32[2,4]{1,0:T(2,128)S(1)}, s32[2,4]{1,0:T(2,128)S(1)}, u32[]{:S(2)}, u32[]{:S(2)}) collective-permute-start(s32[2,4]{1,0:T(2,128)S(1)} %pad_add_fusion.refs_0_), channel_id=1, source_target_pairs={{0,16},{8,24},{16,0},{24,8},{1,17},{9,25},{17,1},{25,9},{2,18},{10... | collective-permute-start | bytes 104 | tf_op jit(solution)/shard_map/ppermute | solution.py:182
  7.2 1.3 %collective-permute-start.5 = (s32[2,4]{1,0:T(2,128)S(1)}, s32[2,4]{1,0:T(2,128)S(1)}, u32[]{:S(2)}, u32[]{:S(2)}) collective-permute-start(s32[2,4]{1,0:T(2,128)S(1)} %pad_add_fusion.refs_0_), channel_id=1, source_target_pairs={{0,24},{8,16},{16,8},{24,0},{1,25},{9,17},{17,9},{25,1},{2,26},{10... | collective-permute-start | bytes 104 | tf_op jit(solution)/shard_map/ppermute | solution.py:182
  8.5 0.2 collective-permute-start.6
  8.8 1.4 %project.1.refs_4_ = bf16[2,2,128,256]{3,2,1,0:T(8,128)(2,1)S(1)} custom-call(bf16[256,512]{1,0:T(8,128)(2,1)} %own_hbm, bf16[256,512]{1,0:T(8,128)(2,1)S(1)} %collective-permute-done.1.peer_hbm, bf16[512,512]{1,0:T(8,128)(2,1)} %weight_hbm.1), custom_call_target="tpu_custom_call" | custom-call | flops 1000000000 | bytes 10000000 | tf_op jit(solution)/shard_map/project/pallas_call | solution.py:162
  10.4 2.1 %collective-permute-done.5.refs_2_ = s32[2,4]{1,0:T(2,128)S(1)} collective-permute-done((s32[2,4]{1,0:T(2,128)S(1)}, s32[2,4]{1,0:T(2,128)S(1)}, u32[]{:S(2)}, u32[]{:S(2)}) %collective-permute-start.5) | collective-permute-done | bytes 64 | tf_op jit(solution)/shard_map/ppermute | solution.py:182
  12.6 0.2 select.1
  12.8 1.3 %collective-permute-start.7 = (bf16[2,128,128]{2,1,0:T(8,128)(2,1)S(1)}, bf16[2,128,128]{2,1,0:T(8,128)(2,1)S(1)}, u32[]{:S(2)}, u32[]{:S(2)}) collective-permute-start(bf16[2,128,128]{2,1,0:T(8,128)(2,1)S(1)} %get-tuple-element.58), channel_id=1, source_target_pairs={{0,16},{8,24},{16,0},{24,8},{1,17},{9,25},{17,1},{25,9},{2,18},{10... | collective-permute-start | bytes 196616 | tf_op jit(solution)/shard_map/ppermute | solution.py:182
  14.1 0.9 %collective-permute-start.8 = (bf16[2,128,128]{2,1,0:T(8,128)(2,1)S(1)}, bf16[2,128,128]{2,1,0:T(8,128)(2,1)S(1)}, u32[]{:S(2)}, u32[]{:S(2)}) collective-permute-start(bf16[2,128,128]{2,1,0:T(8,128)(2,1)S(1)} %get-tuple-element.59), channel_id=1, source_target_pairs={{0,24},{8,16},{16,8},{24,0},{1,25},{9,17},{17,9},{25,1},{2,26},{10... | collective-permute-start | bytes 196616 | tf_op jit(solution)/shard_map/ppermute | solution.py:182
  15.0 1.3 %collective-permute-start.9 = (bf16[2,128,128]{2,1,0:T(8,128)(2,1)S(1)}, bf16[2,128,128]{2,1,0:T(8,128)(2,1)S(1)}, u32[]{:S(2)}, u32[]{:S(2)}) collective-permute-start(bf16[2,128,128]{2,1,0:T(8,128)(2,1)S(1)} %get-tuple-element.60), channel_id=1, source_target_pairs={{0,8},{8,0},{16,24},{24,16},{1,9},{9,1},{17,25},{25,17},{2,10},{10... | collective-permute-start | bytes 196616 | tf_op jit(solution)/shard_map/ppermute | solution.py:182
  16.3 2.1 %collective-permute-start.19 = (bf16[2,128,128]{2,1,0:T(8,128)(2,1)S(1)}, bf16[2,128,128]{2,1,0:T(8,128)(2,1)S(1)}, u32[]{:S(2)}, u32[]{:S(2)}) collective-permute-start(bf16[2,128,128]{2,1,0:T(8,128)(2,1)S(1)} %get-tuple-element.75), channel_id=1, source_target_pairs={{0,16},{8,24},{16,0},{24,8},{1,17},{9,25},{17,1},{25,9},{2,18},{10... | collective-permute-start | bytes 196616 | tf_op jit(solution)/shard_map/ppermute | solution.py:182
  18.5 0.9 %collective-permute-start.20 = (bf16[2,128,128]{2,1,0:T(8,128)(2,1)S(1)}, bf16[2,128,128]{2,1,0:T(8,128)(2,1)S(1)}, u32[]{:S(2)}, u32[]{:S(2)}) collective-permute-start(bf16[2,128,128]{2,1,0:T(8,128)(2,1)S(1)} %get-tuple-element.76), channel_id=1, source_target_pairs={{0,24},{8,16},{16,8},{24,0},{1,25},{9,17},{17,9},{25,1},{2,26},{10... | collective-permute-start | bytes 196616 | tf_op jit(solution)/shard_map/ppermute | solution.py:182
  19.4 0.9 %build.1 = (bf16[2,8,128,512]{3,2,1,0:T(8,128)(2,1)S(1)}, s32[16,1,128]{2,1,0:T(1,128)S(1)}) custom-call(s32[1,33]{1,0:T(1,128)S(1)} %pad_add_fusion.1.own_table, s32[1,33]{1,0:T(1,128)S(1)} %collective-permute-done.2.peer_table, bf16[1,16,128,128]{3,2,1,0:T(8,128)(2,1)S(1)} %copy-done, bf16[1,16,128,128]{3,2,1,0:T(8,128)(2,1)S(1)} %collective-permute-done.3.peer_tiles), custom_call_target="tpu_custom_call" | custom-call | flops 1000000000 | bytes 10000000 | tf_op jit(solution)/shard_map/build/pallas_call | solution.py:162
  20.3 0.5 collective-permute-start.21
  21.1 0.7 %multiply.4 = (bf16[2,2,128,128]{3,2,1,0:T(8,128)(2,1)S(1)}, bf16[2,2,128,128]{3,2,1,0:T(8,128)(2,1)S(1)}, bf16[2,2,128,128]{3,2,1,0:T(8,128)(2,1)S(1)}, bf16[2,2,128,128]{3,2,1,0:T(8,128)(2,1)S(1)}) custom-call(s32[16,1,128]{2,1,0:T(1,128)S(1)} %get-tuple-element.53.refs_0_, bf16[2,8,128,512]{3,2,1,0:T(8,128)(2,1)S(1)} %get-tuple-element.54.refs_1_, ...), custom_call_target="tpu_custom_call" | custom-call | flops 1000000000 | bytes 10000000 | tf_op jit(solution)/shard_map/multiply/pallas_call | solution.py:162
  21.8 1.6 %collective-permute-start.10 = (bf16[2,2,128,128]{3,2,1,0:T(8,128)(2,1)S(1)}, bf16[2,2,128,128]{3,2,1,0:T(8,128)(2,1)S(1)}, u32[]{:S(2)}, u32[]{:S(2)}) collective-permute-start(bf16[2,2,128,128]{3,2,1,0:T(8,128)(2,1)S(1)} %get-tuple-element.62), channel_id=1, source_target_pairs={{0,2},{1,3},{2,0},{3,1},{4,6},{5,7},{6,4},{7,5},{8,10},{9,11},{10,... | collective-permute-start | bytes 393224 | tf_op jit(solution)/shard_map/ppermute | solution.py:176
  23.3 1.5 %collective-permute-start.11 = (bf16[2,2,128,128]{3,2,1,0:T(8,128)(2,1)S(1)}, bf16[2,2,128,128]{3,2,1,0:T(8,128)(2,1)S(1)}, u32[]{:S(2)}, u32[]{:S(2)}) collective-permute-start(bf16[2,2,128,128]{3,2,1,0:T(8,128)(2,1)S(1)} %get-tuple-element.63), channel_id=1, source_target_pairs={{0,4},{1,5},{2,6},{3,7},{4,0},{5,1},{6,2},{7,3},{8,12},{9,13},{10,... | collective-permute-start | bytes 393224 | tf_op jit(solution)/shard_map/ppermute | solution.py:176
  24.9 0.9 %collective-permute-done.19.refs_3_ = bf16[2,128,128]{2,1,0:T(8,128)(2,1)S(1)} collective-permute-done((bf16[2,128,128]{2,1,0:T(8,128)(2,1)S(1)}, bf16[2,128,128]{2,1,0:T(8,128)(2,1)S(1)}, u32[]{:S(2)}, u32[]{:S(2)}) %collective-permute-start.19) | collective-permute-done | bytes 65568 | tf_op jit(solution)/shard_map/ppermute | solution.py:182
  25.8 2.4 %collective-permute-start.12 = (bf16[2,2,128,128]{3,2,1,0:T(8,128)(2,1)S(1)}, bf16[2,2,128,128]{3,2,1,0:T(8,128)(2,1)S(1)}, u32[]{:S(2)}, u32[]{:S(2)}) collective-permute-start(bf16[2,2,128,128]{3,2,1,0:T(8,128)(2,1)S(1)} %get-tuple-element.64), channel_id=1, source_target_pairs={{0,6},{1,7},{2,4},{3,5},{4,2},{5,3},{6,0},{7,1},{8,14},{9,15},{10,... | collective-permute-start | bytes 393224 | tf_op jit(solution)/shard_map/ppermute | solution.py:176
  28.3 0.7 %multiply.6 = (bf16[2,2,128,128]{3,2,1,0:T(8,128)(2,1)S(1)}, bf16[2,2,128,128]{3,2,1,0:T(8,128)(2,1)S(1)}, bf16[2,2,128,128]{3,2,1,0:T(8,128)(2,1)S(1)}, bf16[2,2,128,128]{3,2,1,0:T(8,128)(2,1)S(1)}) custom-call(s32[16,1,128]{2,1,0:T(1,128)S(1)} %get-tuple-element.53.refs_0_, bf16[2,8,128,512]{3,2,1,0:T(8,128)(2,1)S(1)} %get-tuple-element.54.refs_1_, ...), custom_call_target="tpu_custom_call" | custom-call | flops 1000000000 | bytes 10000000 | tf_op jit(solution)/shard_map/multiply/pallas_call | solution.py:162
  29.0 0.6 %collective-permute-start.22 = (bf16[2,2,128,128]{3,2,1,0:T(8,128)(2,1)S(1)}, bf16[2,2,128,128]{3,2,1,0:T(8,128)(2,1)S(1)}, u32[]{:S(2)}, u32[]{:S(2)}) collective-permute-start(bf16[2,2,128,128]{3,2,1,0:T(8,128)(2,1)S(1)} %get-tuple-element.79), channel_id=1, source_target_pairs={{0,2},{1,3},{2,0},{3,1},{4,6},{5,7},{6,4},{7,5},{8,10},{9,11},{10,... | collective-permute-start | bytes 393224 | tf_op jit(solution)/shard_map/ppermute | solution.py:176
  29.6 0.5 collective-permute-start.23
  30.1 2.4 %collective-permute-start.24 = (bf16[2,2,128,128]{3,2,1,0:T(8,128)(2,1)S(1)}, bf16[2,2,128,128]{3,2,1,0:T(8,128)(2,1)S(1)}, u32[]{:S(2)}, u32[]{:S(2)}) collective-permute-start(bf16[2,2,128,128]{3,2,1,0:T(8,128)(2,1)S(1)} %get-tuple-element.81), channel_id=1, source_target_pairs={{0,6},{1,7},{2,4},{3,5},{4,2},{5,3},{6,0},{7,1},{8,14},{9,15},{10,... | collective-permute-start | bytes 393224 | tf_op jit(solution)/shard_map/ppermute | solution.py:176
  32.7 0.5 collective-permute-done.12.refs_7_
  33.4 3.8 %collective-permute-start.13 = (bf16[2,128,128]{2,1,0:T(8,128)(2,1)S(1)}, bf16[2,128,128]{2,1,0:T(8,128)(2,1)S(1)}, u32[]{:S(2)}, u32[]{:S(2)}) collective-permute-start(bf16[2,128,128]{2,1,0:T(8,128)(2,1)S(1)} %get-tuple-element.66), channel_id=1, source_target_pairs={{0,16},{8,24},{16,0},{24,8},{1,17},{9,25},{17,1},{25,9},{2,18},{10... | collective-permute-start | bytes 196616 | tf_op jit(solution)/shard_map/ppermute | solution.py:182
  37.1 0.7 %collective-permute-start.14 = (bf16[2,128,128]{2,1,0:T(8,128)(2,1)S(1)}, bf16[2,128,128]{2,1,0:T(8,128)(2,1)S(1)}, u32[]{:S(2)}, u32[]{:S(2)}) collective-permute-start(bf16[2,128,128]{2,1,0:T(8,128)(2,1)S(1)} %get-tuple-element.67), channel_id=1, source_target_pairs={{0,24},{8,16},{16,8},{24,0},{1,25},{9,17},{17,9},{25,1},{2,26},{10... | collective-permute-start | bytes 196616 | tf_op jit(solution)/shard_map/ppermute | solution.py:182
  38.0 3.8 %collective-permute-start.25 = (bf16[2,128,128]{2,1,0:T(8,128)(2,1)S(1)}, bf16[2,128,128]{2,1,0:T(8,128)(2,1)S(1)}, u32[]{:S(2)}, u32[]{:S(2)}) collective-permute-start(bf16[2,128,128]{2,1,0:T(8,128)(2,1)S(1)} %get-tuple-element.83), channel_id=1, source_target_pairs={{0,16},{8,24},{16,0},{24,8},{1,17},{9,25},{17,1},{25,9},{2,18},{10... | collective-permute-start | bytes 196616 | tf_op jit(solution)/shard_map/ppermute | solution.py:182
  41.7 0.7 %collective-permute-start.26 = (bf16[2,128,128]{2,1,0:T(8,128)(2,1)S(1)}, bf16[2,128,128]{2,1,0:T(8,128)(2,1)S(1)}, u32[]{:S(2)}, u32[]{:S(2)}) collective-permute-start(bf16[2,128,128]{2,1,0:T(8,128)(2,1)S(1)} %get-tuple-element.84), channel_id=1, source_target_pairs={{0,24},{8,16},{16,8},{24,0},{1,25},{9,17},{17,9},{25,1},{2,26},{10... | collective-permute-start | bytes 196616 | tf_op jit(solution)/shard_map/ppermute | solution.py:182
  42.4 0.9 %collective-permute-done.14.refs_4_ = bf16[2,128,128]{2,1,0:T(8,128)(2,1)S(1)} collective-permute-done((bf16[2,128,128]{2,1,0:T(8,128)(2,1)S(1)}, bf16[2,128,128]{2,1,0:T(8,128)(2,1)S(1)}, u32[]{:S(2)}, u32[]{:S(2)}) %collective-permute-start.14) | collective-permute-done | bytes 65568 | tf_op jit(solution)/shard_map/ppermute | solution.py:182
  43.4 0.3 collective-permute-done.15.refs_5_
  43.7 0.7 %multiply.5 = (bf16[2,2,128,128]{3,2,1,0:T(8,128)(2,1)S(1)}, bf16[2,2,128,128]{3,2,1,0:T(8,128)(2,1)S(1)}, bf16[2,2,128,128]{3,2,1,0:T(8,128)(2,1)S(1)}, bf16[2,2,128,128]{3,2,1,0:T(8,128)(2,1)S(1)}) custom-call(s32[16,1,128]{2,1,0:T(1,128)S(1)} %get-tuple-element.53.refs_0_, bf16[2,8,128,512]{3,2,1,0:T(8,128)(2,1)S(1)} %get-tuple-element.54.refs_1_, ...), custom_call_target="tpu_custom_call" | custom-call | flops 1000000000 | bytes 10000000 | tf_op jit(solution)/shard_map/multiply/pallas_call | solution.py:162
  44.4 1.9 %collective-permute-start.16 = (bf16[2,2,128,128]{3,2,1,0:T(8,128)(2,1)S(1)}, bf16[2,2,128,128]{3,2,1,0:T(8,128)(2,1)S(1)}, u32[]{:S(2)}, u32[]{:S(2)}) collective-permute-start(bf16[2,2,128,128]{3,2,1,0:T(8,128)(2,1)S(1)} %get-tuple-element.70), channel_id=1, source_target_pairs={{0,2},{1,3},{2,0},{3,1},{4,6},{5,7},{6,4},{7,5},{8,10},{9,11},{10,... | collective-permute-start | bytes 393224 | tf_op jit(solution)/shard_map/ppermute | solution.py:176
  46.2 0.8 %collective-permute-start.17 = (bf16[2,2,128,128]{3,2,1,0:T(8,128)(2,1)S(1)}, bf16[2,2,128,128]{3,2,1,0:T(8,128)(2,1)S(1)}, u32[]{:S(2)}, u32[]{:S(2)}) collective-permute-start(bf16[2,2,128,128]{3,2,1,0:T(8,128)(2,1)S(1)} %get-tuple-element.71), channel_id=1, source_target_pairs={{0,4},{1,5},{2,6},{3,7},{4,0},{5,1},{6,2},{7,3},{8,12},{9,13},{10,... | collective-permute-start | bytes 393224 | tf_op jit(solution)/shard_map/ppermute | solution.py:176
  47.0 1.4 %collective-permute-start.18 = (bf16[2,2,128,128]{3,2,1,0:T(8,128)(2,1)S(1)}, bf16[2,2,128,128]{3,2,1,0:T(8,128)(2,1)S(1)}, u32[]{:S(2)}, u32[]{:S(2)}) collective-permute-start(bf16[2,2,128,128]{3,2,1,0:T(8,128)(2,1)S(1)} %get-tuple-element.72), channel_id=1, source_target_pairs={{0,6},{1,7},{2,4},{3,5},{4,2},{5,3},{6,0},{7,1},{8,14},{9,15},{10,... | collective-permute-start | bytes 393224 | tf_op jit(solution)/shard_map/ppermute | solution.py:176
  48.4 0.7 %multiply.7 = (bf16[2,2,128,128]{3,2,1,0:T(8,128)(2,1)S(1)}, bf16[2,2,128,128]{3,2,1,0:T(8,128)(2,1)S(1)}, bf16[2,2,128,128]{3,2,1,0:T(8,128)(2,1)S(1)}, bf16[2,2,128,128]{3,2,1,0:T(8,128)(2,1)S(1)}) custom-call(s32[16,1,128]{2,1,0:T(1,128)S(1)} %get-tuple-element.53.refs_0_, bf16[2,8,128,512]{3,2,1,0:T(8,128)(2,1)S(1)} %get-tuple-element.54.refs_1_, ...), custom_call_target="tpu_custom_call" | custom-call | flops 1000000000 | bytes 10000000 | tf_op jit(solution)/shard_map/multiply/pallas_call | solution.py:162
  49.1 1.4 %collective-permute-start.28 = (bf16[2,2,128,128]{3,2,1,0:T(8,128)(2,1)S(1)}, bf16[2,2,128,128]{3,2,1,0:T(8,128)(2,1)S(1)}, u32[]{:S(2)}, u32[]{:S(2)}) collective-permute-start(bf16[2,2,128,128]{3,2,1,0:T(8,128)(2,1)S(1)} %get-tuple-element.87), channel_id=1, source_target_pairs={{0,2},{1,3},{2,0},{3,1},{4,6},{5,7},{6,4},{7,5},{8,10},{9,11},{10,... | collective-permute-start | bytes 393224 | tf_op jit(solution)/shard_map/ppermute | solution.py:176
  50.5 0.8 %collective-permute-start.29 = (bf16[2,2,128,128]{3,2,1,0:T(8,128)(2,1)S(1)}, bf16[2,2,128,128]{3,2,1,0:T(8,128)(2,1)S(1)}, u32[]{:S(2)}, u32[]{:S(2)}) collective-permute-start(bf16[2,2,128,128]{3,2,1,0:T(8,128)(2,1)S(1)} %get-tuple-element.88), channel_id=1, source_target_pairs={{0,4},{1,5},{2,6},{3,7},{4,0},{5,1},{6,2},{7,3},{8,12},{9,13},{10,... | collective-permute-start | bytes 393224 | tf_op jit(solution)/shard_map/ppermute | solution.py:176
  51.3 1.4 %collective-permute-start.30 = (bf16[2,2,128,128]{3,2,1,0:T(8,128)(2,1)S(1)}, bf16[2,2,128,128]{3,2,1,0:T(8,128)(2,1)S(1)}, u32[]{:S(2)}, u32[]{:S(2)}) collective-permute-start(bf16[2,2,128,128]{3,2,1,0:T(8,128)(2,1)S(1)} %get-tuple-element.89), channel_id=1, source_target_pairs={{0,6},{1,7},{2,4},{3,5},{4,2},{5,3},{6,0},{7,1},{8,14},{9,15},{10,... | collective-permute-start | bytes 393224 | tf_op jit(solution)/shard_map/ppermute | solution.py:176
  52.9 1.9 %collective-permute-done.18.refs_3_ = bf16[2,2,128,128]{3,2,1,0:T(8,128)(2,1)S(1)} collective-permute-done((bf16[2,2,128,128]{3,2,1,0:T(8,128)(2,1)S(1)}, bf16[2,2,128,128]{3,2,1,0:T(8,128)(2,1)S(1)}, u32[]{:S(2)}, u32[]{:S(2)}) %collective-permute-start.18) | collective-permute-done | bytes 131104 | tf_op jit(solution)/shard_map/ppermute | solution.py:176
  55.0 1.2 %collective-permute-done.29.refs_2_ = bf16[2,2,128,128]{3,2,1,0:T(8,128)(2,1)S(1)} collective-permute-done((bf16[2,2,128,128]{3,2,1,0:T(8,128)(2,1)S(1)}, bf16[2,2,128,128]{3,2,1,0:T(8,128)(2,1)S(1)}, u32[]{:S(2)}, u32[]{:S(2)}) %collective-permute-start.29) | collective-permute-done | bytes 131104 | tf_op jit(solution)/shard_map/ppermute | solution.py:176
  56.1 1.4 %collective-permute-done.30.refs_3_ = bf16[2,2,128,128]{3,2,1,0:T(8,128)(2,1)S(1)} collective-permute-done((bf16[2,2,128,128]{3,2,1,0:T(8,128)(2,1)S(1)}, bf16[2,2,128,128]{3,2,1,0:T(8,128)(2,1)S(1)}, u32[]{:S(2)}, u32[]{:S(2)}) %collective-permute-start.30) | collective-permute-done | bytes 131104 | tf_op jit(solution)/shard_map/ppermute | solution.py:176
  57.7 0.4 partial.1
  58.1 0.9 %collective-permute-done.32.last = bf16[2,128,128]{2,1,0:T(8,128)(2,1)S(1)} collective-permute-done((bf16[2,128,128]{2,1,0:T(8,128)(2,1)S(1)}, bf16[2,128,128]{2,1,0:T(8,128)(2,1)S(1)}, u32[]{:S(2)}, u32[]{:S(2)}) %collective-permute-start.32) | collective-permute-done | bytes 65568 | tf_op jit(solution)/shard_map/ppermute | solution.py:176
  58.9 0.9 %final.1 = bf16[256,512]{1,0:T(8,128)(2,1)} custom-call(f32[256,512]{1,0:T(8,128)S(1)} %partial.1, bf16[2,128,128]{2,1,0:T(8,128)(2,1)S(1)} %collective-permute-done.32.last, bf16[512,512]{1,0:T(8,128)(2,1)S(1)} %copy-done.1), custom_call_target="tpu_custom_call" | custom-call | flops 1000000000 | bytes 10000000 | tf_op jit(solution)/shard_map/final/pallas_call | solution.py:162
  (41 shorter events, 1.5 us)
Async XLA Ops:
  0.0 10.1 %copy-start.2 = (s32[1,16,2]{1,2,0:T(2,128)S(1)}, s32[1,16,2]{1,2,0:T(2,128)}, u32[]{:S(2)}) copy-start(s32[1,16,2]{1,2,0:T(2,128)} %param.9) | copy-start | bytes 388
  0.0 1.4 %collective-permute-start = (s32[1,4]{1,0:T(1,128)}, s32[1,4]{1,0:T(1,128)S(1)}, u32[]{:S(2)}, u32[]{:S(2)}) collective-permute-start(s32[1,4]{1,0:T(1,128)} %param.11), channel_id=1, source_target_pairs={{0,1},{1,0},{2,3},{3,2},{4,5},{5,4},{6,7},{7,6},{8,9},{9,8},{10,11... | collective-permute-start | bytes 56 | tf_op jit(solution)/shard_map/ppermute | solution.py:176
  2.1 6.7 %collective-permute-start.1 = (bf16[256,512]{1,0:T(8,128)(2,1)}, bf16[256,512]{1,0:T(8,128)(2,1)S(1)}, u32[]{:S(2)}, u32[]{:S(2)}) collective-permute-start(bf16[256,512]{1,0:T(8,128)(2,1)} %own_hbm), channel_id=1, source_target_pairs={{0,1},{1,0},{2,3},{3,2},{4,5},{5,4},{6,7},{7,6},{8,9},{9,8},{10,11... | collective-permute-start | bytes 786440 | tf_op jit(solution)/shard_map/ppermute | solution.py:176
  2.4 16.1 %collective-permute-start.3 = (bf16[1,16,128,128]{3,2,1,0:T(8,128)(2,1)}, bf16[1,16,128,128]{3,2,1,0:T(8,128)(2,1)S(1)}, u32[]{:S(2)}, u32[]{:S(2)}) collective-permute-start(bf16[1,16,128,128]{3,2,1,0:T(8,128)(2,1)} %own_tiles), channel_id=1, source_target_pairs={{0,1},{1,0},{2,3},{3,2},{4,5},{5,4},{6,7},{7,6},{8,9},{9,8},{10,11... | collective-permute-start | bytes 1572872 | tf_op jit(solution)/shard_map/ppermute | solution.py:176
  3.2 7.2 %collective-permute-start.4 = (s32[2,4]{1,0:T(2,128)S(1)}, s32[2,4]{1,0:T(2,128)S(1)}, u32[]{:S(2)}, u32[]{:S(2)}) collective-permute-start(s32[2,4]{1,0:T(2,128)S(1)} %pad_add_fusion.refs_0_), channel_id=1, source_target_pairs={{0,16},{8,24},{16,0},{24,8},{1,17},{9,25},{17,1},{25,9},{2,18},{10... | collective-permute-start | bytes 104 | tf_op jit(solution)/shard_map/ppermute | solution.py:182
  7.2 5.4 %collective-permute-start.5 = (s32[2,4]{1,0:T(2,128)S(1)}, s32[2,4]{1,0:T(2,128)S(1)}, u32[]{:S(2)}, u32[]{:S(2)}) collective-permute-start(s32[2,4]{1,0:T(2,128)S(1)} %pad_add_fusion.refs_0_), channel_id=1, source_target_pairs={{0,24},{8,16},{16,8},{24,0},{1,25},{9,17},{17,9},{25,1},{2,26},{10... | collective-permute-start | bytes 104 | tf_op jit(solution)/shard_map/ppermute | solution.py:182
  8.5 4.0 %collective-permute-start.6 = (s32[2,4]{1,0:T(2,128)S(1)}, s32[2,4]{1,0:T(2,128)S(1)}, u32[]{:S(2)}, u32[]{:S(2)}) collective-permute-start(s32[2,4]{1,0:T(2,128)S(1)} %pad_add_fusion.refs_0_), channel_id=1, source_target_pairs={{0,8},{8,0},{16,24},{24,16},{1,9},{9,1},{17,25},{25,17},{2,10},{10... | collective-permute-start | bytes 104 | tf_op jit(solution)/shard_map/ppermute | solution.py:182
  10.1 9.2 %copy-start = (bf16[1,16,128,128]{3,2,1,0:T(8,128)(2,1)S(1)}, bf16[1,16,128,128]{3,2,1,0:T(8,128)(2,1)}, u32[]{:S(2)}) copy-start(bf16[1,16,128,128]{3,2,1,0:T(8,128)(2,1)} %own_tiles) | copy-start | bytes 1572868
  10.4 5.9 %collective-permute-start.2 = (s32[1,33]{1,0:T(1,128)S(1)}, s32[1,33]{1,0:T(1,128)S(1)}, u32[]{:S(2)}, u32[]{:S(2)}) collective-permute-start(s32[1,33]{1,0:T(1,128)S(1)} %pad_add_fusion.1.own_table), channel_id=1, source_target_pairs={{0,1},{1,0},{2,3},{3,2},{4,5},{5,4},{6,7},{7,6},{8,9},{9,8},{10,11... | collective-permute-start | bytes 404 | tf_op jit(solution)/shard_map/ppermute | solution.py:176
  12.8 7.5 %collective-permute-start.7 = (bf16[2,128,128]{2,1,0:T(8,128)(2,1)S(1)}, bf16[2,128,128]{2,1,0:T(8,128)(2,1)S(1)}, u32[]{:S(2)}, u32[]{:S(2)}) collective-permute-start(bf16[2,128,128]{2,1,0:T(8,128)(2,1)S(1)} %get-tuple-element.58), channel_id=1, source_target_pairs={{0,16},{8,24},{16,0},{24,8},{1,17},{9,25},{17,1},{25,9},{2,18},{10... | collective-permute-start | bytes 196616 | tf_op jit(solution)/shard_map/ppermute | solution.py:182
  14.1 6.9 %collective-permute-start.8 = (bf16[2,128,128]{2,1,0:T(8,128)(2,1)S(1)}, bf16[2,128,128]{2,1,0:T(8,128)(2,1)S(1)}, u32[]{:S(2)}, u32[]{:S(2)}) collective-permute-start(bf16[2,128,128]{2,1,0:T(8,128)(2,1)S(1)} %get-tuple-element.59), channel_id=1, source_target_pairs={{0,24},{8,16},{16,8},{24,0},{1,25},{9,17},{17,9},{25,1},{2,26},{10... | collective-permute-start | bytes 196616 | tf_op jit(solution)/shard_map/ppermute | solution.py:182
  15.0 6.1 %collective-permute-start.9 = (bf16[2,128,128]{2,1,0:T(8,128)(2,1)S(1)}, bf16[2,128,128]{2,1,0:T(8,128)(2,1)S(1)}, u32[]{:S(2)}, u32[]{:S(2)}) collective-permute-start(bf16[2,128,128]{2,1,0:T(8,128)(2,1)S(1)} %get-tuple-element.60), channel_id=1, source_target_pairs={{0,8},{8,0},{16,24},{24,16},{1,9},{9,1},{17,25},{25,17},{2,10},{10... | collective-permute-start | bytes 196616 | tf_op jit(solution)/shard_map/ppermute | solution.py:182
  16.3 9.5 %collective-permute-start.19 = (bf16[2,128,128]{2,1,0:T(8,128)(2,1)S(1)}, bf16[2,128,128]{2,1,0:T(8,128)(2,1)S(1)}, u32[]{:S(2)}, u32[]{:S(2)}) collective-permute-start(bf16[2,128,128]{2,1,0:T(8,128)(2,1)S(1)} %get-tuple-element.75), channel_id=1, source_target_pairs={{0,16},{8,24},{16,0},{24,8},{1,17},{9,25},{17,1},{25,9},{2,18},{10... | collective-permute-start | bytes 196616 | tf_op jit(solution)/shard_map/ppermute | solution.py:182
  18.5 9.8 %collective-permute-start.20 = (bf16[2,128,128]{2,1,0:T(8,128)(2,1)S(1)}, bf16[2,128,128]{2,1,0:T(8,128)(2,1)S(1)}, u32[]{:S(2)}, u32[]{:S(2)}) collective-permute-start(bf16[2,128,128]{2,1,0:T(8,128)(2,1)S(1)} %get-tuple-element.76), channel_id=1, source_target_pairs={{0,24},{8,16},{16,8},{24,0},{1,25},{9,17},{17,9},{25,1},{2,26},{10... | collective-permute-start | bytes 196616 | tf_op jit(solution)/shard_map/ppermute | solution.py:182
  20.3 8.0 %collective-permute-start.21 = (bf16[2,128,128]{2,1,0:T(8,128)(2,1)S(1)}, bf16[2,128,128]{2,1,0:T(8,128)(2,1)S(1)}, u32[]{:S(2)}, u32[]{:S(2)}) collective-permute-start(bf16[2,128,128]{2,1,0:T(8,128)(2,1)S(1)} %get-tuple-element.77), channel_id=1, source_target_pairs={{0,8},{8,0},{16,24},{24,16},{1,9},{9,1},{17,25},{25,17},{2,10},{10... | collective-permute-start | bytes 196616 | tf_op jit(solution)/shard_map/ppermute | solution.py:182
  21.8 8.3 %collective-permute-start.10 = (bf16[2,2,128,128]{3,2,1,0:T(8,128)(2,1)S(1)}, bf16[2,2,128,128]{3,2,1,0:T(8,128)(2,1)S(1)}, u32[]{:S(2)}, u32[]{:S(2)}) collective-permute-start(bf16[2,2,128,128]{3,2,1,0:T(8,128)(2,1)S(1)} %get-tuple-element.62), channel_id=1, source_target_pairs={{0,2},{1,3},{2,0},{3,1},{4,6},{5,7},{6,4},{7,5},{8,10},{9,11},{10,... | collective-permute-start | bytes 393224 | tf_op jit(solution)/shard_map/ppermute | solution.py:176
  23.3 9.4 %collective-permute-start.11 = (bf16[2,2,128,128]{3,2,1,0:T(8,128)(2,1)S(1)}, bf16[2,2,128,128]{3,2,1,0:T(8,128)(2,1)S(1)}, u32[]{:S(2)}, u32[]{:S(2)}) collective-permute-start(bf16[2,2,128,128]{3,2,1,0:T(8,128)(2,1)S(1)} %get-tuple-element.63), channel_id=1, source_target_pairs={{0,4},{1,5},{2,6},{3,7},{4,0},{5,1},{6,2},{7,3},{8,12},{9,13},{10,... | collective-permute-start | bytes 393224 | tf_op jit(solution)/shard_map/ppermute | solution.py:176
  25.8 7.4 %collective-permute-start.12 = (bf16[2,2,128,128]{3,2,1,0:T(8,128)(2,1)S(1)}, bf16[2,2,128,128]{3,2,1,0:T(8,128)(2,1)S(1)}, u32[]{:S(2)}, u32[]{:S(2)}) collective-permute-start(bf16[2,2,128,128]{3,2,1,0:T(8,128)(2,1)S(1)} %get-tuple-element.64), channel_id=1, source_target_pairs={{0,6},{1,7},{2,4},{3,5},{4,2},{5,3},{6,0},{7,1},{8,14},{9,15},{10,... | collective-permute-start | bytes 393224 | tf_op jit(solution)/shard_map/ppermute | solution.py:176
  29.0 8.8 %collective-permute-start.22 = (bf16[2,2,128,128]{3,2,1,0:T(8,128)(2,1)S(1)}, bf16[2,2,128,128]{3,2,1,0:T(8,128)(2,1)S(1)}, u32[]{:S(2)}, u32[]{:S(2)}) collective-permute-start(bf16[2,2,128,128]{3,2,1,0:T(8,128)(2,1)S(1)} %get-tuple-element.79), channel_id=1, source_target_pairs={{0,2},{1,3},{2,0},{3,1},{4,6},{5,7},{6,4},{7,5},{8,10},{9,11},{10,... | collective-permute-start | bytes 393224 | tf_op jit(solution)/shard_map/ppermute | solution.py:176
  29.6 8.2 %collective-permute-start.23 = (bf16[2,2,128,128]{3,2,1,0:T(8,128)(2,1)S(1)}, bf16[2,2,128,128]{3,2,1,0:T(8,128)(2,1)S(1)}, u32[]{:S(2)}, u32[]{:S(2)}) collective-permute-start(bf16[2,2,128,128]{3,2,1,0:T(8,128)(2,1)S(1)} %get-tuple-element.80), channel_id=1, source_target_pairs={{0,4},{1,5},{2,6},{3,7},{4,0},{5,1},{6,2},{7,3},{8,12},{9,13},{10,... | collective-permute-start | bytes 393224 | tf_op jit(solution)/shard_map/ppermute | solution.py:176
  30.1 7.7 %collective-permute-start.24 = (bf16[2,2,128,128]{3,2,1,0:T(8,128)(2,1)S(1)}, bf16[2,2,128,128]{3,2,1,0:T(8,128)(2,1)S(1)}, u32[]{:S(2)}, u32[]{:S(2)}) collective-permute-start(bf16[2,2,128,128]{3,2,1,0:T(8,128)(2,1)S(1)} %get-tuple-element.81), channel_id=1, source_target_pairs={{0,6},{1,7},{2,4},{3,5},{4,2},{5,3},{6,0},{7,1},{8,14},{9,15},{10,... | collective-permute-start | bytes 393224 | tf_op jit(solution)/shard_map/ppermute | solution.py:176
  33.4 9.0 %collective-permute-start.13 = (bf16[2,128,128]{2,1,0:T(8,128)(2,1)S(1)}, bf16[2,128,128]{2,1,0:T(8,128)(2,1)S(1)}, u32[]{:S(2)}, u32[]{:S(2)}) collective-permute-start(bf16[2,128,128]{2,1,0:T(8,128)(2,1)S(1)} %get-tuple-element.66), channel_id=1, source_target_pairs={{0,16},{8,24},{16,0},{24,8},{1,17},{9,25},{17,1},{25,9},{2,18},{10... | collective-permute-start | bytes 196616 | tf_op jit(solution)/shard_map/ppermute | solution.py:182
  37.1 6.2 %collective-permute-start.14 = (bf16[2,128,128]{2,1,0:T(8,128)(2,1)S(1)}, bf16[2,128,128]{2,1,0:T(8,128)(2,1)S(1)}, u32[]{:S(2)}, u32[]{:S(2)}) collective-permute-start(bf16[2,128,128]{2,1,0:T(8,128)(2,1)S(1)} %get-tuple-element.67), channel_id=1, source_target_pairs={{0,24},{8,16},{16,8},{24,0},{1,25},{9,17},{17,9},{25,1},{2,26},{10... | collective-permute-start | bytes 196616 | tf_op jit(solution)/shard_map/ppermute | solution.py:182
  37.8 5.9 %collective-permute-start.15 = (bf16[2,128,128]{2,1,0:T(8,128)(2,1)S(1)}, bf16[2,128,128]{2,1,0:T(8,128)(2,1)S(1)}, u32[]{:S(2)}, u32[]{:S(2)}) collective-permute-start(bf16[2,128,128]{2,1,0:T(8,128)(2,1)S(1)} %get-tuple-element.68), channel_id=1, source_target_pairs={{0,8},{8,0},{16,24},{24,16},{1,9},{9,1},{17,25},{25,17},{2,10},{10... | collective-permute-start | bytes 196616 | tf_op jit(solution)/shard_map/ppermute | solution.py:182
  38.0 9.1 %collective-permute-start.25 = (bf16[2,128,128]{2,1,0:T(8,128)(2,1)S(1)}, bf16[2,128,128]{2,1,0:T(8,128)(2,1)S(1)}, u32[]{:S(2)}, u32[]{:S(2)}) collective-permute-start(bf16[2,128,128]{2,1,0:T(8,128)(2,1)S(1)} %get-tuple-element.83), channel_id=1, source_target_pairs={{0,16},{8,24},{16,0},{24,8},{1,17},{9,25},{17,1},{25,9},{2,18},{10... | collective-permute-start | bytes 196616 | tf_op jit(solution)/shard_map/ppermute | solution.py:182
  41.7 6.7 %collective-permute-start.26 = (bf16[2,128,128]{2,1,0:T(8,128)(2,1)S(1)}, bf16[2,128,128]{2,1,0:T(8,128)(2,1)S(1)}, u32[]{:S(2)}, u32[]{:S(2)}) collective-permute-start(bf16[2,128,128]{2,1,0:T(8,128)(2,1)S(1)} %get-tuple-element.84), channel_id=1, source_target_pairs={{0,24},{8,16},{16,8},{24,0},{1,25},{9,17},{17,9},{25,1},{2,26},{10... | collective-permute-start | bytes 196616 | tf_op jit(solution)/shard_map/ppermute | solution.py:182
  42.4 6.0 %collective-permute-start.27 = (bf16[2,128,128]{2,1,0:T(8,128)(2,1)S(1)}, bf16[2,128,128]{2,1,0:T(8,128)(2,1)S(1)}, u32[]{:S(2)}, u32[]{:S(2)}) collective-permute-start(bf16[2,128,128]{2,1,0:T(8,128)(2,1)S(1)} %get-tuple-element.85), channel_id=1, source_target_pairs={{0,8},{8,0},{16,24},{24,16},{1,9},{9,1},{17,25},{25,17},{2,10},{10... | collective-permute-start | bytes 196616 | tf_op jit(solution)/shard_map/ppermute | solution.py:182
  44.4 6.9 %collective-permute-start.16 = (bf16[2,2,128,128]{3,2,1,0:T(8,128)(2,1)S(1)}, bf16[2,2,128,128]{3,2,1,0:T(8,128)(2,1)S(1)}, u32[]{:S(2)}, u32[]{:S(2)}) collective-permute-start(bf16[2,2,128,128]{3,2,1,0:T(8,128)(2,1)S(1)} %get-tuple-element.70), channel_id=1, source_target_pairs={{0,2},{1,3},{2,0},{3,1},{4,6},{5,7},{6,4},{7,5},{8,10},{9,11},{10,... | collective-permute-start | bytes 393224 | tf_op jit(solution)/shard_map/ppermute | solution.py:176
  46.2 6.7 %collective-permute-start.17 = (bf16[2,2,128,128]{3,2,1,0:T(8,128)(2,1)S(1)}, bf16[2,2,128,128]{3,2,1,0:T(8,128)(2,1)S(1)}, u32[]{:S(2)}, u32[]{:S(2)}) collective-permute-start(bf16[2,2,128,128]{3,2,1,0:T(8,128)(2,1)S(1)} %get-tuple-element.71), channel_id=1, source_target_pairs={{0,4},{1,5},{2,6},{3,7},{4,0},{5,1},{6,2},{7,3},{8,12},{9,13},{10,... | collective-permute-start | bytes 393224 | tf_op jit(solution)/shard_map/ppermute | solution.py:176
  47.0 7.8 %collective-permute-start.18 = (bf16[2,2,128,128]{3,2,1,0:T(8,128)(2,1)S(1)}, bf16[2,2,128,128]{3,2,1,0:T(8,128)(2,1)S(1)}, u32[]{:S(2)}, u32[]{:S(2)}) collective-permute-start(bf16[2,2,128,128]{3,2,1,0:T(8,128)(2,1)S(1)} %get-tuple-element.72), channel_id=1, source_target_pairs={{0,6},{1,7},{2,4},{3,5},{4,2},{5,3},{6,0},{7,1},{8,14},{9,15},{10,... | collective-permute-start | bytes 393224 | tf_op jit(solution)/shard_map/ppermute | solution.py:176
  49.1 5.8 %collective-permute-start.28 = (bf16[2,2,128,128]{3,2,1,0:T(8,128)(2,1)S(1)}, bf16[2,2,128,128]{3,2,1,0:T(8,128)(2,1)S(1)}, u32[]{:S(2)}, u32[]{:S(2)}) collective-permute-start(bf16[2,2,128,128]{3,2,1,0:T(8,128)(2,1)S(1)} %get-tuple-element.87), channel_id=1, source_target_pairs={{0,2},{1,3},{2,0},{3,1},{4,6},{5,7},{6,4},{7,5},{8,10},{9,11},{10,... | collective-permute-start | bytes 393224 | tf_op jit(solution)/shard_map/ppermute | solution.py:176
  50.5 5.6 %collective-permute-start.29 = (bf16[2,2,128,128]{3,2,1,0:T(8,128)(2,1)S(1)}, bf16[2,2,128,128]{3,2,1,0:T(8,128)(2,1)S(1)}, u32[]{:S(2)}, u32[]{:S(2)}) collective-permute-start(bf16[2,2,128,128]{3,2,1,0:T(8,128)(2,1)S(1)} %get-tuple-element.88), channel_id=1, source_target_pairs={{0,4},{1,5},{2,6},{3,7},{4,0},{5,1},{6,2},{7,3},{8,12},{9,13},{10,... | collective-permute-start | bytes 393224 | tf_op jit(solution)/shard_map/ppermute | solution.py:176
  51.3 6.2 %collective-permute-start.30 = (bf16[2,2,128,128]{3,2,1,0:T(8,128)(2,1)S(1)}, bf16[2,2,128,128]{3,2,1,0:T(8,128)(2,1)S(1)}, u32[]{:S(2)}, u32[]{:S(2)}) collective-permute-start(bf16[2,2,128,128]{3,2,1,0:T(8,128)(2,1)S(1)} %get-tuple-element.89), channel_id=1, source_target_pairs={{0,6},{1,7},{2,4},{3,5},{4,2},{5,3},{6,0},{7,1},{8,14},{9,15},{10,... | collective-permute-start | bytes 393224 | tf_op jit(solution)/shard_map/ppermute | solution.py:176
  54.9 2.8 %copy-start.1 = (bf16[512,512]{1,0:T(8,128)(2,1)S(1)}, bf16[512,512]{1,0:T(8,128)(2,1)}, u32[]{:S(2)}) copy-start(bf16[512,512]{1,0:T(8,128)(2,1)} %weight.1) | copy-start | bytes 1572868
  54.9 2.8 %collective-permute-start.31 = (bf16[2,128,128]{2,1,0:T(8,128)(2,1)S(1)}, bf16[2,128,128]{2,1,0:T(8,128)(2,1)S(1)}, u32[]{:S(2)}, u32[]{:S(2)}) collective-permute-start(bf16[2,128,128]{2,1,0:T(8,128)(2,1)S(1)} %get-tuple-element.91), channel_id=1, source_target_pairs={{0,1},{1,0},{2,3},{3,2},{4,5},{5,4},{6,7},{7,6},{8,9},{9,8},{10,11... | collective-permute-start | bytes 196616 | tf_op jit(solution)/shard_map/ppermute | solution.py:176
  57.6 1.3 %collective-permute-start.32 = (bf16[2,128,128]{2,1,0:T(8,128)(2,1)S(1)}, bf16[2,128,128]{2,1,0:T(8,128)(2,1)S(1)}, u32[]{:S(2)}, u32[]{:S(2)}) collective-permute-start(bf16[2,128,128]{2,1,0:T(8,128)(2,1)S(1)} %get-tuple-element.92), channel_id=1, source_target_pairs={{0,1},{1,0},{2,3},{3,2},{4,5},{5,4},{6,7},{7,6},{8,9},{9,8},{10,11... | collective-permute-start | bytes 196616 | tf_op jit(solution)/shard_map/ppermute | solution.py:176

commit v6 on v5

--- a/solution.py
+++ b/solution.py
@@ -56,12 +56,12 @@
         out[r] = product.reshape(out.shape[1:])
 
 
-def distances(rows):
-    return [0] + sorted(range(1, rows), key=lambda s: s ^ rows // 2)
-
-
-def by_distance(items):
-    order = distances(len(items))
+def distances(rows, layer=0):
+    return [0] + sorted(range(1, rows), key=lambda s: (s != rows // 2, s) if layer else s ^ rows // 2)
+
+
+def by_distance(items, layer=0):
+    order = distances(len(items), layer)
     return [items[order.index(s)] for s in range(len(items))]
 
 
@@ -82,14 +82,14 @@
                 outs[j * rows + s][r] = block[:, j * columns : (j + 1) * columns]
 
 
-def multiply_kernel(*refs):
+def multiply_kernel(*refs, layer):
     picks, dense = refs[:2]
     _, owners, tile, depth = dense.shape
     rows = depth // tile
     pieces, outs = refs[2 : 2 + rows], refs[2 + rows :]
     chips = owners // 2
     columns = outs[0].shape[-1]
-    operands = [jnp.concatenate([piece[r] for piece in by_distance(pieces)], axis=0) for r in range(2)]
+    operands = [jnp.concatenate([piece[r] for piece in by_distance(pieces, layer)], axis=0) for r in range(2)]
     products = [jnp.dot(dense[r].reshape(owners * tile, depth), operands[r], preferred_element_type=FULL) for r in range(2)]
     for e in range(owners):
         own, peer = (product[e * tile : (e + 1) * tile] for product in products)
@@ -212,13 +212,13 @@
     )
     columns = width // CHUNKS
 
-    def to_readers(pieces):
-        return [pieces[0]] + [by_row(pieces[s], s) for s in distances(row_count)[1:]]
-
-    def to_owners(pieces):
+    def to_readers(pieces, layer):
+        return [pieces[0]] + [by_row(pieces[s], s) for s in distances(row_count, layer)[1:]]
+
+    def to_owners(pieces, layer):
         chunks = pieces[0].shape[-1] // columns
         parts = call(
-            multiply_kernel,
+            functools.partial(multiply_kernel, layer=layer),
             [shape(2, 2, tile, columns)] * (chips * chunks),
             [picks, dense, *pieces],
             name="multiply",
@@ -232,8 +232,8 @@
         [*needs, projected],
         name="select",
     )
-    panels = [to_readers(selected[j * row_count : (j + 1) * row_count]) for j in range(CHUNKS)]
-    arrived = [parts for panel in panels for parts in to_owners(panel)]
+    panels = [to_readers(selected[j * row_count : (j + 1) * row_count], 0) for j in range(CHUNKS)]
+    arrived = [parts for panel in panels for parts in to_owners(panel, 0)]
     panels = []
     for parts in arrived:
         selected = call(
@@ -242,8 +242,8 @@
             [*needs, *parts],
             name="hidden",
         )
-        panels.append(to_readers(selected))
-    arrived = [to_owners(panel)[0] for panel in panels]
+        panels.append(to_readers(selected, 1))
+    arrived = [to_owners(panel, 1)[0] for panel in panels]
     mine, theirs = [], []
     for parts in arrived:
         own, other = call(mixed_kernel, [shape(2, tile, columns)] * 2, parts, name="mixed")

time: 60 us -> 59 us (0.983)
  waiting for transfers between devices: 11.8 us -> 10.2 us
  Pallas kernels: 6.95 us -> 7.58 us
    ppermute x15, waiting for transfers between devices: 4.59 us -> 3.46 us  [by_row(): return lax.ppermute(x, 'row', [(i, i ^ s) for i in range(row_count)])]
    pallas_call x13, Pallas kernels: 6.95 us -> 7.58 us  [call(): pl.pallas_call(kernel, in_specs=in_specs or [VMEM] * len(args), out_specs...]
  transfers between devices with their start and end apart: 33 -> 33, of which waited for: 14 -> 11; matrix products, arithmetic and copies ran while one was open for 0% -> 0% of each run, Pallas kernels for 10% -> 11%
where the time goes in v6:
time: 59 us; the launch traced here: 58.8 us
  starting transfers between devices  39.3 us (67%)
  waiting for transfers between devices  10.2 us (17%)
  Pallas kernels  7.58 us (13%)
  between operations  0.86 us (1%)
  other arithmetic  0.74 us (1%)
    ppermute x15, starting transfers between devices, by_row(): return lax.ppermute(x, 'row', [(i, i ^ s) for i in range(row_count)])  22 us
    ppermute x18, starting transfers between devices, by_col(): lax.ppermute(x, 'col', [(i, i ^ masks[i % 2]) for i in range(col_count)])  17.3 us
    pallas_call x13, Pallas kernels, call(): pl.pallas_call(kernel, in_specs=in_specs or [VMEM] * len(args), out_specs...  7.58 us
    ppermute x18, waiting for transfers between devices, by_col(): lax.ppermute(x, 'col', [(i, i ^ masks[i % 2]) for i in range(col_count)])  6.71 us
    ppermute x15, waiting for transfers between devices, by_row(): return lax.ppermute(x, 'row', [(i, i ^ s) for i in range(row_count)])  3.46 us
  transfers between devices with their start and end apart: 33, of which 11 were waited for; matrix products, arithmetic and copies ran while one was open for 0% of the time, Pallas kernels for 11%

profile of v6, /device:TPU:0, one launch (start us, length us, event | category | flops | bytes accessed | tf_op | source)
XLA Modules:
  0.0 58.8 jit_solution(2959394386392130872)
XLA Ops:
  0.0 0.5 collective-permute-start
  0.5 1.0 %collective-permute-done = s32[1,4]{1,0:T(1,128)S(1)} collective-permute-done((s32[1,4]{1,0:T(1,128)}, s32[1,4]{1,0:T(1,128)S(1)}, u32[]{:S(2)}, u32[]{:S(2)}) %collective-permute-start) | collective-permute-done | bytes 48 | tf_op jit(solution)/shard_map/ppermute | solution.py:176
  1.4 0.7 %pad_add_fusion.refs_0_ = s32[2,4]{1,0:T(2,128)S(1)} fusion(s32[1,4]{1,0:T(1,128)S(1)} %collective-permute-done, s32[1,4]{1,0:T(1,128)} %param.11), kind=kLoop, calls=%fused_computation | loop fusion | flops 8 | bytes 64 | tf_op jit(solution)/shard_map/concatenate | solution.py:187
  2.1 0.3 collective-permute-start.1
  2.4 0.2 collective-permute-start.3
  3.2 4.0 %collective-permute-start.4 = (s32[2,4]{1,0:T(2,128)S(1)}, s32[2,4]{1,0:T(2,128)S(1)}, u32[]{:S(2)}, u32[]{:S(2)}) collective-permute-start(s32[2,4]{1,0:T(2,128)S(1)} %pad_add_fusion.refs_0_), channel_id=1, source_target_pairs={{0,16},{8,24},{16,0},{24,8},{1,17},{9,25},{17,1},{25,9},{2,18},{10... | collective-permute-start | bytes 104 | tf_op jit(solution)/shard_map/ppermute | solution.py:182
  7.2 1.3 %collective-permute-start.5 = (s32[2,4]{1,0:T(2,128)S(1)}, s32[2,4]{1,0:T(2,128)S(1)}, u32[]{:S(2)}, u32[]{:S(2)}) collective-permute-start(s32[2,4]{1,0:T(2,128)S(1)} %pad_add_fusion.refs_0_), channel_id=1, source_target_pairs={{0,24},{8,16},{16,8},{24,0},{1,25},{9,17},{17,9},{25,1},{2,26},{10... | collective-permute-start | bytes 104 | tf_op jit(solution)/shard_map/ppermute | solution.py:182
  8.5 0.2 collective-permute-start.6
  8.8 1.4 %project.1.refs_4_ = bf16[2,2,128,256]{3,2,1,0:T(8,128)(2,1)S(1)} custom-call(bf16[256,512]{1,0:T(8,128)(2,1)} %own_hbm, bf16[256,512]{1,0:T(8,128)(2,1)S(1)} %collective-permute-done.1.peer_hbm, bf16[512,512]{1,0:T(8,128)(2,1)} %weight_hbm.1), custom_call_target="tpu_custom_call" | custom-call | flops 1000000000 | bytes 10000000 | tf_op jit(solution)/shard_map/project/pallas_call | solution.py:162
  10.4 2.1 %collective-permute-done.5.refs_2_ = s32[2,4]{1,0:T(2,128)S(1)} collective-permute-done((s32[2,4]{1,0:T(2,128)S(1)}, s32[2,4]{1,0:T(2,128)S(1)}, u32[]{:S(2)}, u32[]{:S(2)}) %collective-permute-start.5) | collective-permute-done | bytes 64 | tf_op jit(solution)/shard_map/ppermute | solution.py:182
  12.6 0.2 select.1
  12.8 1.3 %collective-permute-start.7 = (bf16[2,128,128]{2,1,0:T(8,128)(2,1)S(1)}, bf16[2,128,128]{2,1,0:T(8,128)(2,1)S(1)}, u32[]{:S(2)}, u32[]{:S(2)}) collective-permute-start(bf16[2,128,128]{2,1,0:T(8,128)(2,1)S(1)} %get-tuple-element.58), channel_id=1, source_target_pairs={{0,16},{8,24},{16,0},{24,8},{1,17},{9,25},{17,1},{25,9},{2,18},{10... | collective-permute-start | bytes 196616 | tf_op jit(solution)/shard_map/ppermute | solution.py:182
  14.1 0.9 %collective-permute-start.8 = (bf16[2,128,128]{2,1,0:T(8,128)(2,1)S(1)}, bf16[2,128,128]{2,1,0:T(8,128)(2,1)S(1)}, u32[]{:S(2)}, u32[]{:S(2)}) collective-permute-start(bf16[2,128,128]{2,1,0:T(8,128)(2,1)S(1)} %get-tuple-element.59), channel_id=1, source_target_pairs={{0,24},{8,16},{16,8},{24,0},{1,25},{9,17},{17,9},{25,1},{2,26},{10... | collective-permute-start | bytes 196616 | tf_op jit(solution)/shard_map/ppermute | solution.py:182
  15.0 1.3 %collective-permute-start.9 = (bf16[2,128,128]{2,1,0:T(8,128)(2,1)S(1)}, bf16[2,128,128]{2,1,0:T(8,128)(2,1)S(1)}, u32[]{:S(2)}, u32[]{:S(2)}) collective-permute-start(bf16[2,128,128]{2,1,0:T(8,128)(2,1)S(1)} %get-tuple-element.60), channel_id=1, source_target_pairs={{0,8},{8,0},{16,24},{24,16},{1,9},{9,1},{17,25},{25,17},{2,10},{10... | collective-permute-start | bytes 196616 | tf_op jit(solution)/shard_map/ppermute | solution.py:182
  16.3 2.1 %collective-permute-start.19 = (bf16[2,128,128]{2,1,0:T(8,128)(2,1)S(1)}, bf16[2,128,128]{2,1,0:T(8,128)(2,1)S(1)}, u32[]{:S(2)}, u32[]{:S(2)}) collective-permute-start(bf16[2,128,128]{2,1,0:T(8,128)(2,1)S(1)} %get-tuple-element.75), channel_id=1, source_target_pairs={{0,16},{8,24},{16,0},{24,8},{1,17},{9,25},{17,1},{25,9},{2,18},{10... | collective-permute-start | bytes 196616 | tf_op jit(solution)/shard_map/ppermute | solution.py:182
  18.5 0.9 %collective-permute-start.20 = (bf16[2,128,128]{2,1,0:T(8,128)(2,1)S(1)}, bf16[2,128,128]{2,1,0:T(8,128)(2,1)S(1)}, u32[]{:S(2)}, u32[]{:S(2)}) collective-permute-start(bf16[2,128,128]{2,1,0:T(8,128)(2,1)S(1)} %get-tuple-element.76), channel_id=1, source_target_pairs={{0,24},{8,16},{16,8},{24,0},{1,25},{9,17},{17,9},{25,1},{2,26},{10... | collective-permute-start | bytes 196616 | tf_op jit(solution)/shard_map/ppermute | solution.py:182
  19.4 1.5 %build.1 = (bf16[2,8,128,512]{3,2,1,0:T(8,128)(2,1)S(1)}, s32[16,1,128]{2,1,0:T(1,128)S(1)}) custom-call(s32[1,33]{1,0:T(1,128)S(1)} %pad_add_fusion.1.own_table, s32[1,33]{1,0:T(1,128)S(1)} %collective-permute-done.2.peer_table, bf16[1,16,128,128]{3,2,1,0:T(8,128)(2,1)S(1)} %copy-done, bf16[1,16,128,128]{3,2,1,0:T(8,128)(2,1)S(1)} %collective-permute-done.3.peer_tiles), custom_call_target="tpu_custom_call" | custom-call | flops 1000000000 | bytes 10000000 | tf_op jit(solution)/shard_map/build/pallas_call | solution.py:162
  21.1 0.7 %multiply.4 = (bf16[2,2,128,128]{3,2,1,0:T(8,128)(2,1)S(1)}, bf16[2,2,128,128]{3,2,1,0:T(8,128)(2,1)S(1)}, bf16[2,2,128,128]{3,2,1,0:T(8,128)(2,1)S(1)}, bf16[2,2,128,128]{3,2,1,0:T(8,128)(2,1)S(1)}) custom-call(s32[16,1,128]{2,1,0:T(1,128)S(1)} %get-tuple-element.53.refs_0_, bf16[2,8,128,512]{3,2,1,0:T(8,128)(2,1)S(1)} %get-tuple-element.54.refs_1_, ...), custom_call_target="tpu_custom_call" | custom-call | flops 1000000000 | bytes 10000000 | tf_op jit(solution)/shard_map/multiply/pallas_call | solution.py:162
  21.8 1.6 %collective-permute-start.10 = (bf16[2,2,128,128]{3,2,1,0:T(8,128)(2,1)S(1)}, bf16[2,2,128,128]{3,2,1,0:T(8,128)(2,1)S(1)}, u32[]{:S(2)}, u32[]{:S(2)}) collective-permute-start(bf16[2,2,128,128]{3,2,1,0:T(8,128)(2,1)S(1)} %get-tuple-element.62), channel_id=1, source_target_pairs={{0,2},{1,3},{2,0},{3,1},{4,6},{5,7},{6,4},{7,5},{8,10},{9,11},{10,... | collective-permute-start | bytes 393224 | tf_op jit(solution)/shard_map/ppermute | solution.py:176
  23.3 1.5 %collective-permute-start.11 = (bf16[2,2,128,128]{3,2,1,0:T(8,128)(2,1)S(1)}, bf16[2,2,128,128]{3,2,1,0:T(8,128)(2,1)S(1)}, u32[]{:S(2)}, u32[]{:S(2)}) collective-permute-start(bf16[2,2,128,128]{3,2,1,0:T(8,128)(2,1)S(1)} %get-tuple-element.63), channel_id=1, source_target_pairs={{0,4},{1,5},{2,6},{3,7},{4,0},{5,1},{6,2},{7,3},{8,12},{9,13},{10,... | collective-permute-start | bytes 393224 | tf_op jit(solution)/shard_map/ppermute | solution.py:176
  24.9 0.9 %collective-permute-done.19.refs_3_ = bf16[2,128,128]{2,1,0:T(8,128)(2,1)S(1)} collective-permute-done((bf16[2,128,128]{2,1,0:T(8,128)(2,1)S(1)}, bf16[2,128,128]{2,1,0:T(8,128)(2,1)S(1)}, u32[]{:S(2)}, u32[]{:S(2)}) %collective-permute-start.19) | collective-permute-done | bytes 65568 | tf_op jit(solution)/shard_map/ppermute | solution.py:182
  25.8 2.4 %collective-permute-start.12 = (bf16[2,2,128,128]{3,2,1,0:T(8,128)(2,1)S(1)}, bf16[2,2,128,128]{3,2,1,0:T(8,128)(2,1)S(1)}, u32[]{:S(2)}, u32[]{:S(2)}) collective-permute-start(bf16[2,2,128,128]{3,2,1,0:T(8,128)(2,1)S(1)} %get-tuple-element.64), channel_id=1, source_target_pairs={{0,6},{1,7},{2,4},{3,5},{4,2},{5,3},{6,0},{7,1},{8,14},{9,15},{10,... | collective-permute-start | bytes 393224 | tf_op jit(solution)/shard_map/ppermute | solution.py:176
  28.3 0.7 %multiply.6 = (bf16[2,2,128,128]{3,2,1,0:T(8,128)(2,1)S(1)}, bf16[2,2,128,128]{3,2,1,0:T(8,128)(2,1)S(1)}, bf16[2,2,128,128]{3,2,1,0:T(8,128)(2,1)S(1)}, bf16[2,2,128,128]{3,2,1,0:T(8,128)(2,1)S(1)}) custom-call(s32[16,1,128]{2,1,0:T(1,128)S(1)} %get-tuple-element.53.refs_0_, bf16[2,8,128,512]{3,2,1,0:T(8,128)(2,1)S(1)} %get-tuple-element.54.refs_1_, ...), custom_call_target="tpu_custom_call" | custom-call | flops 1000000000 | bytes 10000000 | tf_op jit(solution)/shard_map/multiply/pallas_call | solution.py:162
  29.0 0.6 %collective-permute-start.22 = (bf16[2,2,128,128]{3,2,1,0:T(8,128)(2,1)S(1)}, bf16[2,2,128,128]{3,2,1,0:T(8,128)(2,1)S(1)}, u32[]{:S(2)}, u32[]{:S(2)}) collective-permute-start(bf16[2,2,128,128]{3,2,1,0:T(8,128)(2,1)S(1)} %get-tuple-element.79), channel_id=1, source_target_pairs={{0,2},{1,3},{2,0},{3,1},{4,6},{5,7},{6,4},{7,5},{8,10},{9,11},{10,... | collective-permute-start | bytes 393224 | tf_op jit(solution)/shard_map/ppermute | solution.py:176
  29.6 0.5 collective-permute-start.23
  30.1 2.4 %collective-permute-start.24 = (bf16[2,2,128,128]{3,2,1,0:T(8,128)(2,1)S(1)}, bf16[2,2,128,128]{3,2,1,0:T(8,128)(2,1)S(1)}, u32[]{:S(2)}, u32[]{:S(2)}) collective-permute-start(bf16[2,2,128,128]{3,2,1,0:T(8,128)(2,1)S(1)} %get-tuple-element.81), channel_id=1, source_target_pairs={{0,6},{1,7},{2,4},{3,5},{4,2},{5,3},{6,0},{7,1},{8,14},{9,15},{10,... | collective-permute-start | bytes 393224 | tf_op jit(solution)/shard_map/ppermute | solution.py:176
  32.5 0.2 collective-permute-done.11.refs_6_
  32.8 0.5 collective-permute-done.12.refs_7_
  33.4 3.8 %collective-permute-start.13 = (bf16[2,128,128]{2,1,0:T(8,128)(2,1)S(1)}, bf16[2,128,128]{2,1,0:T(8,128)(2,1)S(1)}, u32[]{:S(2)}, u32[]{:S(2)}) collective-permute-start(bf16[2,128,128]{2,1,0:T(8,128)(2,1)S(1)} %get-tuple-element.66), channel_id=1, source_target_pairs={{0,16},{8,24},{16,0},{24,8},{1,17},{9,25},{17,1},{25,9},{2,18},{10... | collective-permute-start | bytes 196616 | tf_op jit(solution)/shard_map/ppermute | solution.py:182
  37.1 1.5 %collective-permute-start.15 = (bf16[2,128,128]{2,1,0:T(8,128)(2,1)S(1)}, bf16[2,128,128]{2,1,0:T(8,128)(2,1)S(1)}, u32[]{:S(2)}, u32[]{:S(2)}) collective-permute-start(bf16[2,128,128]{2,1,0:T(8,128)(2,1)S(1)} %get-tuple-element.68), channel_id=1, source_target_pairs={{0,24},{8,16},{16,8},{24,0},{1,25},{9,17},{17,9},{25,1},{2,26},{10... | collective-permute-start | bytes 196616 | tf_op jit(solution)/shard_map/ppermute | solution.py:182
  38.8 2.0 %collective-permute-start.25 = (bf16[2,128,128]{2,1,0:T(8,128)(2,1)S(1)}, bf16[2,128,128]{2,1,0:T(8,128)(2,1)S(1)}, u32[]{:S(2)}, u32[]{:S(2)}) collective-permute-start(bf16[2,128,128]{2,1,0:T(8,128)(2,1)S(1)} %get-tuple-element.83), channel_id=1, source_target_pairs={{0,16},{8,24},{16,0},{24,8},{1,17},{9,25},{17,1},{25,9},{2,18},{10... | collective-permute-start | bytes 196616 | tf_op jit(solution)/shard_map/ppermute | solution.py:182
  40.8 0.9 %collective-permute-start.26 = (bf16[2,128,128]{2,1,0:T(8,128)(2,1)S(1)}, bf16[2,128,128]{2,1,0:T(8,128)(2,1)S(1)}, u32[]{:S(2)}, u32[]{:S(2)}) collective-permute-start(bf16[2,128,128]{2,1,0:T(8,128)(2,1)S(1)} %get-tuple-element.84), channel_id=1, source_target_pairs={{0,8},{8,0},{16,24},{24,16},{1,9},{9,1},{17,25},{25,17},{2,10},{10... | collective-permute-start | bytes 196616 | tf_op jit(solution)/shard_map/ppermute | solution.py:182
  41.7 1.5 %collective-permute-start.27 = (bf16[2,128,128]{2,1,0:T(8,128)(2,1)S(1)}, bf16[2,128,128]{2,1,0:T(8,128)(2,1)S(1)}, u32[]{:S(2)}, u32[]{:S(2)}) collective-permute-start(bf16[2,128,128]{2,1,0:T(8,128)(2,1)S(1)} %get-tuple-element.85), channel_id=1, source_target_pairs={{0,24},{8,16},{16,8},{24,0},{1,25},{9,17},{17,9},{25,1},{2,26},{10... | collective-permute-start | bytes 196616 | tf_op jit(solution)/shard_map/ppermute | solution.py:182
  43.3 0.3 collective-permute-done.15.refs_5_
  43.6 0.7 %multiply.5 = (bf16[2,2,128,128]{3,2,1,0:T(8,128)(2,1)S(1)}, bf16[2,2,128,128]{3,2,1,0:T(8,128)(2,1)S(1)}, bf16[2,2,128,128]{3,2,1,0:T(8,128)(2,1)S(1)}, bf16[2,2,128,128]{3,2,1,0:T(8,128)(2,1)S(1)}) custom-call(s32[16,1,128]{2,1,0:T(1,128)S(1)} %get-tuple-element.53.refs_0_, bf16[2,8,128,512]{3,2,1,0:T(8,128)(2,1)S(1)} %get-tuple-element.54.refs_1_, ...), custom_call_target="tpu_custom_call" | custom-call | flops 1000000000 | bytes 10000000 | tf_op jit(solution)/shard_map/multiply/pallas_call | solution.py:162
  44.3 1.1 %collective-permute-start.16 = (bf16[2,2,128,128]{3,2,1,0:T(8,128)(2,1)S(1)}, bf16[2,2,128,128]{3,2,1,0:T(8,128)(2,1)S(1)}, u32[]{:S(2)}, u32[]{:S(2)}) collective-permute-start(bf16[2,2,128,128]{3,2,1,0:T(8,128)(2,1)S(1)} %get-tuple-element.70), channel_id=1, source_target_pairs={{0,2},{1,3},{2,0},{3,1},{4,6},{5,7},{6,4},{7,5},{8,10},{9,11},{10,... | collective-permute-start | bytes 393224 | tf_op jit(solution)/shard_map/ppermute | solution.py:176
  45.4 0.8 %collective-permute-start.17 = (bf16[2,2,128,128]{3,2,1,0:T(8,128)(2,1)S(1)}, bf16[2,2,128,128]{3,2,1,0:T(8,128)(2,1)S(1)}, u32[]{:S(2)}, u32[]{:S(2)}) collective-permute-start(bf16[2,2,128,128]{3,2,1,0:T(8,128)(2,1)S(1)} %get-tuple-element.71), channel_id=1, source_target_pairs={{0,4},{1,5},{2,6},{3,7},{4,0},{5,1},{6,2},{7,3},{8,12},{9,13},{10,... | collective-permute-start | bytes 393224 | tf_op jit(solution)/shard_map/ppermute | solution.py:176
  46.2 1.7 %collective-permute-start.18 = (bf16[2,2,128,128]{3,2,1,0:T(8,128)(2,1)S(1)}, bf16[2,2,128,128]{3,2,1,0:T(8,128)(2,1)S(1)}, u32[]{:S(2)}, u32[]{:S(2)}) collective-permute-start(bf16[2,2,128,128]{3,2,1,0:T(8,128)(2,1)S(1)} %get-tuple-element.72), channel_id=1, source_target_pairs={{0,6},{1,7},{2,4},{3,5},{4,2},{5,3},{6,0},{7,1},{8,14},{9,15},{10,... | collective-permute-start | bytes 393224 | tf_op jit(solution)/shard_map/ppermute | solution.py:176
  47.9 0.7 %multiply.7 = (bf16[2,2,128,128]{3,2,1,0:T(8,128)(2,1)S(1)}, bf16[2,2,128,128]{3,2,1,0:T(8,128)(2,1)S(1)}, bf16[2,2,128,128]{3,2,1,0:T(8,128)(2,1)S(1)}, bf16[2,2,128,128]{3,2,1,0:T(8,128)(2,1)S(1)}) custom-call(s32[16,1,128]{2,1,0:T(1,128)S(1)} %get-tuple-element.53.refs_0_, bf16[2,8,128,512]{3,2,1,0:T(8,128)(2,1)S(1)} %get-tuple-element.54.refs_1_, ...), custom_call_target="tpu_custom_call" | custom-call | flops 1000000000 | bytes 10000000 | tf_op jit(solution)/shard_map/multiply/pallas_call | solution.py:162
  48.6 1.3 %collective-permute-start.28 = (bf16[2,2,128,128]{3,2,1,0:T(8,128)(2,1)S(1)}, bf16[2,2,128,128]{3,2,1,0:T(8,128)(2,1)S(1)}, u32[]{:S(2)}, u32[]{:S(2)}) collective-permute-start(bf16[2,2,128,128]{3,2,1,0:T(8,128)(2,1)S(1)} %get-tuple-element.87), channel_id=1, source_target_pairs={{0,2},{1,3},{2,0},{3,1},{4,6},{5,7},{6,4},{7,5},{8,10},{9,11},{10,... | collective-permute-start | bytes 393224 | tf_op jit(solution)/shard_map/ppermute | solution.py:176
  49.9 0.7 %collective-permute-start.29 = (bf16[2,2,128,128]{3,2,1,0:T(8,128)(2,1)S(1)}, bf16[2,2,128,128]{3,2,1,0:T(8,128)(2,1)S(1)}, u32[]{:S(2)}, u32[]{:S(2)}) collective-permute-start(bf16[2,2,128,128]{3,2,1,0:T(8,128)(2,1)S(1)} %get-tuple-element.88), channel_id=1, source_target_pairs={{0,4},{1,5},{2,6},{3,7},{4,0},{5,1},{6,2},{7,3},{8,12},{9,13},{10,... | collective-permute-start | bytes 393224 | tf_op jit(solution)/shard_map/ppermute | solution.py:176
  50.6 1.5 %collective-permute-start.30 = (bf16[2,2,128,128]{3,2,1,0:T(8,128)(2,1)S(1)}, bf16[2,2,128,128]{3,2,1,0:T(8,128)(2,1)S(1)}, u32[]{:S(2)}, u32[]{:S(2)}) collective-permute-start(bf16[2,2,128,128]{3,2,1,0:T(8,128)(2,1)S(1)} %get-tuple-element.89), channel_id=1, source_target_pairs={{0,6},{1,7},{2,4},{3,5},{4,2},{5,3},{6,0},{7,1},{8,14},{9,15},{10,... | collective-permute-start | bytes 393224 | tf_op jit(solution)/shard_map/ppermute | solution.py:176
  52.2 1.4 %collective-permute-done.18.refs_3_ = bf16[2,2,128,128]{3,2,1,0:T(8,128)(2,1)S(1)} collective-permute-done((bf16[2,2,128,128]{3,2,1,0:T(8,128)(2,1)S(1)}, bf16[2,2,128,128]{3,2,1,0:T(8,128)(2,1)S(1)}, u32[]{:S(2)}, u32[]{:S(2)}) %collective-permute-start.18) | collective-permute-done | bytes 131104 | tf_op jit(solution)/shard_map/ppermute | solution.py:176
  53.8 1.2 %collective-permute-done.29.refs_2_ = bf16[2,2,128,128]{3,2,1,0:T(8,128)(2,1)S(1)} collective-permute-done((bf16[2,2,128,128]{3,2,1,0:T(8,128)(2,1)S(1)}, bf16[2,2,128,128]{3,2,1,0:T(8,128)(2,1)S(1)}, u32[]{:S(2)}, u32[]{:S(2)}) %collective-permute-start.29) | collective-permute-done | bytes 131104 | tf_op jit(solution)/shard_map/ppermute | solution.py:176
  55.0 1.5 %collective-permute-done.30.refs_3_ = bf16[2,2,128,128]{3,2,1,0:T(8,128)(2,1)S(1)} collective-permute-done((bf16[2,2,128,128]{3,2,1,0:T(8,128)(2,1)S(1)}, bf16[2,2,128,128]{3,2,1,0:T(8,128)(2,1)S(1)}, u32[]{:S(2)}, u32[]{:S(2)}) %collective-permute-start.30) | collective-permute-done | bytes 131104 | tf_op jit(solution)/shard_map/ppermute | solution.py:176
  56.7 0.4 partial.1
  57.0 0.9 %collective-permute-done.32.last = bf16[2,128,128]{2,1,0:T(8,128)(2,1)S(1)} collective-permute-done((bf16[2,128,128]{2,1,0:T(8,128)(2,1)S(1)}, bf16[2,128,128]{2,1,0:T(8,128)(2,1)S(1)}, u32[]{:S(2)}, u32[]{:S(2)}) %collective-permute-start.32) | collective-permute-done | bytes 65568 | tf_op jit(solution)/shard_map/ppermute | solution.py:176
  57.9 0.9 %final.1 = bf16[256,512]{1,0:T(8,128)(2,1)} custom-call(f32[256,512]{1,0:T(8,128)S(1)} %partial.1, bf16[2,128,128]{2,1,0:T(8,128)(2,1)S(1)} %collective-permute-done.32.last, bf16[512,512]{1,0:T(8,128)(2,1)S(1)} %copy-done.1), custom_call_target="tpu_custom_call" | custom-call | flops 1000000000 | bytes 10000000 | tf_op jit(solution)/shard_map/final/pallas_call | solution.py:162
  (41 shorter events, 1.0 us)
Async XLA Ops:
  0.0 10.1 %copy-start.2 = (s32[1,16,2]{1,2,0:T(2,128)S(1)}, s32[1,16,2]{1,2,0:T(2,128)}, u32[]{:S(2)}) copy-start(s32[1,16,2]{1,2,0:T(2,128)} %param.9) | copy-start | bytes 388
  0.0 1.4 %collective-permute-start = (s32[1,4]{1,0:T(1,128)}, s32[1,4]{1,0:T(1,128)S(1)}, u32[]{:S(2)}, u32[]{:S(2)}) collective-permute-start(s32[1,4]{1,0:T(1,128)} %param.11), channel_id=1, source_target_pairs={{0,1},{1,0},{2,3},{3,2},{4,5},{5,4},{6,7},{7,6},{8,9},{9,8},{10,11... | collective-permute-start | bytes 56 | tf_op jit(solution)/shard_map/ppermute | solution.py:176
  2.1 6.7 %collective-permute-start.1 = (bf16[256,512]{1,0:T(8,128)(2,1)}, bf16[256,512]{1,0:T(8,128)(2,1)S(1)}, u32[]{:S(2)}, u32[]{:S(2)}) collective-permute-start(bf16[256,512]{1,0:T(8,128)(2,1)} %own_hbm), channel_id=1, source_target_pairs={{0,1},{1,0},{2,3},{3,2},{4,5},{5,4},{6,7},{7,6},{8,9},{9,8},{10,11... | collective-permute-start | bytes 786440 | tf_op jit(solution)/shard_map/ppermute | solution.py:176
  2.4 16.1 %collective-permute-start.3 = (bf16[1,16,128,128]{3,2,1,0:T(8,128)(2,1)}, bf16[1,16,128,128]{3,2,1,0:T(8,128)(2,1)S(1)}, u32[]{:S(2)}, u32[]{:S(2)}) collective-permute-start(bf16[1,16,128,128]{3,2,1,0:T(8,128)(2,1)} %own_tiles), channel_id=1, source_target_pairs={{0,1},{1,0},{2,3},{3,2},{4,5},{5,4},{6,7},{7,6},{8,9},{9,8},{10,11... | collective-permute-start | bytes 1572872 | tf_op jit(solution)/shard_map/ppermute | solution.py:176
  3.2 7.2 %collective-permute-start.4 = (s32[2,4]{1,0:T(2,128)S(1)}, s32[2,4]{1,0:T(2,128)S(1)}, u32[]{:S(2)}, u32[]{:S(2)}) collective-permute-start(s32[2,4]{1,0:T(2,128)S(1)} %pad_add_fusion.refs_0_), channel_id=1, source_target_pairs={{0,16},{8,24},{16,0},{24,8},{1,17},{9,25},{17,1},{25,9},{2,18},{10... | collective-permute-start | bytes 104 | tf_op jit(solution)/shard_map/ppermute | solution.py:182
  7.2 5.4 %collective-permute-start.5 = (s32[2,4]{1,0:T(2,128)S(1)}, s32[2,4]{1,0:T(2,128)S(1)}, u32[]{:S(2)}, u32[]{:S(2)}) collective-permute-start(s32[2,4]{1,0:T(2,128)S(1)} %pad_add_fusion.refs_0_), channel_id=1, source_target_pairs={{0,24},{8,16},{16,8},{24,0},{1,25},{9,17},{17,9},{25,1},{2,26},{10... | collective-permute-start | bytes 104 | tf_op jit(solution)/shard_map/ppermute | solution.py:182
  8.5 4.0 %collective-permute-start.6 = (s32[2,4]{1,0:T(2,128)S(1)}, s32[2,4]{1,0:T(2,128)S(1)}, u32[]{:S(2)}, u32[]{:S(2)}) collective-permute-start(s32[2,4]{1,0:T(2,128)S(1)} %pad_add_fusion.refs_0_), channel_id=1, source_target_pairs={{0,8},{8,0},{16,24},{24,16},{1,9},{9,1},{17,25},{25,17},{2,10},{10... | collective-permute-start | bytes 104 | tf_op jit(solution)/shard_map/ppermute | solution.py:182
  10.1 9.2 %copy-start = (bf16[1,16,128,128]{3,2,1,0:T(8,128)(2,1)S(1)}, bf16[1,16,128,128]{3,2,1,0:T(8,128)(2,1)}, u32[]{:S(2)}) copy-start(bf16[1,16,128,128]{3,2,1,0:T(8,128)(2,1)} %own_tiles) | copy-start | bytes 1572868
  10.4 5.9 %collective-permute-start.2 = (s32[1,33]{1,0:T(1,128)S(1)}, s32[1,33]{1,0:T(1,128)S(1)}, u32[]{:S(2)}, u32[]{:S(2)}) collective-permute-start(s32[1,33]{1,0:T(1,128)S(1)} %pad_add_fusion.1.own_table), channel_id=1, source_target_pairs={{0,1},{1,0},{2,3},{3,2},{4,5},{5,4},{6,7},{7,6},{8,9},{9,8},{10,11... | collective-permute-start | bytes 404 | tf_op jit(solution)/shard_map/ppermute | solution.py:176
  12.8 8.1 %collective-permute-start.7 = (bf16[2,128,128]{2,1,0:T(8,128)(2,1)S(1)}, bf16[2,128,128]{2,1,0:T(8,128)(2,1)S(1)}, u32[]{:S(2)}, u32[]{:S(2)}) collective-permute-start(bf16[2,128,128]{2,1,0:T(8,128)(2,1)S(1)} %get-tuple-element.58), channel_id=1, source_target_pairs={{0,16},{8,24},{16,0},{24,8},{1,17},{9,25},{17,1},{25,9},{2,18},{10... | collective-permute-start | bytes 196616 | tf_op jit(solution)/shard_map/ppermute | solution.py:182
  14.1 6.9 %collective-permute-start.8 = (bf16[2,128,128]{2,1,0:T(8,128)(2,1)S(1)}, bf16[2,128,128]{2,1,0:T(8,128)(2,1)S(1)}, u32[]{:S(2)}, u32[]{:S(2)}) collective-permute-start(bf16[2,128,128]{2,1,0:T(8,128)(2,1)S(1)} %get-tuple-element.59), channel_id=1, source_target_pairs={{0,24},{8,16},{16,8},{24,0},{1,25},{9,17},{17,9},{25,1},{2,26},{10... | collective-permute-start | bytes 196616 | tf_op jit(solution)/shard_map/ppermute | solution.py:182
  15.0 6.1 %collective-permute-start.9 = (bf16[2,128,128]{2,1,0:T(8,128)(2,1)S(1)}, bf16[2,128,128]{2,1,0:T(8,128)(2,1)S(1)}, u32[]{:S(2)}, u32[]{:S(2)}) collective-permute-start(bf16[2,128,128]{2,1,0:T(8,128)(2,1)S(1)} %get-tuple-element.60), channel_id=1, source_target_pairs={{0,8},{8,0},{16,24},{24,16},{1,9},{9,1},{17,25},{25,17},{2,10},{10... | collective-permute-start | bytes 196616 | tf_op jit(solution)/shard_map/ppermute | solution.py:182
  16.3 9.5 %collective-permute-start.19 = (bf16[2,128,128]{2,1,0:T(8,128)(2,1)S(1)}, bf16[2,128,128]{2,1,0:T(8,128)(2,1)S(1)}, u32[]{:S(2)}, u32[]{:S(2)}) collective-permute-start(bf16[2,128,128]{2,1,0:T(8,128)(2,1)S(1)} %get-tuple-element.75), channel_id=1, source_target_pairs={{0,16},{8,24},{16,0},{24,8},{1,17},{9,25},{17,1},{25,9},{2,18},{10... | collective-permute-start | bytes 196616 | tf_op jit(solution)/shard_map/ppermute | solution.py:182
  18.5 9.8 %collective-permute-start.20 = (bf16[2,128,128]{2,1,0:T(8,128)(2,1)S(1)}, bf16[2,128,128]{2,1,0:T(8,128)(2,1)S(1)}, u32[]{:S(2)}, u32[]{:S(2)}) collective-permute-start(bf16[2,128,128]{2,1,0:T(8,128)(2,1)S(1)} %get-tuple-element.76), channel_id=1, source_target_pairs={{0,24},{8,16},{16,8},{24,0},{1,25},{9,17},{17,9},{25,1},{2,26},{10... | collective-permute-start | bytes 196616 | tf_op jit(solution)/shard_map/ppermute | solution.py:182
  20.9 7.3 %collective-permute-start.21 = (bf16[2,128,128]{2,1,0:T(8,128)(2,1)S(1)}, bf16[2,128,128]{2,1,0:T(8,128)(2,1)S(1)}, u32[]{:S(2)}, u32[]{:S(2)}) collective-permute-start(bf16[2,128,128]{2,1,0:T(8,128)(2,1)S(1)} %get-tuple-element.77), channel_id=1, source_target_pairs={{0,8},{8,0},{16,24},{24,16},{1,9},{9,1},{17,25},{25,17},{2,10},{10... | collective-permute-start | bytes 196616 | tf_op jit(solution)/shard_map/ppermute | solution.py:182
  21.8 8.3 %collective-permute-start.10 = (bf16[2,2,128,128]{3,2,1,0:T(8,128)(2,1)S(1)}, bf16[2,2,128,128]{3,2,1,0:T(8,128)(2,1)S(1)}, u32[]{:S(2)}, u32[]{:S(2)}) collective-permute-start(bf16[2,2,128,128]{3,2,1,0:T(8,128)(2,1)S(1)} %get-tuple-element.62), channel_id=1, source_target_pairs={{0,2},{1,3},{2,0},{3,1},{4,6},{5,7},{6,4},{7,5},{8,10},{9,11},{10,... | collective-permute-start | bytes 393224 | tf_op jit(solution)/shard_map/ppermute | solution.py:176
  23.3 9.4 %collective-permute-start.11 = (bf16[2,2,128,128]{3,2,1,0:T(8,128)(2,1)S(1)}, bf16[2,2,128,128]{3,2,1,0:T(8,128)(2,1)S(1)}, u32[]{:S(2)}, u32[]{:S(2)}) collective-permute-start(bf16[2,2,128,128]{3,2,1,0:T(8,128)(2,1)S(1)} %get-tuple-element.63), channel_id=1, source_target_pairs={{0,4},{1,5},{2,6},{3,7},{4,0},{5,1},{6,2},{7,3},{8,12},{9,13},{10,... | collective-permute-start | bytes 393224 | tf_op jit(solution)/shard_map/ppermute | solution.py:176
  25.8 7.4 %collective-permute-start.12 = (bf16[2,2,128,128]{3,2,1,0:T(8,128)(2,1)S(1)}, bf16[2,2,128,128]{3,2,1,0:T(8,128)(2,1)S(1)}, u32[]{:S(2)}, u32[]{:S(2)}) collective-permute-start(bf16[2,2,128,128]{3,2,1,0:T(8,128)(2,1)S(1)} %get-tuple-element.64), channel_id=1, source_target_pairs={{0,6},{1,7},{2,4},{3,5},{4,2},{5,3},{6,0},{7,1},{8,14},{9,15},{10,... | collective-permute-start | bytes 393224 | tf_op jit(solution)/shard_map/ppermute | solution.py:176
  29.0 8.2 %collective-permute-start.22 = (bf16[2,2,128,128]{3,2,1,0:T(8,128)(2,1)S(1)}, bf16[2,2,128,128]{3,2,1,0:T(8,128)(2,1)S(1)}, u32[]{:S(2)}, u32[]{:S(2)}) collective-permute-start(bf16[2,2,128,128]{3,2,1,0:T(8,128)(2,1)S(1)} %get-tuple-element.79), channel_id=1, source_target_pairs={{0,2},{1,3},{2,0},{3,1},{4,6},{5,7},{6,4},{7,5},{8,10},{9,11},{10,... | collective-permute-start | bytes 393224 | tf_op jit(solution)/shard_map/ppermute | solution.py:176
  29.6 9.1 %collective-permute-start.23 = (bf16[2,2,128,128]{3,2,1,0:T(8,128)(2,1)S(1)}, bf16[2,2,128,128]{3,2,1,0:T(8,128)(2,1)S(1)}, u32[]{:S(2)}, u32[]{:S(2)}) collective-permute-start(bf16[2,2,128,128]{3,2,1,0:T(8,128)(2,1)S(1)} %get-tuple-element.80), channel_id=1, source_target_pairs={{0,4},{1,5},{2,6},{3,7},{4,0},{5,1},{6,2},{7,3},{8,12},{9,13},{10,... | collective-permute-start | bytes 393224 | tf_op jit(solution)/shard_map/ppermute | solution.py:176
  30.1 8.6 %collective-permute-start.24 = (bf16[2,2,128,128]{3,2,1,0:T(8,128)(2,1)S(1)}, bf16[2,2,128,128]{3,2,1,0:T(8,128)(2,1)S(1)}, u32[]{:S(2)}, u32[]{:S(2)}) collective-permute-start(bf16[2,2,128,128]{3,2,1,0:T(8,128)(2,1)S(1)} %get-tuple-element.81), channel_id=1, source_target_pairs={{0,6},{1,7},{2,4},{3,5},{4,2},{5,3},{6,0},{7,1},{8,14},{9,15},{10,... | collective-permute-start | bytes 393224 | tf_op jit(solution)/shard_map/ppermute | solution.py:176
  33.4 8.4 %collective-permute-start.13 = (bf16[2,128,128]{2,1,0:T(8,128)(2,1)S(1)}, bf16[2,128,128]{2,1,0:T(8,128)(2,1)S(1)}, u32[]{:S(2)}, u32[]{:S(2)}) collective-permute-start(bf16[2,128,128]{2,1,0:T(8,128)(2,1)S(1)} %get-tuple-element.66), channel_id=1, source_target_pairs={{0,16},{8,24},{16,0},{24,8},{1,17},{9,25},{17,1},{25,9},{2,18},{10... | collective-permute-start | bytes 196616 | tf_op jit(solution)/shard_map/ppermute | solution.py:182
  37.1 6.1 %collective-permute-start.14 = (bf16[2,128,128]{2,1,0:T(8,128)(2,1)S(1)}, bf16[2,128,128]{2,1,0:T(8,128)(2,1)S(1)}, u32[]{:S(2)}, u32[]{:S(2)}) collective-permute-start(bf16[2,128,128]{2,1,0:T(8,128)(2,1)S(1)} %get-tuple-element.67), channel_id=1, source_target_pairs={{0,8},{8,0},{16,24},{24,16},{1,9},{9,1},{17,25},{25,17},{2,10},{10... | collective-permute-start | bytes 196616 | tf_op jit(solution)/shard_map/ppermute | solution.py:182
  37.1 6.5 %collective-permute-start.15 = (bf16[2,128,128]{2,1,0:T(8,128)(2,1)S(1)}, bf16[2,128,128]{2,1,0:T(8,128)(2,1)S(1)}, u32[]{:S(2)}, u32[]{:S(2)}) collective-permute-start(bf16[2,128,128]{2,1,0:T(8,128)(2,1)S(1)} %get-tuple-element.68), channel_id=1, source_target_pairs={{0,24},{8,16},{16,8},{24,0},{1,25},{9,17},{17,9},{25,1},{2,26},{10... | collective-permute-start | bytes 196616 | tf_op jit(solution)/shard_map/ppermute | solution.py:182
  38.8 7.4 %collective-permute-start.25 = (bf16[2,128,128]{2,1,0:T(8,128)(2,1)S(1)}, bf16[2,128,128]{2,1,0:T(8,128)(2,1)S(1)}, u32[]{:S(2)}, u32[]{:S(2)}) collective-permute-start(bf16[2,128,128]{2,1,0:T(8,128)(2,1)S(1)} %get-tuple-element.83), channel_id=1, source_target_pairs={{0,16},{8,24},{16,0},{24,8},{1,17},{9,25},{17,1},{25,9},{2,18},{10... | collective-permute-start | bytes 196616 | tf_op jit(solution)/shard_map/ppermute | solution.py:182
  40.8 7.1 %collective-permute-start.26 = (bf16[2,128,128]{2,1,0:T(8,128)(2,1)S(1)}, bf16[2,128,128]{2,1,0:T(8,128)(2,1)S(1)}, u32[]{:S(2)}, u32[]{:S(2)}) collective-permute-start(bf16[2,128,128]{2,1,0:T(8,128)(2,1)S(1)} %get-tuple-element.84), channel_id=1, source_target_pairs={{0,8},{8,0},{16,24},{24,16},{1,9},{9,1},{17,25},{25,17},{2,10},{10... | collective-permute-start | bytes 196616 | tf_op jit(solution)/shard_map/ppermute | solution.py:182
  41.7 6.2 %collective-permute-start.27 = (bf16[2,128,128]{2,1,0:T(8,128)(2,1)S(1)}, bf16[2,128,128]{2,1,0:T(8,128)(2,1)S(1)}, u32[]{:S(2)}, u32[]{:S(2)}) collective-permute-start(bf16[2,128,128]{2,1,0:T(8,128)(2,1)S(1)} %get-tuple-element.85), channel_id=1, source_target_pairs={{0,24},{8,16},{16,8},{24,0},{1,25},{9,17},{17,9},{25,1},{2,26},{10... | collective-permute-start | bytes 196616 | tf_op jit(solution)/shard_map/ppermute | solution.py:182
  44.3 6.3 %collective-permute-start.16 = (bf16[2,2,128,128]{3,2,1,0:T(8,128)(2,1)S(1)}, bf16[2,2,128,128]{3,2,1,0:T(8,128)(2,1)S(1)}, u32[]{:S(2)}, u32[]{:S(2)}) collective-permute-start(bf16[2,2,128,128]{3,2,1,0:T(8,128)(2,1)S(1)} %get-tuple-element.70), channel_id=1, source_target_pairs={{0,2},{1,3},{2,0},{3,1},{4,6},{5,7},{6,4},{7,5},{8,10},{9,11},{10,... | collective-permute-start | bytes 393224 | tf_op jit(solution)/shard_map/ppermute | solution.py:176
  45.4 6.8 %collective-permute-start.17 = (bf16[2,2,128,128]{3,2,1,0:T(8,128)(2,1)S(1)}, bf16[2,2,128,128]{3,2,1,0:T(8,128)(2,1)S(1)}, u32[]{:S(2)}, u32[]{:S(2)}) collective-permute-start(bf16[2,2,128,128]{3,2,1,0:T(8,128)(2,1)S(1)} %get-tuple-element.71), channel_id=1, source_target_pairs={{0,4},{1,5},{2,6},{3,7},{4,0},{5,1},{6,2},{7,3},{8,12},{9,13},{10,... | collective-permute-start | bytes 393224 | tf_op jit(solution)/shard_map/ppermute | solution.py:176
  46.2 7.4 %collective-permute-start.18 = (bf16[2,2,128,128]{3,2,1,0:T(8,128)(2,1)S(1)}, bf16[2,2,128,128]{3,2,1,0:T(8,128)(2,1)S(1)}, u32[]{:S(2)}, u32[]{:S(2)}) collective-permute-start(bf16[2,2,128,128]{3,2,1,0:T(8,128)(2,1)S(1)} %get-tuple-element.72), channel_id=1, source_target_pairs={{0,6},{1,7},{2,4},{3,5},{4,2},{5,3},{6,0},{7,1},{8,14},{9,15},{10,... | collective-permute-start | bytes 393224 | tf_op jit(solution)/shard_map/ppermute | solution.py:176
  48.6 5.1 %collective-permute-start.28 = (bf16[2,2,128,128]{3,2,1,0:T(8,128)(2,1)S(1)}, bf16[2,2,128,128]{3,2,1,0:T(8,128)(2,1)S(1)}, u32[]{:S(2)}, u32[]{:S(2)}) collective-permute-start(bf16[2,2,128,128]{3,2,1,0:T(8,128)(2,1)S(1)} %get-tuple-element.87), channel_id=1, source_target_pairs={{0,2},{1,3},{2,0},{3,1},{4,6},{5,7},{6,4},{7,5},{8,10},{9,11},{10,... | collective-permute-start | bytes 393224 | tf_op jit(solution)/shard_map/ppermute | solution.py:176
  49.9 5.1 %collective-permute-start.29 = (bf16[2,2,128,128]{3,2,1,0:T(8,128)(2,1)S(1)}, bf16[2,2,128,128]{3,2,1,0:T(8,128)(2,1)S(1)}, u32[]{:S(2)}, u32[]{:S(2)}) collective-permute-start(bf16[2,2,128,128]{3,2,1,0:T(8,128)(2,1)S(1)} %get-tuple-element.88), channel_id=1, source_target_pairs={{0,4},{1,5},{2,6},{3,7},{4,0},{5,1},{6,2},{7,3},{8,12},{9,13},{10,... | collective-permute-start | bytes 393224 | tf_op jit(solution)/shard_map/ppermute | solution.py:176
  50.6 5.9 %collective-permute-start.30 = (bf16[2,2,128,128]{3,2,1,0:T(8,128)(2,1)S(1)}, bf16[2,2,128,128]{3,2,1,0:T(8,128)(2,1)S(1)}, u32[]{:S(2)}, u32[]{:S(2)}) collective-permute-start(bf16[2,2,128,128]{3,2,1,0:T(8,128)(2,1)S(1)} %get-tuple-element.89), channel_id=1, source_target_pairs={{0,6},{1,7},{2,4},{3,5},{4,2},{5,3},{6,0},{7,1},{8,14},{9,15},{10,... | collective-permute-start | bytes 393224 | tf_op jit(solution)/shard_map/ppermute | solution.py:176
  53.7 3.0 %copy-start.1 = (bf16[512,512]{1,0:T(8,128)(2,1)S(1)}, bf16[512,512]{1,0:T(8,128)(2,1)}, u32[]{:S(2)}) copy-start(bf16[512,512]{1,0:T(8,128)(2,1)} %weight.1) | copy-start | bytes 1572868
  53.7 3.0 %collective-permute-start.31 = (bf16[2,128,128]{2,1,0:T(8,128)(2,1)S(1)}, bf16[2,128,128]{2,1,0:T(8,128)(2,1)S(1)}, u32[]{:S(2)}, u32[]{:S(2)}) collective-permute-start(bf16[2,128,128]{2,1,0:T(8,128)(2,1)S(1)} %get-tuple-element.91), channel_id=1, source_target_pairs={{0,1},{1,0},{2,3},{3,2},{4,5},{5,4},{6,7},{7,6},{8,9},{9,8},{10,11... | collective-permute-start | bytes 196616 | tf_op jit(solution)/shard_map/ppermute | solution.py:176
  56.6 1.3 %collective-permute-start.32 = (bf16[2,128,128]{2,1,0:T(8,128)(2,1)S(1)}, bf16[2,128,128]{2,1,0:T(8,128)(2,1)S(1)}, u32[]{:S(2)}, u32[]{:S(2)}) collective-permute-start(bf16[2,128,128]{2,1,0:T(8,128)(2,1)S(1)} %get-tuple-element.92), channel_id=1, source_target_pairs={{0,1},{1,0},{2,3},{3,2},{4,5},{5,4},{6,7},{7,6},{8,9},{9,8},{10,11... | collective-permute-start | bytes 196616 | tf_op jit(solution)/shard_map/ppermute | solution.py:176
